TPU v7x, 512 devices: a whole 4x8x8 slice. The times are simulated.
512 devices in a mesh: ta: 8 (over x, z_hi), ha: 8 (over z_lo, core), hd: 8 (over y).
Axes of the slice: x: 4, y: 8, z: 8 (z_hi: 2, z_lo: 4; z = z_hi * 4 + z_lo), core: 2. Of those that a mesh axis runs over, the one named last changes fastest.
Arguments:
- qkv: bfloat16 [32, 32, 64, 9216], P('ta', 'ha', 'hd'), may hold values from -40 to 40, as said below
- q_gain: float32 [128], replicated, may hold values from 0.5 to 4.5
- k_gain: float32 [128], replicated, may hold values from 0.5 to 4.5
- windows: int32 [24, 3], P('hd'), may hold values from 0 to 1, as said below
- frame_counts: int32 [16], replicated, may hold values from 1 to 2, as said below
- row_counts: int32 [16], replicated, may hold values from 1 to 2, as said below
Outputs:
- attended: bfloat16 [32, 32, 64, 3072], P('ta', 'ha', 'hd')
Inputs may be any that keep to these rules, and one draw needn't show every extreme that they name: `qkv`: the last dimension holds the query, then the key, then the value, each as 24 heads of 128 entries. `windows`: every column reaches 1 for some head. `frame_counts`: some tile holds 2 frames. `row_counts`: some tile holds 2 rows.
All inputs are finite; a program needn't handle non-finite values.
Results may differ from a plain program's by a relative error of at most 0.012.
The roundings to bfloat16 on the way count: a program that leaves them out, or rounds other values in their place, can miss the bound.
Values may be sent and summed in bfloat16 or wider, within the bound.
No kernel may reach another device: no remote copies, remote signals or barrier semaphores. Data moves between devices by JAX's collectives and lax.ppermute only.
A program may use at most 64 MiB of HBM per device.

v0:
```python
import math

import jax
import jax.numpy as jnp
from jax import lax
from jax.sharding import PartitionSpec as P

TT = 2
TH = 2
TW = 8


def extended(value, sides, width):
    for axis, dim in sides:
        size, length = (lax.axis_size(axis), value.shape[dim])
        up = [(i, (i + 1) % size) for i in range(size - 1)]
        down = [(j, i) for i, j in up]
        last = lax.slice_in_dim(value, length - width, length, axis=dim)
        initial = lax.slice_in_dim(value, 0, width, axis=dim)
        before = lax.ppermute(last, axis, up)
        after = lax.ppermute(initial, axis, down)
        value = jnp.concatenate([before, value, after], axis=dim)
    return value


def normalize(part_values, gain):
    widened = part_values.astype(jnp.float32)
    meansq = jnp.mean(widened * widened, axis=-1, keepdims=True)
    return (widened * lax.rsqrt(meansq + 1e-06) * gain).astype(jnp.bfloat16)


def valid_cells(position, extent, counts):
    tile_index = position // extent
    listed = jnp.arange(counts.shape[0], dtype=jnp.int32)
    holding = jnp.sum(jnp.where(tile_index[:, None] == listed[None, :], counts[None, :], 0), axis=1)
    return position % extent < holding


def extend_rims(paired):
    grown = extended(paired, (("ta", 0), ("ha", 1)), TT)
    return grown


def shards(qkv, q_gain, k_gain, windows, frame_counts, row_counts):
    frame_num, row_num, col_local, channels = qkv.shape
    head_dim = q_gain.shape[0]
    heads_all = channels // (3 * head_dim)
    sectioned = qkv.reshape(frame_num, row_num, col_local, 3, heads_all, head_dim)
    spread = lax.all_to_all(sectioned, "hd", split_axis=4, concat_axis=2, tiled=True)
    queries = normalize(spread[:, :, :, 0], q_gain)
    paired = jnp.stack([normalize(spread[:, :, :, 1], k_gain), spread[:, :, :, 2]], axis=3)
    padded = extend_rims(paired)
    col_num = queries.shape[2]
    heads_local = queries.shape[3]
    frame_base = lax.axis_index("ta") * frame_num
    row_base = lax.axis_index("ha") * row_num
    time_tiles = frame_num // TT
    score_scale = 1.0 / math.sqrt(head_dim)
    col_tiles = jnp.arange(col_num, dtype=jnp.int32) // TW
    col_gap = jnp.abs(col_tiles[:, None] - col_tiles[None, :])
    query_rows = row_base + jnp.arange(row_num, dtype=jnp.int32)
    key_rows = row_base - TH + jnp.arange(row_num + 2 * TH, dtype=jnp.int32)
    row_gap = jnp.abs(query_rows[:, None] // TH - key_rows[None, :] // TH)
    row_valid = valid_cells(key_rows, TH, row_counts)
    query_row_valid = valid_cells(query_rows, TH, row_counts)

    def attend(item_index):
        tile_at = item_index // heads_local
        head_at = item_index % heads_local
        first_frame = tile_at * TT
        query_block = lax.dynamic_slice(
            queries, (first_frame, 0, 0, head_at, 0), (TT, row_num, col_num, 1, head_dim)
        ).reshape(-1, head_dim)
        pair_block = lax.dynamic_slice(
            padded,
            (first_frame, 0, 0, 0, head_at, 0),
            (3 * TT, row_num + 2 * TH, col_num, 2, 1, head_dim),
        )
        key_block = pair_block[:, :, :, 0, 0].reshape(-1, head_dim)
        value_block = pair_block[:, :, :, 1, 0].reshape(-1, head_dim)
        radius = windows[head_at]
        query_frames = frame_base + first_frame + jnp.arange(TT, dtype=jnp.int32)
        key_frames = frame_base + first_frame - TT + jnp.arange(3 * TT, dtype=jnp.int32)
        time_mask = (
            jnp.abs(query_frames[:, None] // TT - key_frames[None, :] // TT) <= radius[0]
        ) & valid_cells(key_frames, TT, frame_counts)[None, :]
        row_mask = (row_gap <= radius[1]) & row_valid[None, :]
        col_mask = col_gap <= radius[2]
        allowed = (
            time_mask[:, None, None, :, None, None]
            & row_mask[None, :, None, None, :, None]
            & col_mask[None, None, :, None, None, :]
        ).reshape(query_block.shape[0], key_block.shape[0])
        query_live = (
            valid_cells(query_frames, TT, frame_counts)[:, None, None]
            & query_row_valid[None, :, None]
            & (col_tiles >= 0)[None, None, :]
        ).reshape(-1)
        scores = (
            jnp.einsum("qd,kd->qk", query_block, key_block, preferred_element_type=jnp.float32)
            * score_scale
        )
        scores = jnp.where(allowed, scores, -1e30)
        highest = jnp.max(scores, axis=1, keepdims=True)
        raised = jnp.exp(scores - highest)
        summed = jnp.sum(raised, axis=1, keepdims=True)
        weights = raised.astype(jnp.bfloat16)
        blended = jnp.dot(weights, value_block, preferred_element_type=jnp.float32)
        result = jnp.where(query_live[:, None], blended / summed, 0.0)
        return result.astype(jnp.bfloat16).reshape(TT, row_num, col_num, head_dim)

    outputs = lax.map(attend, jnp.arange(time_tiles * heads_local, dtype=jnp.int32))
    outputs = outputs.reshape(time_tiles, heads_local, TT, row_num, col_num, head_dim)
    outputs = outputs.transpose(0, 2, 3, 4, 1, 5).reshape(
        frame_num, row_num, col_num, heads_local, head_dim
    )
    gathered = lax.all_to_all(outputs, "hd", split_axis=2, concat_axis=3, tiled=True)
    return gathered.reshape(frame_num, row_num, col_local, heads_all * head_dim)


def solution(mesh):
    return jax.shard_map(
        shards,
        mesh=mesh,
        in_specs=(P("ta", "ha", "hd", None), P(), P(), P("hd", None), P(), P()),
        out_specs=P("ta", "ha", "hd", None),
        check_vma=False,
    )
```

profile of v0, /device:TPU:67, one launch (start us, length us, event | category | flops | bytes accessed | tf_op | source)
XLA Modules:
  0.0 367.5 jit_solution(7055142364976759079)
XLA Ops:
  2.3 62.1 %all_to_all.33 = bf16[4,4,8,3,24,128]{5,2,3,1,0,4:T(8,128)(2,1)S(1)} all-to-all(bf16[4,4,8,3,24,128]{5,2,3,1,0,4:T(8,128)(2,1)S(1)} %copy.38), channel_id=1, replica_groups=mesh['ta'=8,'ha'=8,'hd'=8] {'hd'}, dimensions={4} | all-to-all | bytes 4718592 | tf_op jit(solution)/shard_map/all_to_all | solution.py:49
  68.4 9.7 %collective-permute-start = (bf16[2,4,64,2,3,128]{5,2,4,3,1,0:T(8,128)(2,1)}, bf16[2,4,64,2,3,128]{5,2,4,3,1,0:T(8,128)(2,1)}, u32[]{:S(2)}, u32[]{:S(2)}) collective-permute-start(bf16[2,4,64,2,3,128]{5,2,4,3,1,0:T(8,128)(2,1)} %get-tuple-element.356), channel_id=1, source_target_pairs={{0,64},{64,128},{128,192},{192,256},{256,320},{320,384},{384,448},... | collective-permute-start | bytes 2359304 | tf_op jit(solution)/shard_map/ppermute | solution.py:20
  80.0 32.6 %collective-permute-done = bf16[2,4,64,2,3,128]{5,2,4,3,1,0:T(8,128)(2,1)} collective-permute-done((bf16[2,4,64,2,3,128]{5,2,4,3,1,0:T(8,128)(2,1)}, bf16[2,4,64,2,3,128]{5,2,4,3,1,0:T(8,128)(2,1)}, u32[]{:S(2)}, u32[]{:S(2)}) %collective-permute-start) | collective-permute-done | bytes 786464 | tf_op jit(solution)/shard_map/ppermute | solution.py:20
  112.7 32.5 %collective-permute-done.1 = bf16[2,4,64,2,3,128]{5,2,4,3,1,0:T(8,128)(2,1)} collective-permute-done((bf16[2,4,64,2,3,128]{5,2,4,3,1,0:T(8,128)(2,1)}, bf16[2,4,64,2,3,128]{5,2,4,3,1,0:T(8,128)(2,1)}, u32[]{:S(2)}, u32[]{:S(2)}) %collective-permute-start.1) | collective-permute-done | bytes 786464 | tf_op jit(solution)/shard_map/ppermute | solution.py:21
  149.4 5.3 %collective-permute-start.2 = (bf16[8,2,64,2,3,128]{5,2,4,3,1,0:T(8,128)(2,1)}, bf16[8,2,64,2,3,128]{5,2,4,3,1,0:T(8,128)(2,1)}, u32[]{:S(2)}, u32[]{:S(2)}) collective-permute-start(bf16[8,2,64,2,3,128]{5,2,4,3,1,0:T(8,128)(2,1)} %get-tuple-element.354), channel_id=1, source_target_pairs={{0,8},{8,16},{16,24},{24,32},{32,40},{40,48},{48,56},{1,9},{9,17},... | collective-permute-start | bytes 4718600 | tf_op jit(solution)/shard_map/ppermute | solution.py:20
  159.2 13.2 %collective-permute-done.2 = bf16[8,2,64,2,3,128]{5,2,4,3,1,0:T(8,128)(2,1)} collective-permute-done((bf16[8,2,64,2,3,128]{5,2,4,3,1,0:T(8,128)(2,1)}, bf16[8,2,64,2,3,128]{5,2,4,3,1,0:T(8,128)(2,1)}, u32[]{:S(2)}, u32[]{:S(2)}) %collective-permute-start.2) | collective-permute-done | bytes 1572896 | tf_op jit(solution)/shard_map/ppermute | solution.py:20
  172.4 4.4 %collective-permute-done.3 = bf16[8,2,64,2,3,128]{5,2,4,3,1,0:T(8,128)(2,1)} collective-permute-done((bf16[8,2,64,2,3,128]{5,2,4,3,1,0:T(8,128)(2,1)}, bf16[8,2,64,2,3,128]{5,2,4,3,1,0:T(8,128)(2,1)}, u32[]{:S(2)}, u32[]{:S(2)}) %collective-permute-start.3) | collective-permute-done | bytes 1572896 | tf_op jit(solution)/shard_map/ppermute | solution.py:21
  176.8 6.3 %pad_maximum_fusion = bf16[8,8,64,2,3,128]{5,2,4,3,1,0:T(8,128)(2,1)} fusion(bf16[8,2,64,2,3,128]{5,2,4,3,1,0:T(8,128)(2,1)} %collective-permute-done.3, bf16[2,4,64,2,3,128]{5,2,4,3,1,0:T(8,128)(2,1)} %collective-permute-done.1, bf16[4,4,64,1,3,128]{5,2,4,3,1,0:T(8,128)(2,1)S(1)} %slice.73, bf16[4,4,64,1,3,128]{5,2,4,3,1,0:T(8,128)(2,1)} %copy-done.1, ...), kind=kLoop, calls=%fused_computation.48 | loop fusion | flops 15728640 | bytes 12582912 | tf_op jit(solution)/shard_map/concatenate | solution.py:22
  183.1 154.3 %while.14 = (s32[]{:T(128)}, bf16[6,2,4,64,128]{4,3,2,1,0:T(8,128)(2,1)}, s32[6]{0:T(128)S(1)}, s32[]{:T(128)}, s32[16]{0:T(128)S(1)}, /*index=5*/pred[4]{0:T(51...) while((s32[]{:T(128)}, ...), condition=%wide.region_9.10_spmd.clone, body=%wide.region_4.9_spmd.clone.sunk | while | flops 818099456 | bytes 33839296 | solution.py:112
  190.8 2.7 constant_dynamic-slice_fusion.7
  195.1 7.8 %and.445 = pred[512,3072]{1,0:T(32,128)(4,1)} reshape(pred[2,4,64,6,8,64]{5,4,3,2,1,0:T(8,128)(4,1)S(1)} %broadcast_and_fusion.9) | data formatting | bytes 3145728 | tf_op jit(solution)/shard_map/while/body/eval_jaxpr/and | solution.py:90
  202.9 3.1 fusion.60
  216.5 2.7 constant_dynamic-slice_fusion.7
  220.8 7.8 %and.445 = pred[512,3072]{1,0:T(32,128)(4,1)} reshape(pred[2,4,64,6,8,64]{5,4,3,2,1,0:T(8,128)(4,1)S(1)} %broadcast_and_fusion.9) | data formatting | bytes 3145728 | tf_op jit(solution)/shard_map/while/body/eval_jaxpr/and | solution.py:90
  228.6 3.1 fusion.60
  246.5 7.8 %and.445 = pred[512,3072]{1,0:T(32,128)(4,1)} reshape(pred[2,4,64,6,8,64]{5,4,3,2,1,0:T(8,128)(4,1)S(1)} %broadcast_and_fusion.9) | data formatting | bytes 3145728 | tf_op jit(solution)/shard_map/while/body/eval_jaxpr/and | solution.py:90
  254.3 3.1 fusion.60
  272.2 7.8 %and.445 = pred[512,3072]{1,0:T(32,128)(4,1)} reshape(pred[2,4,64,6,8,64]{5,4,3,2,1,0:T(8,128)(4,1)S(1)} %broadcast_and_fusion.9) | data formatting | bytes 3145728 | tf_op jit(solution)/shard_map/while/body/eval_jaxpr/and | solution.py:90
  280.0 3.1 fusion.60
  297.9 7.8 %and.445 = pred[512,3072]{1,0:T(32,128)(4,1)} reshape(pred[2,4,64,6,8,64]{5,4,3,2,1,0:T(8,128)(4,1)S(1)} %broadcast_and_fusion.9) | data formatting | bytes 3145728 | tf_op jit(solution)/shard_map/while/body/eval_jaxpr/and | solution.py:90
  305.7 3.1 fusion.60
  323.6 7.8 %and.445 = pred[512,3072]{1,0:T(32,128)(4,1)} reshape(pred[2,4,64,6,8,64]{5,4,3,2,1,0:T(8,128)(4,1)S(1)} %broadcast_and_fusion.9) | data formatting | bytes 3145728 | tf_op jit(solution)/shard_map/while/body/eval_jaxpr/and | solution.py:90
  331.4 3.1 fusion.60
  339.2 25.9 %all_to_all.34 = bf16[4,4,64,3,128]{4,1,3,0,2:T(4,128)(2,1)S(1)} all-to-all(bf16[4,4,64,3,128]{4,1,3,0,2:T(4,128)(2,1)S(1)} %copy.44), channel_id=1, replica_groups=mesh['ta'=8,'ha'=8,'hd'=8] {'hd'}, dimensions={2} | all-to-all | bytes 1572864 | tf_op jit(solution)/shard_map/all_to_all | solution.py:117
  (186 shorter events, 92.4 us)
Async XLA Ops:
  64.4 1.3 copy-start.2
  66.2 0.9 copy-start.1
  68.4 44.3 %collective-permute-start = (bf16[2,4,64,2,3,128]{5,2,4,3,1,0:T(8,128)(2,1)}, bf16[2,4,64,2,3,128]{5,2,4,3,1,0:T(8,128)(2,1)}, u32[]{:S(2)}, u32[]{:S(2)}) collective-permute-start(bf16[2,4,64,2,3,128]{5,2,4,3,1,0:T(8,128)(2,1)} %get-tuple-element.356), channel_id=1, source_target_pairs={{0,64},{64,128},{128,192},{192,256},{256,320},{320,384},{384,448},... | collective-permute-start | bytes 2359304 | tf_op jit(solution)/shard_map/ppermute | solution.py:20
  78.1 67.1 %collective-permute-start.1 = (bf16[2,4,64,2,3,128]{5,2,4,3,1,0:T(8,128)(2,1)}, bf16[2,4,64,2,3,128]{5,2,4,3,1,0:T(8,128)(2,1)}, u32[]{:S(2)}, u32[]{:S(2)}) collective-permute-start(bf16[2,4,64,2,3,128]{5,2,4,3,1,0:T(8,128)(2,1)} %get-tuple-element.357), channel_id=1, source_target_pairs={{64,0},{128,64},{192,128},{256,192},{320,256},{384,320},{448,384},... | collective-permute-start | bytes 2359304 | tf_op jit(solution)/shard_map/ppermute | solution.py:21
  147.0 9.9 %copy-start.4 = (s32[16]{0:T(128)S(1)}, s32[16]{0:T(128)}, u32[]{:S(2)}) copy-start(s32[16]{0:T(128)} %param.13) | copy-start | bytes 196
  147.0 10.8 %copy-start.3 = (f32[128]{0:T(128)S(1)}, f32[128]{0:T(128)}, u32[]{:S(2)}) copy-start(f32[128]{0:T(128)} %param.9) | copy-start | bytes 1540
  149.4 23.0 %collective-permute-start.2 = (bf16[8,2,64,2,3,128]{5,2,4,3,1,0:T(8,128)(2,1)}, bf16[8,2,64,2,3,128]{5,2,4,3,1,0:T(8,128)(2,1)}, u32[]{:S(2)}, u32[]{:S(2)}) collective-permute-start(bf16[8,2,64,2,3,128]{5,2,4,3,1,0:T(8,128)(2,1)} %get-tuple-element.354), channel_id=1, source_target_pairs={{0,8},{8,16},{16,24},{24,32},{32,40},{40,48},{48,56},{1,9},{9,17},... | collective-permute-start | bytes 4718600 | tf_op jit(solution)/shard_map/ppermute | solution.py:20
  154.7 22.1 %collective-permute-start.3 = (bf16[8,2,64,2,3,128]{5,2,4,3,1,0:T(8,128)(2,1)}, bf16[8,2,64,2,3,128]{5,2,4,3,1,0:T(8,128)(2,1)}, u32[]{:S(2)}, u32[]{:S(2)}) collective-permute-start(bf16[8,2,64,2,3,128]{5,2,4,3,1,0:T(8,128)(2,1)} %get-tuple-element.355), channel_id=1, source_target_pairs={{8,0},{16,8},{24,16},{32,24},{40,32},{48,40},{56,48},{9,1},{17,9},... | collective-permute-start | bytes 4718600 | tf_op jit(solution)/shard_map/ppermute | solution.py:21
  159.2 23.9 %copy-start.5 = (s32[16]{0:T(128)S(1)}, s32[16]{0:T(128)}, u32[]{:S(2)}) copy-start(s32[16]{0:T(128)} %param.12) | copy-start | bytes 196
  206.0 1.1 copy-start
  231.7 1.1 copy-start
  257.4 1.1 copy-start
  283.1 1.1 copy-start
  308.8 1.1 copy-start
  334.5 1.1 copy-start
where the time goes:
time: 369 us; the launch traced here: 367 us
  local copies, waits for them, and re-layouts  95.8 us (26%)
  blocking collectives  88 us (24%)
  waiting for transfers between devices  82.7 us (22%)
  other arithmetic  44.7 us (12%)
  matrix products  24.9 us (7%)
  starting transfers between devices  19.1 us (5%)
  loops' own time  12 us (3%)
    all_to_all x1, blocking collectives, shards(): lax.all_to_all(sectioned, 'hd', split_axis=4, concat_axis=2, tiled=True)  62.1 us
    and x6, local copies, waits for them, and re-layouts, attend(): time_mask[:, None, None, :, None, None]  46.6 us
    ppermute x2, waiting for transfers between devices, extended(): before = lax.ppermute(last, axis, up)  45.8 us
    ppermute x2, waiting for transfers between devices, extended(): after = lax.ppermute(initial, axis, down)  36.9 us
    all_to_all x1, blocking collectives, shards(): lax.all_to_all(outputs, 'hd', split_axis=2, concat_axis=3, tiled=True)  25.9 us
    dot_general x6, matrix products, attend(): jnp.einsum('qd,kd->qk', query_block, key_block, preferred_element_type=jn...  18.6 us
    slice x6, local copies, waits for them, and re-layouts, attend(): key_block = pair_block[:, :, :, 0, 0].reshape(-1, head_dim)  16.3 us
    ppermute x2, starting transfers between devices, extended(): before = lax.ppermute(last, axis, up)  15 us
  transfers between devices with their start and end apart: 4, of which 4 were waited for; matrix products, arithmetic and copies ran while one was open for 1% of the time, Pallas kernels for 0%

commit v1 on v0

v1 whole, which is shorter than its diff:
```python
import functools
import math

import jax
import jax.numpy as jnp
from jax import lax
from jax.experimental import pallas as pl
from jax.experimental.pallas import tpu as pltpu
from jax.sharding import PartitionSpec as P

TT = 2
TH = 2
TW = 8
NEG = -1e30


def normed(x, gain):
    meansq = jnp.mean(x * x, axis=-1, keepdims=True)
    return x * lax.rsqrt(meansq + 1e-06) * gain


def pack_kernel(entries, parts, heads_local, groups, *refs):
    part_refs = refs[: len(parts)]
    qg_ref, kg_ref, out_ref = refs[len(parts) :]
    rows, cols = part_refs[0].shape[1:3]
    head_dim = qg_ref.shape[-1]
    gains = {0: qg_ref[...].reshape(1, 1, head_dim), 1: kg_ref[...].reshape(1, 1, head_dim)}
    for dest in range(groups):
        for slot, (part, head) in enumerate(entries):
            at = (heads_local * dest + head) * head_dim
            x = part_refs[parts.index(part)][0, :, :, at : at + head_dim].astype(jnp.float32)
            if part in gains:
                x = normed(x, gains[part])
            out_ref[dest, slot, 0] = x.reshape(rows * cols, head_dim).astype(jnp.bfloat16)


def pack(qkv, q_gain, k_gain, entries, heads_local, groups):
    frames, rows, cols, channels = qkv.shape
    head_dim = q_gain.shape[-1]
    third = channels // 3
    parts = sorted({part for part, _ in entries})
    n = len(entries)
    gain_spec = pl.BlockSpec((1, head_dim), lambda f: (0, 0))
    return pl.pallas_call(
        functools.partial(pack_kernel, entries, parts, heads_local, groups),
        grid=(frames,),
        in_specs=[
            pl.BlockSpec((1, rows, cols, third), functools.partial(lambda p, f: (f, 0, 0, p), part))
            for part in parts
        ]
        + [gain_spec, gain_spec],
        out_specs=pl.BlockSpec(
            (groups, n, 1, rows * cols, head_dim), lambda f: (0, 0, f, 0, 0)
        ),
        out_shape=jax.ShapeDtypeStruct((groups, n, frames, rows * cols, head_dim), jnp.bfloat16),
        cost_estimate=pl.CostEstimate(
            flops=10 * groups * n * frames * rows * cols * head_dim,
            bytes_accessed=2 * 2 * groups * n * frames * rows * cols * head_dim,
            transcendentals=0,
        ),
        name="pack",
    )(*([qkv] * len(parts)), q_gain.reshape(1, -1), k_gain.reshape(1, -1))


def attend_kernel(
    head, q_slot, span, reach, scale,
    info_ref, c_ref, t0_ref, t1_ref, h0_ref, h1_ref, q_ref, out_ref, k_ref, v_ref, bias_ref,
):
    groups, _, frames, own, head_dim = c_ref.shape
    rows = own // TW
    edge = TH * TW
    for slot, dst in ((0, k_ref), (1, v_ref)):
        dst[:, 0:TT, edge : edge + own] = t0_ref[:, slot]
        dst[:, TT : TT + frames, edge : edge + own] = c_ref[:, slot]
        dst[:, TT + frames : 2 * TT + frames, edge : edge + own] = t1_ref[:, slot]
        dst[:, :, 0:edge] = h0_ref[:, slot]
        dst[:, :, edge + own : 2 * edge + own] = h1_ref[:, slot]

    tiles_t = frames // TT
    tiles_h = rows // TH
    halves = groups // span
    nq = span * TT * edge
    nk = reach * 3 * TT * 3 * edge
    per_col = 3 * TT * 3 * edge
    rad_t = info_ref[3 * head]
    rad_h = info_ref[3 * head + 1]
    rad_w = info_ref[3 * head + 2]
    base_t = info_ref.shape[0] - (tiles_t + 2) - (tiles_h + 2)
    base_h = base_t + tiles_t + 2

    q_col = lax.broadcasted_iota(jnp.int32, (nq, nk), 0) // (TT * edge)
    k_col = lax.broadcasted_iota(jnp.int32, (nq, nk), 1) // per_col
    for half in range(halves):
        first = min(max(half * span - 1, 0), groups - reach)
        gap = jnp.abs(q_col + (half * span - first) - k_col)
        bias_ref[half] = jnp.where(gap <= rad_w, 0.0, NEG)

    at = lax.broadcasted_iota(jnp.int32, (1, nk), 1) % per_col
    k_frame = at // (3 * edge)
    k_row = (at % (3 * edge)) // TW
    at_q = lax.broadcasted_iota(jnp.int32, (nq, 1), 0) % (TT * edge)
    q_frame = at_q // edge
    q_row = (at_q % edge) // TW

    @pl.loop(0, tiles_t * tiles_h * halves)
    def _(step):
        half = step % halves
        th = (step // halves) % tiles_h
        tt = step // (halves * tiles_h)
        first = jnp.clip(half * span - 1, 0, groups - reach)
        ok_t = jnp.zeros((1, nk), jnp.bool_)
        ok_h = jnp.zeros((1, nk), jnp.bool_)
        for near in range(3):
            away = abs(near - 1)
            live_t = jnp.where(away <= rad_t, info_ref[base_t + tt + near], 0)
            live_h = jnp.where(away <= rad_h, info_ref[base_h + th + near], 0)
            ok_t = ok_t | ((k_frame // TT == near) & (k_frame % TT < live_t))
            ok_h = ok_h | ((k_row // TH == near) & (k_row % TH < live_h))
        key_bias = jnp.where(ok_t & ok_h, 0.0, NEG)
        q_rows = pl.ds(pl.multiple_of(th * edge, edge), edge)
        k_rows = pl.ds(pl.multiple_of(th * edge, edge), 3 * edge)
        q_cols = pl.ds(half * span, span)
        k_cols = pl.ds(first, reach)
        q_frames = pl.ds(tt * TT, TT)
        k_frames = pl.ds(tt * TT, 3 * TT)
        q = q_ref[q_cols, q_slot, q_frames, q_rows, :].reshape(nq, head_dim)
        k = k_ref[k_cols, k_frames, k_rows, :].reshape(nk, head_dim)
        v = v_ref[k_cols, k_frames, k_rows, :].reshape(nk, head_dim)
        scores = lax.dot_general(
            q, k, (((1,), (1,)), ((), ())), preferred_element_type=jnp.float32
        )
        scores = scores * scale + (bias_ref[half] + key_bias)
        top = jnp.max(scores, axis=1, keepdims=True)
        raised = jnp.exp(scores - top)
        summed = jnp.sum(raised, axis=1, keepdims=True)
        blended = jnp.dot(
            raised.astype(jnp.bfloat16), v, preferred_element_type=jnp.float32
        )
        live = (q_frame < info_ref[base_t + tt + 1]) & (q_row < info_ref[base_h + th + 1])
        result = jnp.where(live, blended / summed, 0.0).astype(jnp.bfloat16)
        out_ref[q_cols, q_frames, q_rows, :] = result.reshape(span, TT, edge, head_dim)


def attend(info, center, t0, t1, h0, h1, queries, head, q_slot):
    groups, _, frames, own, head_dim = center.shape
    span = groups // 2 if groups > 1 else groups
    reach = min(span + 1, groups)
    rows = own // TW
    edge = TH * TW
    nq = span * TT * edge
    nk = reach * 9 * TT * edge
    steps = (frames // TT) * (rows // TH) * (groups // span)
    vmem = pl.BlockSpec(memory_space=pltpu.VMEM)
    ext = (groups, frames + 2 * TT, own + 2 * edge, head_dim)
    return pl.pallas_call(
        functools.partial(attend_kernel, head, q_slot, span, reach, 1.0 / math.sqrt(head_dim)),
        in_specs=[pl.BlockSpec(memory_space=pltpu.SMEM)] + [vmem] * 6,
        out_specs=vmem,
        out_shape=jax.ShapeDtypeStruct((groups, frames, own, head_dim), jnp.bfloat16),
        scratch_shapes=[
            pltpu.VMEM(ext, jnp.bfloat16),
            pltpu.VMEM(ext, jnp.bfloat16),
            pltpu.VMEM((groups // span, nq, nk), jnp.float32),
        ],
        cost_estimate=pl.CostEstimate(
            flops=4 * steps * nq * nk * head_dim,
            bytes_accessed=4 << 20,
            transcendentals=steps * nq * nk,
        ),
        compiler_params=pltpu.CompilerParams(vmem_limit_bytes=40 << 20),
        name="attend",
    )(info, center, t0, t1, h0, h1, queries)


def unpack_kernel(*refs):
    out_ref = refs[-1]
    rows, cols = out_ref.shape[1:3]
    groups, _, own, head_dim = refs[0].shape
    heads = len(refs) - 1
    for head, ref in enumerate(refs[:-1]):
        for group in range(groups):
            at = (heads * group + head) * head_dim
            x = ref[group, 0].astype(jnp.float32).reshape(rows, cols, head_dim)
            out_ref[0, :, :, at : at + head_dim] = x.astype(jnp.bfloat16)


def unpack(pieces, rows, cols):
    groups, frames, own, head_dim = pieces[0].shape
    channels = groups * len(pieces) * head_dim
    return pl.pallas_call(
        unpack_kernel,
        grid=(frames,),
        in_specs=[pl.BlockSpec((groups, 1, own, head_dim), lambda f: (0, f, 0, 0))] * len(pieces),
        out_specs=pl.BlockSpec((1, rows, cols, channels), lambda f: (f, 0, 0, 0)),
        out_shape=jax.ShapeDtypeStruct((frames, rows, cols, channels), jnp.bfloat16),
        name="unpack",
    )(*pieces)


def shifted(value, axis, step):
    size = lax.axis_size(axis)
    if step > 0:
        return lax.ppermute(value, axis, [(i, i + 1) for i in range(size - 1)])
    return lax.ppermute(value, axis, [(i + 1, i) for i in range(size - 1)])


def exchange(value):
    return lax.all_to_all(value, "hd", split_axis=0, concat_axis=0, tiled=True)


def shards(qkv, q_gain, k_gain, windows, frame_counts, row_counts):
    frames, rows, cols, channels = qkv.shape
    head_dim = q_gain.shape[0]
    groups = lax.axis_size("hd")
    heads_local = channels // (3 * head_dim) // groups
    edge = TH * TW
    own = rows * cols
    tiles_t = frames // TT
    tiles_h = rows // TH
    near_t = lax.dynamic_slice(
        jnp.pad(frame_counts, (1, 1)), (lax.axis_index("ta") * tiles_t,), (tiles_t + 2,)
    )
    near_h = lax.dynamic_slice(
        jnp.pad(row_counts, (1, 1)), (lax.axis_index("ha") * tiles_h,), (tiles_h + 2,)
    )
    info = jnp.concatenate([windows.reshape(-1), near_t, near_h])

    plan = [[(1, head), (2, head)] for head in range(heads_local)]
    where_q = {}
    for head in range(heads_local):
        ride = min(head + 1, heads_local - 1)
        where_q[head] = (ride, len(plan[ride]))
        plan[ride].append((0, head))
    got = [exchange(pack(qkv, q_gain, k_gain, tuple(p), heads_local, groups)) for p in plan]

    outs = []
    for head in range(heads_local):
        center = got[head]
        pair = center[:, :2]
        t0 = shifted(pair[:, :, frames - TT :], "ta", 1)
        t1 = shifted(pair[:, :, :TT], "ta", -1)
        low = jnp.concatenate(
            [t0[:, :, :, :edge], pair[:, :, :, :edge], t1[:, :, :, :edge]], axis=2
        )
        high = jnp.concatenate(
            [t0[:, :, :, own - edge :], pair[:, :, :, own - edge :], t1[:, :, :, own - edge :]],
            axis=2,
        )
        h0 = shifted(high, "ha", 1)
        h1 = shifted(low, "ha", -1)
        ride, slot = where_q[head]
        out = attend(info, center, t0, t1, h0, h1, got[ride], head, slot)
        outs.append(exchange(out))
    return unpack(outs, rows, cols)


def solution(mesh):
    return jax.shard_map(
        shards,
        mesh=mesh,
        in_specs=(P("ta", "ha", "hd", None), P(), P(), P("hd", None), P(), P()),
        out_specs=P("ta", "ha", "hd", None),
        check_vma=False,
    )
```

time: 369 us -> 211 us (0.57)
  the two profiles are of different devices: /device:TPU:67 before, /device:TPU:3 now
where the time goes in v1:
time: 211 us; the launch traced here: 210 us
  starting transfers between devices  75.5 us (36%)
  waiting for transfers between devices  72.4 us (34%)
  Pallas kernels  36.4 us (17%)
  blocking collectives  15.3 us (7%)
  other arithmetic  5.27 us (2%)
  local copies, waits for them, and re-layouts  4.51 us (2%)
    ppermute x6, waiting for transfers between devices, shifted(): return lax.ppermute(value, axis, [(i + 1, i) for i in range(size - 1)])  41.7 us
    all_to_all x5, starting transfers between devices, exchange(): return lax.all_to_all(value, 'hd', split_axis=0, concat_axis=0, tiled=True)  26.8 us
    ppermute x6, starting transfers between devices, shifted(): return lax.ppermute(value, axis, [(i + 1, i) for i in range(size - 1)])  25.7 us
    all_to_all x5, waiting for transfers between devices, exchange(): return lax.all_to_all(value, 'hd', split_axis=0, concat_axis=0, tiled=True)  25 us
    ppermute x6, starting transfers between devices, shifted(): return lax.ppermute(value, axis, [(i, i + 1) for i in range(size - 1)])  23 us
    pallas_call x3, Pallas kernels, attend(): pl.pallas_call(functools.partial(attend_kernel, head, q_slot, span, reach...  21.5 us
    all_to_all x1, blocking collectives, exchange(): return lax.all_to_all(value, 'hd', split_axis=0, concat_axis=0, tiled=True)  15.3 us
    pallas_call x3, Pallas kernels, pack(): pl.pallas_call(functools.partial(pack_kernel, entries, parts, heads_local...  11.7 us
  transfers between devices with their start and end apart: 17, of which 7 were waited for; matrix products, arithmetic and copies ran while one was open for 4% of the time, Pallas kernels for 14%

profile of v1, /device:TPU:3, one launch (start us, length us, event | category | flops | bytes accessed | tf_op | source)
XLA Modules:
  0.0 209.8 jit_solution(4350175830803278512)
XLA Ops:
  0.0 3.7 %pack.3 = bf16[8,2,4,32,128]{4,3,2,1,0:T(8,128)(2,1)} custom-call(bf16[4,4,8,9216]{3,2,1,0:T(8,128)(2,1)} %refs_2_.3, bf16[4,4,8,9216]{3,2,1,0:T(8,128)(2,1)} %refs_2_.3, f32[1,128]{1,0:T(1,128)} %bitcast.2, f32[1,128]{1,0:T(1,128)} %bitcast.5), custom_call_target="tpu_custom_call" | custom-call | flops 2621440 | bytes 1048576 | tf_op jit(solution)/shard_map/pack/pallas_call | solution.py:44
  3.7 6.8 %all-to-all-start = ((bf16[8,2,4,32,128]{4,3,2,1,0:T(8,128)(2,1)}), bf16[8,2,4,32,128]{4,3,2,1,0:T(8,128)(2,1)S(1)}, u32[]{:S(2)}, u32[]{:S(2)}) async-start(bf16[8,2,4,32,128]{4,3,2,1,0:T(8,128)(2,1)} %pack.3), calls=%async_computation | async-start | bytes 1048576 | tf_op jit(solution)/shard_map/all_to_all | solution.py:208
  10.5 3.9 %pack.4 = bf16[8,3,4,32,128]{4,3,2,1,0:T(8,128)(2,1)} custom-call(bf16[4,4,8,9216]{3,2,1,0:T(8,128)(2,1)} %refs_2_.3, bf16[4,4,8,9216]{3,2,1,0:T(8,128)(2,1)} %refs_2_.3, bf16[4,4,8,9216]{3,2,1,0:T(8,128)(2,1)} %refs_2_.3, f32[1,128]{1,0:T(1,128)} %bitcast.3, f32[1,128]{1,0:T(1,128)} %bitcast.6), custom_call_target="tpu_custom_call" | custom-call | flops 3932160 | bytes 1572864 | tf_op jit(solution)/shard_map/pack/pallas_call | solution.py:44
  14.5 14.0 %all-to-all-done.c_ref = bf16[8,2,4,32,128]{4,3,2,1,0:T(8,128)(2,1)S(1)} async-done(((bf16[8,2,4,32,128]{4,3,2,1,0:T(8,128)(2,1)}), bf16[8,2,4,32,128]{4,3,2,1,0:T(8,128)(2,1)S(1)}, u32[]{:S(2)}, u32[]{:S(2)}) %all-to-all-start) | async-done | bytes 524320 | tf_op jit(solution)/shard_map/all_to_all | solution.py:208
  28.5 3.5 %all-to-all-start.1 = ((bf16[8,3,4,32,128]{4,3,2,1,0:T(8,128)(2,1)}), bf16[8,3,4,32,128]{4,3,2,1,0:T(8,128)(2,1)S(1)}, u32[]{:S(2)}, u32[]{:S(2)}) async-start(bf16[8,3,4,32,128]{4,3,2,1,0:T(8,128)(2,1)} %pack.4), calls=%async_computation.1 | async-start | bytes 1572864 | tf_op jit(solution)/shard_map/all_to_all | solution.py:208
  33.1 10.6 %collective-permute-start = (bf16[8,2,2,32,128]{4,3,2,1,0:T(8,128)(2,1)}, bf16[8,2,2,32,128]{4,3,2,1,0:T(8,128)(2,1)S(1)}, u32[]{:S(2)}, u32[]{:S(2)}) collective-permute-start(bf16[8,2,2,32,128]{4,3,2,1,0:T(8,128)(2,1)} %get-tuple-element.16), channel_id=1, source_target_pairs={{0,64},{64,128},{128,192},{192,256},{256,320},{320,384},{384,448},... | collective-permute-start | bytes 786440 | tf_op jit(solution)/shard_map/ppermute | solution.py:203
  43.8 4.1 %pack.5 = bf16[8,4,4,32,128]{4,3,2,1,0:T(8,128)(2,1)} custom-call(bf16[4,4,8,9216]{3,2,1,0:T(8,128)(2,1)} %refs_2_.3, bf16[4,4,8,9216]{3,2,1,0:T(8,128)(2,1)} %refs_2_.3, bf16[4,4,8,9216]{3,2,1,0:T(8,128)(2,1)} %refs_2_.3, f32[1,128]{1,0:T(1,128)} %bitcast.4, f32[1,128]{1,0:T(1,128)} %bitcast.7), custom_call_target="tpu_custom_call" | custom-call | flops 5242880 | bytes 2097152 | tf_op jit(solution)/shard_map/pack/pallas_call | solution.py:44
  49.8 5.7 %all-to-all-done.1.q_ref.c_ref = bf16[8,3,4,32,128]{4,3,2,1,0:T(8,128)(2,1)S(1)} async-done(((bf16[8,3,4,32,128]{4,3,2,1,0:T(8,128)(2,1)}), bf16[8,3,4,32,128]{4,3,2,1,0:T(8,128)(2,1)S(1)}, u32[]{:S(2)}, u32[]{:S(2)}) %all-to-all-start.1) | async-done | bytes 786464 | tf_op jit(solution)/shard_map/all_to_all | solution.py:208
  55.5 3.6 %all-to-all-start.3 = ((bf16[8,4,4,32,128]{4,3,2,1,0:T(8,128)(2,1)}), bf16[8,4,4,32,128]{4,3,2,1,0:T(8,128)(2,1)S(1)}, u32[]{:S(2)}, u32[]{:S(2)}) async-start(bf16[8,4,4,32,128]{4,3,2,1,0:T(8,128)(2,1)} %pack.5), calls=%async_computation.3 | async-start | bytes 2097152 | tf_op jit(solution)/shard_map/all_to_all | solution.py:208
  59.1 13.2 %collective-permute-done.1.t1_ref = bf16[8,2,2,32,128]{4,3,2,1,0:T(8,128)(2,1)S(1)} collective-permute-done((bf16[8,2,2,32,128]{4,3,2,1,0:T(8,128)(2,1)}, bf16[8,2,2,32,128]{4,3,2,1,0:T(8,128)(2,1)S(1)}, u32[]{:S(2)}, u32[]{:S(2)}) %collective-permute-start.1) | collective-permute-done | bytes 262176 | tf_op jit(solution)/shard_map/ppermute | solution.py:204
  75.7 3.4 %collective-permute-start.4 = (bf16[8,2,2,32,128]{4,3,2,1,0:T(8,128)(2,1)S(1)}, bf16[8,2,2,32,128]{4,3,2,1,0:T(8,128)(2,1)S(1)}, u32[]{:S(2)}, u32[]{:S(2)}) collective-permute-start(bf16[8,2,2,32,128]{4,3,2,1,0:T(8,128)(2,1)S(1)} %get-tuple-element.12), channel_id=1, source_target_pairs={{0,64},{64,128},{128,192},{192,256},{256,320},{320,384},{384,448},... | collective-permute-start | bytes 786440 | tf_op jit(solution)/shard_map/ppermute | solution.py:203
  83.2 6.9 %collective-permute-start.5 = (bf16[8,2,2,32,128]{4,3,2,1,0:T(8,128)(2,1)S(1)}, bf16[8,2,2,32,128]{4,3,2,1,0:T(8,128)(2,1)S(1)}, u32[]{:S(2)}, u32[]{:S(2)}) collective-permute-start(bf16[8,2,2,32,128]{4,3,2,1,0:T(8,128)(2,1)S(1)} %get-tuple-element.11), channel_id=1, source_target_pairs={{64,0},{128,64},{192,128},{256,192},{320,256},{384,320},{448,384},... | collective-permute-start | bytes 786440 | tf_op jit(solution)/shard_map/ppermute | solution.py:204
  90.1 5.7 %collective-permute-done.4.t0_ref = bf16[8,2,2,32,128]{4,3,2,1,0:T(8,128)(2,1)S(1)} collective-permute-done((bf16[8,2,2,32,128]{4,3,2,1,0:T(8,128)(2,1)S(1)}, bf16[8,2,2,32,128]{4,3,2,1,0:T(8,128)(2,1)S(1)}, u32[]{:S(2)}, u32[]{:S(2)}) %collective-permute-start.4) | collective-permute-done | bytes 262176 | tf_op jit(solution)/shard_map/ppermute | solution.py:203
  95.9 16.9 %collective-permute-done.5.t1_ref = bf16[8,2,2,32,128]{4,3,2,1,0:T(8,128)(2,1)S(1)} collective-permute-done((bf16[8,2,2,32,128]{4,3,2,1,0:T(8,128)(2,1)S(1)}, bf16[8,2,2,32,128]{4,3,2,1,0:T(8,128)(2,1)S(1)}, u32[]{:S(2)}, u32[]{:S(2)}) %collective-permute-start.5) | collective-permute-done | bytes 262176 | tf_op jit(solution)/shard_map/ppermute | solution.py:204
  123.4 7.1 %attend.3 = bf16[8,4,32,128]{3,2,1,0:T(8,128)(2,1)S(1)} custom-call(s32[17]{0:T(128)S(1)} %pad_add_fusion.info_ref, bf16[8,2,4,32,128]{4,3,2,1,0:T(8,128)(2,1)S(1)} %all-to-all-done.c_ref, bf16[8,2,2,32,128]{4,3,2,1,0:T(8,128)(2,1)S(1)} %collective-permute-done.t0_ref, bf16[8,2,2,32,128]{4,3,2,1,0:T(8,128)(2,1)S(1)} %copy-done.1, ...), custom_call_target="tpu_custom_call" | custom-call | flops 754974720 | bytes 4194304 | tf_op jit(solution)/shard_map/attend/pallas_call | solution.py:155
  131.3 6.5 %all-to-all-start.2 = ((bf16[8,4,32,128]{3,2,1,0:T(8,128)(2,1)}), bf16[8,4,32,128]{3,2,1,0:T(8,128)(2,1)}, u32[]{:S(2)}, u32[]{:S(2)}) async-start(bf16[8,4,32,128]{3,2,1,0:T(8,128)(2,1)} %copy-done.2), calls=%async_computation.2 | async-start | bytes 524288 | tf_op jit(solution)/shard_map/all_to_all | solution.py:208
  137.8 8.2 %collective-permute-start.9 = (bf16[8,2,2,32,128]{4,3,2,1,0:T(8,128)(2,1)}, bf16[8,2,2,32,128]{4,3,2,1,0:T(8,128)(2,1)S(1)}, u32[]{:S(2)}, u32[]{:S(2)}) collective-permute-start(bf16[8,2,2,32,128]{4,3,2,1,0:T(8,128)(2,1)} %get-tuple-element.7), channel_id=1, source_target_pairs={{64,0},{128,64},{192,128},{256,192},{320,256},{384,320},{448,384},... | collective-permute-start | bytes 786440 | tf_op jit(solution)/shard_map/ppermute | solution.py:204
  146.1 11.5 %collective-permute-done.9.t1_ref = bf16[8,2,2,32,128]{4,3,2,1,0:T(8,128)(2,1)S(1)} collective-permute-done((bf16[8,2,2,32,128]{4,3,2,1,0:T(8,128)(2,1)}, bf16[8,2,2,32,128]{4,3,2,1,0:T(8,128)(2,1)S(1)}, u32[]{:S(2)}, u32[]{:S(2)}) %collective-permute-start.9) | collective-permute-done | bytes 262176 | tf_op jit(solution)/shard_map/ppermute | solution.py:204
  164.5 7.2 %attend.4 = bf16[8,4,32,128]{3,2,1,0:T(8,128)(2,1)S(1)} custom-call(s32[17]{0:T(128)S(1)} %pad_add_fusion.info_ref, bf16[8,3,4,32,128]{4,3,2,1,0:T(8,128)(2,1)S(1)} %all-to-all-done.1.q_ref.c_ref, bf16[8,2,2,32,128]{4,3,2,1,0:T(8,128)(2,1)S(1)} %collective-permute-done.4.t0_ref, bf16[8,2,2,32,128]{4,3,2,1,0:T(8,128)(2,1)S(1)} %collective-permute-done.5.t1_ref, ...), custom_call_target="tpu_custom_call" | custom-call | flops 754974720 | bytes 4194304 | tf_op jit(solution)/shard_map/attend/pallas_call | solution.py:155
  172.4 6.4 %all-to-all-start.4 = ((bf16[8,4,32,128]{3,2,1,0:T(8,128)(2,1)}), bf16[8,4,32,128]{3,2,1,0:T(8,128)(2,1)S(1)}, u32[]{:S(2)}, u32[]{:S(2)}) async-start(bf16[8,4,32,128]{3,2,1,0:T(8,128)(2,1)} %copy-done.3), calls=%async_computation.4 | async-start | bytes 524288 | tf_op jit(solution)/shard_map/all_to_all | solution.py:208
  178.8 7.2 %attend.5 = bf16[8,4,32,128]{3,2,1,0:T(8,128)(2,1)S(1)} custom-call(s32[17]{0:T(128)S(1)} %pad_add_fusion.info_ref, bf16[8,4,4,32,128]{4,3,2,1,0:T(8,128)(2,1)S(1)} %all-to-all-done.3.q_ref.c_ref, bf16[8,2,2,32,128]{4,3,2,1,0:T(8,128)(2,1)S(1)} %collective-permute-done.8.t0_ref, bf16[8,2,2,32,128]{4,3,2,1,0:T(8,128)(2,1)S(1)} %collective-permute-done.9.t1_ref, ...), custom_call_target="tpu_custom_call" | custom-call | flops 754974720 | bytes 4194304 | tf_op jit(solution)/shard_map/attend/pallas_call | solution.py:155
  185.9 5.2 %all-to-all-done.4.refs_1_ = bf16[8,4,32,128]{3,2,1,0:T(8,128)(2,1)S(1)} async-done(((bf16[8,4,32,128]{3,2,1,0:T(8,128)(2,1)}), bf16[8,4,32,128]{3,2,1,0:T(8,128)(2,1)S(1)}, u32[]{:S(2)}, u32[]{:S(2)}) %all-to-all-start.4) | async-done | bytes 262176 | tf_op jit(solution)/shard_map/all_to_all | solution.py:208
  191.2 15.3 %all_to_all.30.refs_2_ = bf16[8,4,32,128]{3,2,1,0:T(8,128)(2,1)} all-to-all(bf16[8,4,32,128]{3,2,1,0:T(8,128)(2,1)S(1)} %attend.5), channel_id=1, replica_groups=mesh['ta'=8,'ha'=8,'hd'=8] {'hd'}, dimensions={0} | all-to-all | bytes 524288 | tf_op jit(solution)/shard_map/all_to_all | solution.py:208
  206.5 3.3 %unpack.1 = bf16[4,4,8,3072]{3,2,1,0:T(8,128)(2,1)} custom-call(bf16[8,4,32,128]{3,2,1,0:T(8,128)(2,1)} %all-to-all-done.2.refs_0_, bf16[8,4,32,128]{3,2,1,0:T(8,128)(2,1)} %copy-done.4, bf16[8,4,32,128]{3,2,1,0:T(8,128)(2,1)} %all_to_all.30.refs_2_), custom_call_target="tpu_custom_call" | custom-call | tf_op jit(solution)/shard_map/unpack/pallas_call | solution.py:190
  (55 shorter events, 29.4 us)
Async XLA Ops:
  3.7 24.8 %all-to-all-start = ((bf16[8,2,4,32,128]{4,3,2,1,0:T(8,128)(2,1)}), bf16[8,2,4,32,128]{4,3,2,1,0:T(8,128)(2,1)S(1)}, u32[]{:S(2)}, u32[]{:S(2)}) async-start(bf16[8,2,4,32,128]{4,3,2,1,0:T(8,128)(2,1)} %pack.3), calls=%async_computation | async-start | bytes 1048576 | tf_op jit(solution)/shard_map/all_to_all | solution.py:208
  10.5 21.5 %copy-start.5 = (s32[3,3]{1,0:T(4,128)S(1)}, s32[3,3]{1,0:T(4,128)}, u32[]{:S(2)}) copy-start(s32[3,3]{1,0:T(4,128)} %param.9) | copy-start | bytes 112
  10.5 21.6 %copy-start.6 = (s32[16]{0:T(128)S(1)}, s32[16]{0:T(128)}, u32[]{:S(2)}) copy-start(s32[16]{0:T(128)} %param.11) | copy-start | bytes 196
  10.5 21.6 %copy-start.7 = (s32[16]{0:T(128)S(1)}, s32[16]{0:T(128)}, u32[]{:S(2)}) copy-start(s32[16]{0:T(128)} %param.10) | copy-start | bytes 196
  28.5 27.0 %all-to-all-start.1 = ((bf16[8,3,4,32,128]{4,3,2,1,0:T(8,128)(2,1)}), bf16[8,3,4,32,128]{4,3,2,1,0:T(8,128)(2,1)S(1)}, u32[]{:S(2)}, u32[]{:S(2)}) async-start(bf16[8,3,4,32,128]{4,3,2,1,0:T(8,128)(2,1)} %pack.4), calls=%async_computation.1 | async-start | bytes 1572864 | tf_op jit(solution)/shard_map/all_to_all | solution.py:208
  33.1 26.0 %collective-permute-start = (bf16[8,2,2,32,128]{4,3,2,1,0:T(8,128)(2,1)}, bf16[8,2,2,32,128]{4,3,2,1,0:T(8,128)(2,1)S(1)}, u32[]{:S(2)}, u32[]{:S(2)}) collective-permute-start(bf16[8,2,2,32,128]{4,3,2,1,0:T(8,128)(2,1)} %get-tuple-element.16), channel_id=1, source_target_pairs={{0,64},{64,128},{128,192},{192,256},{256,320},{320,384},{384,448},... | collective-permute-start | bytes 786440 | tf_op jit(solution)/shard_map/ppermute | solution.py:203
  47.8 24.5 %collective-permute-start.1 = (bf16[8,2,2,32,128]{4,3,2,1,0:T(8,128)(2,1)}, bf16[8,2,2,32,128]{4,3,2,1,0:T(8,128)(2,1)S(1)}, u32[]{:S(2)}, u32[]{:S(2)}) collective-permute-start(bf16[8,2,2,32,128]{4,3,2,1,0:T(8,128)(2,1)} %get-tuple-element.15), channel_id=1, source_target_pairs={{64,0},{128,64},{192,128},{256,192},{320,256},{384,320},{448,384},... | collective-permute-start | bytes 786440 | tf_op jit(solution)/shard_map/ppermute | solution.py:204
  55.5 64.2 %all-to-all-start.3 = ((bf16[8,4,4,32,128]{4,3,2,1,0:T(8,128)(2,1)}), bf16[8,4,4,32,128]{4,3,2,1,0:T(8,128)(2,1)S(1)}, u32[]{:S(2)}, u32[]{:S(2)}) async-start(bf16[8,4,4,32,128]{4,3,2,1,0:T(8,128)(2,1)} %pack.5), calls=%async_computation.3 | async-start | bytes 2097152 | tf_op jit(solution)/shard_map/all_to_all | solution.py:208
  72.3 17.8 %copy-start = (bf16[8,2,2,32,128]{4,3,2,1,0:T(8,128)(2,1)}, bf16[8,2,2,32,128]{4,3,2,1,0:T(8,128)(2,1)S(1)}, u32[]{:S(2)}) copy-start(bf16[8,2,2,32,128]{4,3,2,1,0:T(8,128)(2,1)S(1)} %collective-permute-done.1.t1_ref) | copy-start | bytes 786436
  73.2 49.2 %collective-permute-start.3 = (bf16[8,2,8,16,128]{4,3,2,1,0:T(8,128)(2,1)}, bf16[8,2,8,16,128]{4,3,2,1,0:T(8,128)(2,1)}, u32[]{:S(2)}, u32[]{:S(2)}) collective-permute-start(bf16[8,2,8,16,128]{4,3,2,1,0:T(8,128)(2,1)} %pad_maximum_fusion.1), channel_id=1, source_target_pairs={{8,0},{16,8},{24,16},{32,24},{40,32},{48,40},{56,48},{9,1},{17,9},... | collective-permute-start | bytes 1572872 | tf_op jit(solution)/shard_map/ppermute | solution.py:204
  75.7 20.2 %collective-permute-start.4 = (bf16[8,2,2,32,128]{4,3,2,1,0:T(8,128)(2,1)S(1)}, bf16[8,2,2,32,128]{4,3,2,1,0:T(8,128)(2,1)S(1)}, u32[]{:S(2)}, u32[]{:S(2)}) collective-permute-start(bf16[8,2,2,32,128]{4,3,2,1,0:T(8,128)(2,1)S(1)} %get-tuple-element.12), channel_id=1, source_target_pairs={{0,64},{64,128},{128,192},{192,256},{256,320},{320,384},{384,448},... | collective-permute-start | bytes 786440 | tf_op jit(solution)/shard_map/ppermute | solution.py:203
  79.9 42.5 %collective-permute-start.2 = (bf16[8,2,8,16,128]{4,3,2,1,0:T(8,128)(2,1)}, bf16[8,2,8,16,128]{4,3,2,1,0:T(8,128)(2,1)}, u32[]{:S(2)}, u32[]{:S(2)}) collective-permute-start(bf16[8,2,8,16,128]{4,3,2,1,0:T(8,128)(2,1)} %pad_maximum_fusion), channel_id=1, source_target_pairs={{0,8},{8,16},{16,24},{24,32},{32,40},{40,48},{48,56},{1,9},{9,17},... | collective-permute-start | bytes 1572872 | tf_op jit(solution)/shard_map/ppermute | solution.py:203
  83.2 29.6 %collective-permute-start.5 = (bf16[8,2,2,32,128]{4,3,2,1,0:T(8,128)(2,1)S(1)}, bf16[8,2,2,32,128]{4,3,2,1,0:T(8,128)(2,1)S(1)}, u32[]{:S(2)}, u32[]{:S(2)}) collective-permute-start(bf16[8,2,2,32,128]{4,3,2,1,0:T(8,128)(2,1)S(1)} %get-tuple-element.11), channel_id=1, source_target_pairs={{64,0},{128,64},{192,128},{256,192},{320,256},{384,320},{448,384},... | collective-permute-start | bytes 786440 | tf_op jit(solution)/shard_map/ppermute | solution.py:204
  113.7 50.8 %collective-permute-start.6 = (bf16[8,2,8,16,128]{4,3,2,1,0:T(8,128)(2,1)}, bf16[8,2,8,16,128]{4,3,2,1,0:T(8,128)(2,1)}, u32[]{:S(2)}, u32[]{:S(2)}) collective-permute-start(bf16[8,2,8,16,128]{4,3,2,1,0:T(8,128)(2,1)} %pad_maximum_fusion.2), channel_id=1, source_target_pairs={{0,8},{8,16},{16,24},{24,32},{32,40},{40,48},{48,56},{1,9},{9,17},... | collective-permute-start | bytes 1572872 | tf_op jit(solution)/shard_map/ppermute | solution.py:203
  116.5 48.0 %collective-permute-start.7 = (bf16[8,2,8,16,128]{4,3,2,1,0:T(8,128)(2,1)}, bf16[8,2,8,16,128]{4,3,2,1,0:T(8,128)(2,1)}, u32[]{:S(2)}, u32[]{:S(2)}) collective-permute-start(bf16[8,2,8,16,128]{4,3,2,1,0:T(8,128)(2,1)} %pad_maximum_fusion.3), channel_id=1, source_target_pairs={{8,0},{16,8},{24,16},{32,24},{40,32},{48,40},{56,48},{9,1},{17,9},... | collective-permute-start | bytes 1572872 | tf_op jit(solution)/shard_map/ppermute | solution.py:204
  120.5 25.5 %collective-permute-start.8 = (bf16[8,2,2,32,128]{4,3,2,1,0:T(8,128)(2,1)}, bf16[8,2,2,32,128]{4,3,2,1,0:T(8,128)(2,1)S(1)}, u32[]{:S(2)}, u32[]{:S(2)}) collective-permute-start(bf16[8,2,2,32,128]{4,3,2,1,0:T(8,128)(2,1)} %get-tuple-element.8), channel_id=1, source_target_pairs={{0,64},{64,128},{128,192},{192,256},{256,320},{320,384},{384,448},... | collective-permute-start | bytes 786440 | tf_op jit(solution)/shard_map/ppermute | solution.py:203
  122.5 1.0 copy-start.1
  130.6 0.7 copy-start.2
  131.3 41.1 %all-to-all-start.2 = ((bf16[8,4,32,128]{3,2,1,0:T(8,128)(2,1)}), bf16[8,4,32,128]{3,2,1,0:T(8,128)(2,1)}, u32[]{:S(2)}, u32[]{:S(2)}) async-start(bf16[8,4,32,128]{3,2,1,0:T(8,128)(2,1)} %copy-done.2), calls=%async_computation.2 | async-start | bytes 524288 | tf_op jit(solution)/shard_map/all_to_all | solution.py:208
  137.8 19.8 %collective-permute-start.9 = (bf16[8,2,2,32,128]{4,3,2,1,0:T(8,128)(2,1)}, bf16[8,2,2,32,128]{4,3,2,1,0:T(8,128)(2,1)S(1)}, u32[]{:S(2)}, u32[]{:S(2)}) collective-permute-start(bf16[8,2,2,32,128]{4,3,2,1,0:T(8,128)(2,1)} %get-tuple-element.7), channel_id=1, source_target_pairs={{64,0},{128,64},{192,128},{256,192},{320,256},{384,320},{448,384},... | collective-permute-start | bytes 786440 | tf_op jit(solution)/shard_map/ppermute | solution.py:204
  158.5 20.2 %collective-permute-start.10 = (bf16[8,2,8,16,128]{4,3,2,1,0:T(8,128)(2,1)}, bf16[8,2,8,16,128]{4,3,2,1,0:T(8,128)(2,1)}, u32[]{:S(2)}, u32[]{:S(2)}) collective-permute-start(bf16[8,2,8,16,128]{4,3,2,1,0:T(8,128)(2,1)} %pad_maximum_fusion.4), channel_id=1, source_target_pairs={{0,8},{8,16},{16,24},{24,32},{32,40},{40,48},{48,56},{1,9},{9,17},... | collective-permute-start | bytes 1572872 | tf_op jit(solution)/shard_map/ppermute | solution.py:203
  161.3 17.5 %collective-permute-start.11 = (bf16[8,2,8,16,128]{4,3,2,1,0:T(8,128)(2,1)}, bf16[8,2,8,16,128]{4,3,2,1,0:T(8,128)(2,1)}, u32[]{:S(2)}, u32[]{:S(2)}) collective-permute-start(bf16[8,2,8,16,128]{4,3,2,1,0:T(8,128)(2,1)} %pad_maximum_fusion.5), channel_id=1, source_target_pairs={{8,0},{16,8},{24,16},{32,24},{40,32},{48,40},{56,48},{9,1},{17,9},... | collective-permute-start | bytes 1572872 | tf_op jit(solution)/shard_map/ppermute | solution.py:204
  172.4 18.8 %all-to-all-start.4 = ((bf16[8,4,32,128]{3,2,1,0:T(8,128)(2,1)}), bf16[8,4,32,128]{3,2,1,0:T(8,128)(2,1)S(1)}, u32[]{:S(2)}, u32[]{:S(2)}) async-start(bf16[8,4,32,128]{3,2,1,0:T(8,128)(2,1)} %copy-done.3), calls=%async_computation.4 | async-start | bytes 524288 | tf_op jit(solution)/shard_map/all_to_all | solution.py:208
  191.2 15.3 %copy-start.4 = (bf16[8,4,32,128]{3,2,1,0:T(8,128)(2,1)}, bf16[8,4,32,128]{3,2,1,0:T(8,128)(2,1)S(1)}, u32[]{:S(2)}) copy-start(bf16[8,4,32,128]{3,2,1,0:T(8,128)(2,1)S(1)} %all-to-all-done.4.refs_1_) | copy-start | bytes 786436
  (1 other events, 0.7 us)

commit v2 on v1

v2 whole, which is shorter than its diff:
```python
import functools
import math

import jax
import jax.numpy as jnp
from jax import lax
from jax.experimental import pallas as pl
from jax.experimental.pallas import tpu as pltpu
from jax.sharding import PartitionSpec as P


TT = 2
TH = 2
TW = 8
NEG = -1e30

GRANT = 62 << 20


def cost(flops, size, transcendentals=0):
    return pl.CostEstimate(flops=flops, bytes_accessed=size, transcendentals=transcendentals)


def pack_kernel(entries, parts, heads_local, tiles, *refs):
    part_refs = refs[: len(parts)]
    qg_ref, kg_ref, out_ref = refs[len(parts) : len(parts) + 3]
    rim_refs = refs[len(parts) + 3 :]
    frames, rows, cols = part_refs[0].shape[:3]
    groups = out_ref.shape[0]
    head_dim = qg_ref.shape[-1]
    gains = {0: qg_ref[...].reshape(1, 1, 1, head_dim), 1: kg_ref[...].reshape(1, 1, 1, head_dim)}
    for dest in range(groups):
        for slot, (part, head) in enumerate(entries):
            at = (heads_local * dest + head) * head_dim
            x = part_refs[parts.index(part)][:, :, :, at : at + head_dim].astype(jnp.float32)
            if part in gains:
                meansq = jnp.mean(x * x, axis=-1, keepdims=True)
                x = x * lax.rsqrt(meansq + 1e-06) * gains[part]
            x = x.reshape(frames, rows * cols, head_dim).astype(jnp.bfloat16)
            out_ref[dest, slot * frames : (slot + 1) * frames] = x
            if tiles:
                rim_refs[0][dest, slot * TT : (slot + 1) * TT] = x[:TT]
                rim_refs[1][dest, slot * TT : (slot + 1) * TT] = x[frames - TT :]


def whole(shape):
    return pl.BlockSpec(shape, lambda i: (0,) * len(shape))


def one_step(kernel, in_specs, outs, size):
    shapes = [jax.ShapeDtypeStruct(shape, jnp.bfloat16) for shape in outs]
    return pl.pallas_call(
        kernel,
        grid=(1,),
        in_specs=in_specs,
        out_specs=[whole(shape) for shape in outs],
        out_shape=shapes,
        cost_estimate=cost(size, size),
        compiler_params=pltpu.CompilerParams(vmem_limit_bytes=GRANT),
    )


def pack(qkv, q_gain, k_gain, entries, heads_local, groups, tiles=False):
    frames, rows, cols, channels = qkv.shape
    head_dim = q_gain.shape[-1]
    third = channels // 3
    parts = sorted({part for part, _ in entries})
    n = len(entries)
    own = rows * cols
    outs = [(groups, n * frames, own, head_dim)] + [(groups, n * TT, own, head_dim)] * (2 * tiles)
    in_specs = [
        pl.BlockSpec((frames, rows, cols, third), functools.partial(lambda p, i: (0, 0, 0, p), part))
        for part in parts
    ] + [whole((1, head_dim))] * 2
    kernel = functools.partial(pack_kernel, entries, parts, heads_local, tiles)
    packed = one_step(kernel, in_specs, outs, 4 * math.prod(outs[0]))(
        *([qkv] * len(parts)), q_gain.reshape(1, -1), k_gain.reshape(1, -1)
    )
    return packed if tiles else packed[0]


def join_kernel(frames, c_ref, t0_ref, t1_ref, q_ref, out_ref):
    long = frames + 2 * TT
    for kv in range(2):
        at = kv * long
        out_ref[:, at : at + TT] = t0_ref[:, kv * TT : (kv + 1) * TT]
        out_ref[:, at + TT : at + TT + frames] = c_ref[:, kv * frames : (kv + 1) * frames]
        out_ref[:, at + TT + frames : at + long] = t1_ref[:, kv * TT : (kv + 1) * TT]
    out_ref[:, 2 * long :] = q_ref[...]


def join(center, t0, t1, queries):
    groups, slabs, own, head_dim = center.shape
    frames = slabs // 2
    total = 2 * (frames + 2 * TT) + queries.shape[1]
    arrays = (center, t0, t1, queries)
    out = (groups, total, own, head_dim)
    return one_step(
        functools.partial(join_kernel, frames),
        [whole(a.shape) for a in arrays],
        [out],
        4 * math.prod(out),
    )(*arrays)[0]


def tiles_kernel(frames, ref, first_ref, last_ref):
    for n in range(ref.shape[1] // frames):
        to = slice(n * TT, (n + 1) * TT)
        first_ref[:, to] = ref[:, n * frames : n * frames + TT]
        last_ref[:, to] = ref[:, (n + 1) * frames - TT : (n + 1) * frames]


def tiles_of(value, frames):
    groups, slabs, own, head_dim = value.shape
    out = (groups, slabs // frames * TT, own, head_dim)
    return one_step(
        functools.partial(tiles_kernel, frames),
        [whole(value.shape)],
        [out, out],
        8 * math.prod(out),
    )(value)


def rim_kernel(edge, counts, *refs):
    low_ref, high_ref = refs[-2:]
    sources = refs[:-2]
    own = sources[0].shape[2]
    total = sum(counts)
    for n in range(low_ref.shape[1] // total):
        at = n * total
        for ref, count in zip(sources, counts):
            src = slice(n * count, (n + 1) * count)
            low_ref[:, at : at + count] = ref[:, src, 0:edge]
            high_ref[:, at : at + count] = ref[:, src, own - edge : own]
            at += count


def rim(arrays, counts, heads, edge):
    groups, _, own, head_dim = arrays[0].shape
    out = (groups, heads * sum(counts), edge, head_dim)
    in_specs = [whole((groups, heads * c, own, head_dim)) for c in counts]
    return one_step(
        functools.partial(rim_kernel, edge, counts), in_specs, [out, out], 8 * math.prod(out)
    )(*arrays)


def attend_kernel(pieces, frames, span, reach, scale, slot, info_ref, *refs):
    count = len(pieces)
    piece_refs = refs[:count]
    q_ref = refs[count]
    out_ref, k_ref, v_ref, bias_ref = refs[-4:]
    here = slot + pl.program_id(0)
    if len(refs) > count + 5:
        out_ref[:, 0:slot] = refs[count + 1][...]
    groups = q_ref.shape[0]
    own, head_dim = q_ref.shape[2:]
    edge = TH * TW
    for ref, (spans, low) in zip(piece_refs, pieces):
        tokens = slice(low, low + ref.shape[2])
        at = 0
        for dst in (k_ref, v_ref):
            for start, n in spans:
                dst[:, start : start + n, tokens] = ref[:, at : at + n]
                at += n

    tiles_t = frames // TT
    tiles_h = own // edge
    halves = groups // span
    per_col = 3 * TT * 3 * edge
    nq = span * TT * edge
    nk = reach * per_col
    firsts = [min(max(half * span - 1, 0), groups - reach) for half in range(halves)]
    base_t = info_ref.shape[0] - (tiles_t + 2) - (tiles_h + 2)
    base_h = base_t + tiles_t + 2
    head = here
    rad_t = info_ref[3 * head]
    rad_h = info_ref[3 * head + 1]
    rad_w = info_ref[3 * head + 2]

    q_col = lax.broadcasted_iota(jnp.int32, (nq, nk), 0) // (TT * edge)
    k_col = lax.broadcasted_iota(jnp.int32, (nq, nk), 1) // per_col
    for half, first in enumerate(firsts):
        gap = jnp.abs(q_col - k_col + (half * span - first))
        bias_ref[half] = jnp.where(gap <= rad_w, 0.0, NEG)

    at = lax.broadcasted_iota(jnp.int32, (1, nk), 1) % per_col
    k_frame = at // (3 * edge)
    k_row = (at % (3 * edge)) // TW
    at_q = lax.broadcasted_iota(jnp.int32, (nq, 1), 0) % (TT * edge)
    q_frame = at_q // edge
    q_row = (at_q % edge) // TW

    @pl.loop(0, tiles_t * tiles_h)
    def _(step):
        th = step % tiles_h
        tt = step // tiles_h
        ok_t = jnp.zeros((1, nk), jnp.bool_)
        ok_h = jnp.zeros((1, nk), jnp.bool_)
        for near in range(3):
            away = abs(near - 1)
            live_t = jnp.where(away <= rad_t, info_ref[base_t + tt + near], 0)
            live_h = jnp.where(away <= rad_h, info_ref[base_h + th + near], 0)
            ok_t = ok_t | ((k_frame // TT == near) & (k_frame % TT < live_t))
            ok_h = ok_h | ((k_row // TH == near) & (k_row % TH < live_h))
        key_bias = jnp.where(ok_t & ok_h, 0.0, NEG)
        live = (q_frame < info_ref[base_t + tt + 1]) & (q_row < info_ref[base_h + th + 1])
        q_rows = pl.ds(pl.multiple_of(th * edge, edge), edge)
        k_rows = pl.ds(pl.multiple_of(th * edge, edge), 3 * edge)
        q_frames = pl.ds(tt * TT, TT)
        k_frames = pl.ds(tt * TT, 3 * TT)
        for half, first in enumerate(firsts):
            q_cols = slice(half * span, (half + 1) * span)
            k_cols = slice(first, first + reach)
            q = q_ref[q_cols, q_frames, q_rows, :].reshape(nq, head_dim)
            k = k_ref[k_cols, k_frames, k_rows, :].reshape(nk, head_dim)
            v = v_ref[k_cols, k_frames, k_rows, :].reshape(nk, head_dim)
            scores = lax.dot_general(
                q, k, (((1,), (1,)), ((), ())), preferred_element_type=jnp.float32
            )
            scores = scores * scale + (bias_ref[half] + key_bias)
            top = jnp.max(scores, axis=1, keepdims=True)
            raised = jnp.exp2(scores - top)
            summed = jnp.sum(raised, axis=1, keepdims=True)
            blended = jnp.dot(
                raised.astype(jnp.bfloat16), v, preferred_element_type=jnp.float32
            )
            result = jnp.where(live, blended / summed, 0.0).astype(jnp.bfloat16)
            out_ref[q_cols, here, q_frames, q_rows, :] = result.reshape(span, TT, edge, head_dim)


def attend(info, pieces, queries, q_block, heads, slot, before, frames):
    groups, _, own, head_dim = queries.shape
    span = max(groups // 2, 1)
    reach = min(span + 1, groups)
    edge = TH * TW
    nq = span * TT * edge
    nk = reach * 9 * TT * edge
    steps = heads * (frames // TT) * (own // edge) * (groups // span)
    ext = (groups, frames + 2 * TT, own + 2 * edge, head_dim)
    in_specs = [pl.BlockSpec(memory_space=pltpu.SMEM)]
    in_specs += [
        pl.BlockSpec(
            (groups, 2 * sum(n for _, n in spans), a.shape[2], head_dim), lambda h: (0, h, 0, 0)
        )
        for a, spans, _ in pieces
    ]
    in_specs += [
        pl.BlockSpec((groups, frames, own, head_dim), lambda h: (0, q_block + slot + h, 0, 0)),
    ]
    args = [info, *(a for a, _, _ in pieces), queries]
    total = slot + heads
    if before is not None:
        in_specs.append(pl.BlockSpec(before.shape, lambda h: (0, 0, 0, 0, 0)))
        args.append(before)
    return pl.pallas_call(
        functools.partial(
            attend_kernel,
            tuple((spans, low) for _, spans, low in pieces),
            frames,
            span,
            reach,
            math.log2(math.e) / math.sqrt(head_dim),
            slot,
        ),
        grid=(heads,),
        in_specs=in_specs,
        out_specs=pl.BlockSpec(memory_space=pltpu.VMEM),
        out_shape=pltpu.VMEM((groups, total, frames, own, head_dim), jnp.bfloat16),
        scratch_shapes=[
            pltpu.VMEM(ext, jnp.bfloat16),
            pltpu.VMEM(ext, jnp.bfloat16),
            pltpu.VMEM((groups // span, nq, nk), jnp.float32),
        ],
        cost_estimate=cost(4 * steps * nq * nk * head_dim, heads * (4 << 20), steps * nq * nk),
        compiler_params=pltpu.CompilerParams(vmem_limit_bytes=GRANT),
        name="attend",
    )(*args)


def unpack_kernel(in_ref, out_ref):
    frames, rows, cols = out_ref.shape[:3]
    groups, heads, _, _, head_dim = in_ref.shape
    for head in range(heads):
        for group in range(groups):
            at = (heads * group + head) * head_dim
            x = in_ref[group, head].astype(jnp.float32).reshape(frames, rows, cols, head_dim)
            out_ref[:, :, :, at : at + head_dim] = x.astype(jnp.bfloat16)


def unpack(value, rows, cols):
    groups, heads, frames, _, head_dim = value.shape
    out = (frames, rows, cols, groups * heads * head_dim)
    return pl.pallas_call(
        unpack_kernel,
        in_specs=[pl.BlockSpec(memory_space=pltpu.VMEM)],
        out_specs=pl.BlockSpec(memory_space=pltpu.VMEM),
        out_shape=jax.ShapeDtypeStruct(out, jnp.bfloat16),
        compiler_params=pltpu.CompilerParams(vmem_limit_bytes=16 << 20),
        name="unpack",
    )(value)


def shifted(value, axis, step):
    size = lax.axis_size(axis)
    pairs = [(i, i + 1) if step > 0 else (i + 1, i) for i in range(size - 1)]
    return lax.ppermute(value, axis, pairs)


def exchange(value):
    return lax.all_to_all(value, "hd", split_axis=0, concat_axis=0, tiled=True)


def shards(qkv, q_gain, k_gain, windows, frame_counts, row_counts):
    frames, rows, cols, channels = qkv.shape
    head_dim = q_gain.shape[0]
    groups = lax.axis_size("hd")
    heads = channels // (3 * head_dim) // groups
    edge = TH * TW
    own = rows * cols
    tiles_t = frames // TT
    tiles_h = rows // TH
    near_t = lax.dynamic_slice(
        jnp.pad(frame_counts, (1, 1)), (lax.axis_index("ta") * tiles_t,), (tiles_t + 2,)
    )
    near_h = lax.dynamic_slice(
        jnp.pad(row_counts, (1, 1)), (lax.axis_index("ha") * tiles_h,), (tiles_h + 2,)
    )
    info = jnp.concatenate([windows.reshape(-1), near_t, near_h])

    def packed(entries, tiles=False):
        return pack(qkv, q_gain, k_gain, tuple(entries), heads, groups, tiles)

    rest = heads - 1
    long = frames + 2 * TT
    value_z, first_z, last_z = packed([(1, rest), (2, rest)], True)
    tz0 = shifted(last_z, "ta", 1)
    tz1 = shifted(first_z, "ta", -1)
    value_n = packed([(part, head) for head in range(rest) for part in (1, 2)])
    got_n = exchange(value_n)
    value_q = packed([(0, head) for head in range(heads)])
    joined = join(value_z, tz0, tz1, value_q)
    got_z = exchange(joined)

    first_n, last_n = tiles_of(got_n, frames)
    tn0 = shifted(last_n, "ta", 1)
    tn1 = shifted(first_n, "ta", -1)
    low_c, high_c = rim((got_n,), (frames,), 2 * rest, edge)
    hc0 = shifted(high_c, "ha", 1)
    hc1 = shifted(low_c, "ha", -1)
    low_z, high_z = rim((got_z,), (long,), 2, edge)
    hz0 = shifted(high_z, "ha", 1)
    hz1 = shifted(low_z, "ha", -1)
    low_t, high_t = rim((tn0, tn1), (TT, TT), 2 * rest, edge)
    ht0 = shifted(high_t, "ha", 1)
    ht1 = shifted(low_t, "ha", -1)

    q_block = 2 * long // frames
    mine, every = ((TT, frames),), ((0, long),)
    beside = ((0, TT), (TT + frames, TT))
    pieces_n = (
        (got_n, mine, edge),
        (tn0, ((0, TT),), edge),
        (tn1, ((TT + frames, TT),), edge),
        (hc0, mine, 0),
        (hc1, mine, edge + own),
        (ht0, beside, 0),
        (ht1, beside, edge + own),
    )
    pieces_z = ((got_z, every, edge), (hz0, every, 0), (hz1, every, edge + own))
    out = attend(info, pieces_n, got_z, q_block, rest, 0, None, frames)
    out = attend(info, pieces_z, got_z, q_block, 1, rest, out, frames)
    return unpack(exchange(out), rows, cols)


def solution(mesh):
    return jax.shard_map(
        shards,
        mesh=mesh,
        in_specs=(P("ta", "ha", "hd", None), P(), P(), P("hd", None), P(), P()),
        out_specs=P("ta", "ha", "hd", None),
        check_vma=False,
    )
```

time: 211 us -> 181 us (0.86)
  the two profiles are of different devices: /device:TPU:3 before, /device:TPU:1 now
where the time goes in v2:
time: 181 us
  starting transfers between devices  91.6 us (51%)
  Pallas kernels  39.4 us (22%)
  blocking collectives  28.7 us (16%)
  waiting for transfers between devices  14.5 us (8%)
  local copies, waits for them, and re-layouts  5.46 us (3%)
    ppermute x10, starting transfers between devices, shifted(): return lax.ppermute(value, axis, pairs)  77.6 us
    all_to_all x1, blocking collectives, exchange(): return lax.all_to_all(value, 'hd', split_axis=0, concat_axis=0, tiled=True)  28.7 us
    pallas_call x2, Pallas kernels, attend(): pl.pallas_call(functools.partial(attend_kernel, tuple(((spans, low) for _...  18.5 us
    ppermute x10, waiting for transfers between devices, shifted(): return lax.ppermute(value, axis, pairs)  14.5 us
    all_to_all x2, starting transfers between devices, exchange(): return lax.all_to_all(value, 'hd', split_axis=0, concat_axis=0, tiled=True)  14 us
    pallas_call x3, Pallas kernels, pack(): one_step(kernel, in_specs, outs, 4 * math.prod(outs[0]))  7.86 us
    pallas_call x3, Pallas kernels, rim(): one_step(functools.partial(rim_kernel, edge, counts), in_specs, [out, out...  6.85 us
    unnamed x20, local copies, waits for them, and re-layouts  5.29 us
  transfers between devices with their start and end apart: 12, of which 3 were waited for; matrix products, arithmetic and copies ran while one was open for 0% of the time, Pallas kernels for 16%

profile of v2, /device:TPU:1, one launch (start us, length us, event | category | flops | bytes accessed | tf_op | source)
XLA Modules:
  0.0 180.6 jit_solution(4559940085648423123)
XLA Ops:
  0.0 2.7 %shard_map.68 = bf16[8,16,32,128]{3,2,1,0:T(8,128)(2,1)} custom-call(bf16[4,4,8,9216]{3,2,1,0:T(8,128)(2,1)} %refs_1_.3, bf16[4,4,8,9216]{3,2,1,0:T(8,128)(2,1)} %refs_1_.3, f32[1,128]{1,0:T(1,128)} %bitcast.2, f32[1,128]{1,0:T(1,128)} %bitcast.5), custom_call_target="tpu_custom_call" | custom-call | flops 2097152 | bytes 2097152 | tf_op jit(solution)/shard_map/pallas_call | solution.py:76
  2.7 7.6 %all-to-all-start.1 = ((bf16[8,16,32,128]{3,2,1,0:T(8,128)(2,1)}), bf16[8,16,32,128]{3,2,1,0:T(8,128)(2,1)S(1)}, u32[]{:S(2)}, u32[]{:S(2)}) async-start(bf16[8,16,32,128]{3,2,1,0:T(8,128)(2,1)} %shard_map.68), calls=%async_computation.1 | async-start | bytes 2097152 | tf_op jit(solution)/shard_map/all_to_all | solution.py:310
  10.4 2.6 %shard_map.64 = (bf16[8,8,32,128]{3,2,1,0:T(8,128)(2,1)}, bf16[8,4,32,128]{3,2,1,0:T(8,128)(2,1)}, bf16[8,4,32,128]{3,2,1,0:T(8,128)(2,1)}) custom-call(bf16[4,4,8,9216]{3,2,1,0:T(8,128)(2,1)} %refs_1_.3, bf16[4,4,8,9216]{3,2,1,0:T(8,128)(2,1)} %refs_1_.3, f32[1,128]{1,0:T(1,128)} %bitcast.3, f32[1,128]{1,0:T(1,128)} %bitcast.6), custom_call_target="tpu_custom_call" | custom-call | flops 1048576 | bytes 1048576 | tf_op jit(solution)/shard_map/pallas_call | solution.py:76
  13.0 10.6 %collective-permute-start = (bf16[8,4,32,128]{3,2,1,0:T(8,128)(2,1)}, bf16[8,4,32,128]{3,2,1,0:T(8,128)(2,1)S(1)}, u32[]{:S(2)}, u32[]{:S(2)}) collective-permute-start(bf16[8,4,32,128]{3,2,1,0:T(8,128)(2,1)} %get-tuple-element.17), channel_id=1, source_target_pairs={{0,64},{64,128},{128,192},{192,256},{256,320},{320,384},{384,448},... | collective-permute-start | bytes 786440 | tf_op jit(solution)/shard_map/ppermute | solution.py:306
  24.9 2.5 %shard_map.65.q_ref = bf16[8,12,32,128]{3,2,1,0:T(8,128)(2,1)} custom-call(bf16[4,4,8,9216]{3,2,1,0:T(8,128)(2,1)} %refs_1_.3, f32[1,128]{1,0:T(1,128)} %bitcast.4, f32[1,128]{1,0:T(1,128)} %bitcast.7), custom_call_target="tpu_custom_call" | custom-call | flops 1572864 | bytes 1572864 | tf_op jit(solution)/shard_map/pallas_call | solution.py:76
  27.4 1.3 collective-permute-done.t0_ref
  28.8 13.0 %collective-permute-done.1.t1_ref = bf16[8,4,32,128]{3,2,1,0:T(8,128)(2,1)S(1)} collective-permute-done((bf16[8,4,32,128]{3,2,1,0:T(8,128)(2,1)}, bf16[8,4,32,128]{3,2,1,0:T(8,128)(2,1)S(1)}, u32[]{:S(2)}, u32[]{:S(2)}) %collective-permute-start.1) | collective-permute-done | bytes 262176 | tf_op jit(solution)/shard_map/ppermute | solution.py:306
  42.5 2.8 %shard_map.66 = bf16[8,28,32,128]{3,2,1,0:T(8,128)(2,1)} custom-call(bf16[8,8,32,128]{3,2,1,0:T(8,128)(2,1)} %get-tuple-element.16.c_ref, bf16[8,4,32,128]{3,2,1,0:T(8,128)(2,1)} %copy-done.5, bf16[8,4,32,128]{3,2,1,0:T(8,128)(2,1)} %copy-done.6, bf16[8,12,32,128]{3,2,1,0:T(8,128)(2,1)} %shard_map.65.q_ref), custom_call_target="tpu_custom_call" | custom-call | flops 3670016 | bytes 3670016 | tf_op jit(solution)/shard_map/pallas_call | solution.py:98
  46.2 6.4 %all-to-all-start = ((bf16[8,28,32,128]{3,2,1,0:T(8,128)(2,1)}), bf16[8,28,32,128]{3,2,1,0:T(8,128)(2,1)S(1)}, u32[]{:S(2)}, u32[]{:S(2)}) async-start(bf16[8,28,32,128]{3,2,1,0:T(8,128)(2,1)} %shard_map.66), calls=%async_computation | async-start | bytes 3670016 | tf_op jit(solution)/shard_map/all_to_all | solution.py:310
  52.6 2.3 %shard_map.69 = (bf16[8,8,32,128]{3,2,1,0:T(8,128)(2,1)}, bf16[8,8,32,128]{3,2,1,0:T(8,128)(2,1)}) custom-call(bf16[8,16,32,128]{3,2,1,0:T(8,128)(2,1)} %copy-done.2), custom_call_target="tpu_custom_call" | custom-call | flops 2097152 | bytes 2097152 | tf_op jit(solution)/shard_map/pallas_call | solution.py:116
  54.9 5.5 %collective-permute-start.4 = (bf16[8,8,32,128]{3,2,1,0:T(8,128)(2,1)}, bf16[8,8,32,128]{3,2,1,0:T(8,128)(2,1)}, u32[]{:S(2)}, u32[]{:S(2)}) collective-permute-start(bf16[8,8,32,128]{3,2,1,0:T(8,128)(2,1)} %get-tuple-element.21), channel_id=1, source_target_pairs={{0,64},{64,128},{128,192},{192,256},{256,320},{320,384},{384,448},... | collective-permute-start | bytes 1572872 | tf_op jit(solution)/shard_map/ppermute | solution.py:306
  60.4 1.4 collective-permute-start.5
  61.8 2.3 %shard_map.70 = (bf16[8,16,16,128]{3,2,1,0:T(8,128)(2,1)}, bf16[8,16,16,128]{3,2,1,0:T(8,128)(2,1)}) custom-call(bf16[8,16,32,128]{3,2,1,0:T(8,128)(2,1)} %copy-done.2), custom_call_target="tpu_custom_call" | custom-call | flops 2097152 | bytes 2097152 | tf_op jit(solution)/shard_map/pallas_call | solution.py:142
  64.1 13.5 %collective-permute-start.6 = (bf16[8,16,16,128]{3,2,1,0:T(8,128)(2,1)}, bf16[8,16,16,128]{3,2,1,0:T(8,128)(2,1)}, u32[]{:S(2)}, u32[]{:S(2)}) collective-permute-start(bf16[8,16,16,128]{3,2,1,0:T(8,128)(2,1)} %get-tuple-element.23), channel_id=1, source_target_pairs={{0,8},{8,16},{16,24},{24,32},{32,40},{40,48},{48,56},{1,9},{9,17},... | collective-permute-start | bytes 1572872 | tf_op jit(solution)/shard_map/ppermute | solution.py:306
  77.6 1.9 %collective-permute-start.7 = (bf16[8,16,16,128]{3,2,1,0:T(8,128)(2,1)}, bf16[8,16,16,128]{3,2,1,0:T(8,128)(2,1)}, u32[]{:S(2)}, u32[]{:S(2)}) collective-permute-start(bf16[8,16,16,128]{3,2,1,0:T(8,128)(2,1)} %get-tuple-element.24), channel_id=1, source_target_pairs={{8,0},{16,8},{24,16},{32,24},{40,32},{48,40},{56,48},{9,1},{17,9},... | collective-permute-start | bytes 1572872 | tf_op jit(solution)/shard_map/ppermute | solution.py:306
  79.7 2.3 %shard_map.71 = (bf16[8,16,16,128]{3,2,1,0:T(8,128)(2,1)}, bf16[8,16,16,128]{3,2,1,0:T(8,128)(2,1)}) custom-call(bf16[8,8,32,128]{3,2,1,0:T(8,128)(2,1)} %collective-permute-done.4.refs_0_.refs_1_, bf16[8,8,32,128]{3,2,1,0:T(8,128)(2,1)} %collective-permute-done.5.refs_1_.refs_2_), custom_call_target="tpu_custom_call" | custom-call | flops 2097152 | bytes 2097152 | tf_op jit(solution)/shard_map/pallas_call | solution.py:142
  82.1 35.8 %collective-permute-start.8 = (bf16[8,16,16,128]{3,2,1,0:T(8,128)(2,1)}, bf16[8,16,16,128]{3,2,1,0:T(8,128)(2,1)}, u32[]{:S(2)}, u32[]{:S(2)}) collective-permute-start(bf16[8,16,16,128]{3,2,1,0:T(8,128)(2,1)} %get-tuple-element.25), channel_id=1, source_target_pairs={{0,8},{8,16},{16,24},{24,32},{32,40},{40,48},{48,56},{1,9},{9,17},... | collective-permute-start | bytes 1572872 | tf_op jit(solution)/shard_map/ppermute | solution.py:306
  117.9 1.9 %collective-permute-start.9 = (bf16[8,16,16,128]{3,2,1,0:T(8,128)(2,1)}, bf16[8,16,16,128]{3,2,1,0:T(8,128)(2,1)}, u32[]{:S(2)}, u32[]{:S(2)}) collective-permute-start(bf16[8,16,16,128]{3,2,1,0:T(8,128)(2,1)} %get-tuple-element.26), channel_id=1, source_target_pairs={{8,0},{16,8},{24,16},{32,24},{40,32},{48,40},{56,48},{9,1},{17,9},... | collective-permute-start | bytes 1572872 | tf_op jit(solution)/shard_map/ppermute | solution.py:306
  121.1 2.2 %shard_map.67 = (bf16[8,16,16,128]{3,2,1,0:T(8,128)(2,1)}, bf16[8,16,16,128]{3,2,1,0:T(8,128)(2,1)}) custom-call(bf16[8,28,32,128]{3,2,1,0:T(8,128)(2,1)} %copy-done.1), custom_call_target="tpu_custom_call" | custom-call | flops 2097152 | bytes 2097152 | tf_op jit(solution)/shard_map/pallas_call | solution.py:142
  123.4 3.6 %collective-permute-start.2 = (bf16[8,16,16,128]{3,2,1,0:T(8,128)(2,1)}, bf16[8,16,16,128]{3,2,1,0:T(8,128)(2,1)S(1)}, u32[]{:S(2)}, u32[]{:S(2)}) collective-permute-start(bf16[8,16,16,128]{3,2,1,0:T(8,128)(2,1)} %get-tuple-element.19), channel_id=1, source_target_pairs={{0,8},{8,16},{16,24},{24,32},{32,40},{40,48},{48,56},{1,9},{9,17},... | collective-permute-start | bytes 1572872 | tf_op jit(solution)/shard_map/ppermute | solution.py:306
  127.0 1.9 %collective-permute-start.3 = (bf16[8,16,16,128]{3,2,1,0:T(8,128)(2,1)}, bf16[8,16,16,128]{3,2,1,0:T(8,128)(2,1)S(1)}, u32[]{:S(2)}, u32[]{:S(2)}) collective-permute-start(bf16[8,16,16,128]{3,2,1,0:T(8,128)(2,1)} %get-tuple-element.20), channel_id=1, source_target_pairs={{8,0},{16,8},{24,16},{32,24},{40,32},{48,40},{56,48},{9,1},{17,9},... | collective-permute-start | bytes 1572872 | tf_op jit(solution)/shard_map/ppermute | solution.py:306
  129.8 11.7 %attend.2.refs_4_ = bf16[8,2,4,32,128]{4,3,2,1,0:T(8,128)(2,1)S(1)} custom-call(s32[17]{0:T(128)} %pad_add_fusion.info_ref, bf16[8,16,32,128]{3,2,1,0:T(8,128)(2,1)} %copy-done.2, bf16[8,8,32,128]{3,2,1,0:T(8,128)(2,1)} %collective-permute-done.4.refs_0_.refs_1_, bf16[8,8,32,128]{3,2,1,0:T(8,128)(2,1)} %collective-permute-done.5.refs_1_.refs_2_, ...), custom_call_target="tpu_custom_call" | custom-call | flops 1509949440 | bytes 8388608 | tf_op jit(solution)/shard_map/attend/pallas_call | solution.py:255
  143.9 6.8 %attend.3 = bf16[8,3,4,32,128]{4,3,2,1,0:T(8,128)(2,1)S(1)} custom-call(s32[17]{0:T(128)} %pad_add_fusion.info_ref, bf16[8,28,32,128]{3,2,1,0:T(8,128)(2,1)} %copy-done.1, bf16[8,16,16,128]{3,2,1,0:T(8,128)(2,1)} %copy-done.3, bf16[8,16,16,128]{3,2,1,0:T(8,128)(2,1)} %copy-done.4, bf16[8,28,32,128]{3,2,1,0:T(8,128)(2,1)} %copy-done.1, ...), custom_call_target="tpu_custom_call" | custom-call | flops 754974720 | bytes 4194304 | tf_op jit(solution)/shard_map/attend/pallas_call | solution.py:255
  150.7 28.7 %all_to_all.15.in_ref = bf16[8,3,4,32,128]{4,3,2,1,0:T(8,128)(2,1)S(1)} all-to-all(bf16[8,3,4,32,128]{4,3,2,1,0:T(8,128)(2,1)S(1)} %attend.3), channel_id=1, replica_groups=mesh['ta'=8,'ha'=8,'hd'=8] {'hd'}, dimensions={0} | all-to-all | bytes 1572864 | tf_op jit(solution)/shard_map/all_to_all | solution.py:310
  (35 shorter events, 8.7 us)
Async XLA Ops:
  2.7 42.5 %all-to-all-start.1 = ((bf16[8,16,32,128]{3,2,1,0:T(8,128)(2,1)}), bf16[8,16,32,128]{3,2,1,0:T(8,128)(2,1)S(1)}, u32[]{:S(2)}, u32[]{:S(2)}) async-start(bf16[8,16,32,128]{3,2,1,0:T(8,128)(2,1)} %shard_map.68), calls=%async_computation.1 | async-start | bytes 2097152 | tf_op jit(solution)/shard_map/all_to_all | solution.py:310
  13.0 15.8 %collective-permute-start = (bf16[8,4,32,128]{3,2,1,0:T(8,128)(2,1)}, bf16[8,4,32,128]{3,2,1,0:T(8,128)(2,1)S(1)}, u32[]{:S(2)}, u32[]{:S(2)}) collective-permute-start(bf16[8,4,32,128]{3,2,1,0:T(8,128)(2,1)} %get-tuple-element.17), channel_id=1, source_target_pairs={{0,64},{64,128},{128,192},{192,256},{256,320},{320,384},{384,448},... | collective-permute-start | bytes 786440 | tf_op jit(solution)/shard_map/ppermute | solution.py:306
  23.6 18.1 %collective-permute-start.1 = (bf16[8,4,32,128]{3,2,1,0:T(8,128)(2,1)}, bf16[8,4,32,128]{3,2,1,0:T(8,128)(2,1)S(1)}, u32[]{:S(2)}, u32[]{:S(2)}) collective-permute-start(bf16[8,4,32,128]{3,2,1,0:T(8,128)(2,1)} %get-tuple-element.18), channel_id=1, source_target_pairs={{64,0},{128,64},{192,128},{256,192},{320,256},{384,320},{448,384},... | collective-permute-start | bytes 786440 | tf_op jit(solution)/shard_map/ppermute | solution.py:306
  28.8 13.0 %copy-start.5 = (bf16[8,4,32,128]{3,2,1,0:T(8,128)(2,1)}, bf16[8,4,32,128]{3,2,1,0:T(8,128)(2,1)S(1)}, u32[]{:S(2)}) copy-start(bf16[8,4,32,128]{3,2,1,0:T(8,128)(2,1)S(1)} %collective-permute-done.t0_ref) | copy-start | bytes 786436
  41.8 0.7 copy-start.6
  45.3 1.0 copy-start.2
  46.2 73.6 %all-to-all-start = ((bf16[8,28,32,128]{3,2,1,0:T(8,128)(2,1)}), bf16[8,28,32,128]{3,2,1,0:T(8,128)(2,1)S(1)}, u32[]{:S(2)}, u32[]{:S(2)}) async-start(bf16[8,28,32,128]{3,2,1,0:T(8,128)(2,1)} %shard_map.66), calls=%async_computation | async-start | bytes 3670016 | tf_op jit(solution)/shard_map/all_to_all | solution.py:310
  54.9 24.6 %collective-permute-start.4 = (bf16[8,8,32,128]{3,2,1,0:T(8,128)(2,1)}, bf16[8,8,32,128]{3,2,1,0:T(8,128)(2,1)}, u32[]{:S(2)}, u32[]{:S(2)}) collective-permute-start(bf16[8,8,32,128]{3,2,1,0:T(8,128)(2,1)} %get-tuple-element.21), channel_id=1, source_target_pairs={{0,64},{64,128},{128,192},{192,256},{256,320},{320,384},{384,448},... | collective-permute-start | bytes 1572872 | tf_op jit(solution)/shard_map/ppermute | solution.py:306
  60.4 68.6 %copy-start.7 = (s32[3,3]{1,0:T(4,128)S(1)}, s32[3,3]{1,0:T(4,128)}, u32[]{:S(2)}) copy-start(s32[3,3]{1,0:T(4,128)} %param.9) | copy-start | bytes 112
  60.4 68.6 %copy-start.8 = (s32[16]{0:T(128)S(1)}, s32[16]{0:T(128)}, u32[]{:S(2)}) copy-start(s32[16]{0:T(128)} %param.11) | copy-start | bytes 196
  60.4 68.6 %copy-start.9 = (s32[16]{0:T(128)S(1)}, s32[16]{0:T(128)}, u32[]{:S(2)}) copy-start(s32[16]{0:T(128)} %param.10) | copy-start | bytes 196
  60.4 19.3 %collective-permute-start.5 = (bf16[8,8,32,128]{3,2,1,0:T(8,128)(2,1)}, bf16[8,8,32,128]{3,2,1,0:T(8,128)(2,1)}, u32[]{:S(2)}, u32[]{:S(2)}) collective-permute-start(bf16[8,8,32,128]{3,2,1,0:T(8,128)(2,1)} %get-tuple-element.22), channel_id=1, source_target_pairs={{64,0},{128,64},{192,128},{256,192},{320,256},{384,320},{448,384},... | collective-permute-start | bytes 1572872 | tf_op jit(solution)/shard_map/ppermute | solution.py:306
  64.1 62.9 %collective-permute-start.6 = (bf16[8,16,16,128]{3,2,1,0:T(8,128)(2,1)}, bf16[8,16,16,128]{3,2,1,0:T(8,128)(2,1)}, u32[]{:S(2)}, u32[]{:S(2)}) collective-permute-start(bf16[8,16,16,128]{3,2,1,0:T(8,128)(2,1)} %get-tuple-element.23), channel_id=1, source_target_pairs={{0,8},{8,16},{16,24},{24,32},{32,40},{40,48},{48,56},{1,9},{9,17},... | collective-permute-start | bytes 1572872 | tf_op jit(solution)/shard_map/ppermute | solution.py:306
  77.6 52.2 %collective-permute-start.7 = (bf16[8,16,16,128]{3,2,1,0:T(8,128)(2,1)}, bf16[8,16,16,128]{3,2,1,0:T(8,128)(2,1)}, u32[]{:S(2)}, u32[]{:S(2)}) collective-permute-start(bf16[8,16,16,128]{3,2,1,0:T(8,128)(2,1)} %get-tuple-element.24), channel_id=1, source_target_pairs={{8,0},{16,8},{24,16},{32,24},{40,32},{48,40},{56,48},{9,1},{17,9},... | collective-permute-start | bytes 1572872 | tf_op jit(solution)/shard_map/ppermute | solution.py:306
  82.1 47.7 %collective-permute-start.8 = (bf16[8,16,16,128]{3,2,1,0:T(8,128)(2,1)}, bf16[8,16,16,128]{3,2,1,0:T(8,128)(2,1)}, u32[]{:S(2)}, u32[]{:S(2)}) collective-permute-start(bf16[8,16,16,128]{3,2,1,0:T(8,128)(2,1)} %get-tuple-element.25), channel_id=1, source_target_pairs={{0,8},{8,16},{16,24},{24,32},{32,40},{40,48},{48,56},{1,9},{9,17},... | collective-permute-start | bytes 1572872 | tf_op jit(solution)/shard_map/ppermute | solution.py:306
  117.9 11.9 %collective-permute-start.9 = (bf16[8,16,16,128]{3,2,1,0:T(8,128)(2,1)}, bf16[8,16,16,128]{3,2,1,0:T(8,128)(2,1)}, u32[]{:S(2)}, u32[]{:S(2)}) collective-permute-start(bf16[8,16,16,128]{3,2,1,0:T(8,128)(2,1)} %get-tuple-element.26), channel_id=1, source_target_pairs={{8,0},{16,8},{24,16},{32,24},{40,32},{48,40},{56,48},{9,1},{17,9},... | collective-permute-start | bytes 1572872 | tf_op jit(solution)/shard_map/ppermute | solution.py:306
  119.9 1.2 copy-start.1
  123.4 18.9 %collective-permute-start.2 = (bf16[8,16,16,128]{3,2,1,0:T(8,128)(2,1)}, bf16[8,16,16,128]{3,2,1,0:T(8,128)(2,1)S(1)}, u32[]{:S(2)}, u32[]{:S(2)}) collective-permute-start(bf16[8,16,16,128]{3,2,1,0:T(8,128)(2,1)} %get-tuple-element.19), channel_id=1, source_target_pairs={{0,8},{8,16},{16,24},{24,32},{32,40},{40,48},{48,56},{1,9},{9,17},... | collective-permute-start | bytes 1572872 | tf_op jit(solution)/shard_map/ppermute | solution.py:306
  127.0 15.3 %collective-permute-start.3 = (bf16[8,16,16,128]{3,2,1,0:T(8,128)(2,1)}, bf16[8,16,16,128]{3,2,1,0:T(8,128)(2,1)S(1)}, u32[]{:S(2)}, u32[]{:S(2)}) collective-permute-start(bf16[8,16,16,128]{3,2,1,0:T(8,128)(2,1)} %get-tuple-element.20), channel_id=1, source_target_pairs={{8,0},{16,8},{24,16},{32,24},{40,32},{48,40},{56,48},{9,1},{17,9},... | collective-permute-start | bytes 1572872 | tf_op jit(solution)/shard_map/ppermute | solution.py:306
  141.5 0.8 copy-start
  142.3 0.8 copy-start.3
  143.1 0.8 copy-start.4

commit v3 on v2

--- a/solution.py
+++ b/solution.py
@@ -14,7 +14,8 @@
 TW = 8
 NEG = -1e30
 
-GRANT = 62 << 20
+GRANT = 24 << 20
+PACK_GRANT = 62 << 20
 
 
 def cost(flops, size, transcendentals=0):
@@ -47,7 +48,7 @@
     return pl.BlockSpec(shape, lambda i: (0,) * len(shape))
 
 
-def one_step(kernel, in_specs, outs, size):
+def one_step(kernel, in_specs, outs, size, grant=None):
     shapes = [jax.ShapeDtypeStruct(shape, jnp.bfloat16) for shape in outs]
     return pl.pallas_call(
         kernel,
@@ -56,7 +57,7 @@
         out_specs=[whole(shape) for shape in outs],
         out_shape=shapes,
         cost_estimate=cost(size, size),
-        compiler_params=pltpu.CompilerParams(vmem_limit_bytes=GRANT),
+        compiler_params=pltpu.CompilerParams(vmem_limit_bytes=grant or GRANT),
     )
 
 
@@ -73,33 +74,33 @@
         for part in parts
     ] + [whole((1, head_dim))] * 2
     kernel = functools.partial(pack_kernel, entries, parts, heads_local, tiles)
-    packed = one_step(kernel, in_specs, outs, 4 * math.prod(outs[0]))(
+    packed = one_step(kernel, in_specs, outs, 4 * math.prod(outs[0]), PACK_GRANT)(
         *([qkv] * len(parts)), q_gain.reshape(1, -1), k_gain.reshape(1, -1)
     )
     return packed if tiles else packed[0]
 
 
-def join_kernel(frames, c_ref, t0_ref, t1_ref, q_ref, out_ref):
+def join_kernel(frames, c_ref, t0_ref, t1_ref, out_ref):
     long = frames + 2 * TT
     for kv in range(2):
         at = kv * long
         out_ref[:, at : at + TT] = t0_ref[:, kv * TT : (kv + 1) * TT]
         out_ref[:, at + TT : at + TT + frames] = c_ref[:, kv * frames : (kv + 1) * frames]
         out_ref[:, at + TT + frames : at + long] = t1_ref[:, kv * TT : (kv + 1) * TT]
-    out_ref[:, 2 * long :] = q_ref[...]
-
-
-def join(center, t0, t1, queries):
+
+
+def join(center, t0, t1):
     groups, slabs, own, head_dim = center.shape
     frames = slabs // 2
-    total = 2 * (frames + 2 * TT) + queries.shape[1]
-    arrays = (center, t0, t1, queries)
+    total = 2 * (frames + 2 * TT)
+    arrays = (center, t0, t1)
     out = (groups, total, own, head_dim)
     return one_step(
         functools.partial(join_kernel, frames),
         [whole(a.shape) for a in arrays],
         [out],
         4 * math.prod(out),
+        PACK_GRANT,
     )(*arrays)[0]
 
 
@@ -228,7 +229,7 @@
             out_ref[q_cols, here, q_frames, q_rows, :] = result.reshape(span, TT, edge, head_dim)
 
 
-def attend(info, pieces, queries, q_block, heads, slot, before, frames):
+def attend(info, pieces, queries, heads, slot, before, frames):
     groups, _, own, head_dim = queries.shape
     span = max(groups // 2, 1)
     reach = min(span + 1, groups)
@@ -245,7 +246,7 @@
         for a, spans, _ in pieces
     ]
     in_specs += [
-        pl.BlockSpec((groups, frames, own, head_dim), lambda h: (0, q_block + slot + h, 0, 0)),
+        pl.BlockSpec((groups, frames, own, head_dim), lambda h: (0, slot + h, 0, 0)),
     ]
     args = [info, *(a for a, _, _ in pieces), queries]
     total = slot + heads
@@ -337,8 +338,8 @@
     tz1 = shifted(first_z, "ta", -1)
     value_n = packed([(part, head) for head in range(rest) for part in (1, 2)])
     got_n = exchange(value_n)
-    value_q = packed([(0, head) for head in range(heads)])
-    joined = join(value_z, tz0, tz1, value_q)
+    got_q = exchange(packed([(0, head) for head in range(heads)]))
+    joined = join(value_z, tz0, tz1)
     got_z = exchange(joined)
 
     first_n, last_n = tiles_of(got_n, frames)
@@ -354,7 +355,6 @@
     ht0 = shifted(high_t, "ha", 1)
     ht1 = shifted(low_t, "ha", -1)
 
-    q_block = 2 * long // frames
     mine, every = ((TT, frames),), ((0, long),)
     beside = ((0, TT), (TT + frames, TT))
     pieces_n = (
@@ -367,8 +367,8 @@
         (ht1, beside, edge + own),
     )
     pieces_z = ((got_z, every, edge), (hz0, every, 0), (hz1, every, edge + own))
-    out = attend(info, pieces_n, got_z, q_block, rest, 0, None, frames)
-    out = attend(info, pieces_z, got_z, q_block, 1, rest, out, frames)
+    out = attend(info, pieces_n, got_q, rest, 0, None, frames)
+    out = attend(info, pieces_z, got_q, 1, rest, out, frames)
     return unpack(exchange(out), rows, cols)
 
 

time: 181 us -> 210 us (1.16)
  waiting for transfers between devices: 14.5 us -> 53.5 us
  Pallas kernels: 39.4 us -> 31.8 us
  starting transfers between devices: 91.6 us -> 87.7 us
  local copies, waits for them, and re-layouts: 5.46 us -> 7.86 us
    all_to_all x2 -> x3, waiting for transfers between devices: 0.01 us -> 24.6 us  [exchange(): return lax.all_to_all(value, 'hd', split_axis=0, concat_axis=0, tiled=True)]
    ppermute x10, waiting for transfers between devices: 14.5 us -> 28.9 us  [shifted(): return lax.ppermute(value, axis, pairs)]
    ppermute x10, starting transfers between devices: 77.6 us -> 70.2 us  [shifted(): return lax.ppermute(value, axis, pairs)]
    pallas_call x3, Pallas kernels: 6.85 us -> 3.04 us  [rim(): one_step(functools.partial(rim_kernel, edge, counts), in_specs, [out, out...]
    all_to_all x2 -> x3, starting transfers between devices: 14 us -> 17.6 us  [exchange(): return lax.all_to_all(value, 'hd', split_axis=0, concat_axis=0, tiled=True)]
    unnamed x20 -> x28, local copies, waits for them, and re-layouts: 5.29 us -> 7.69 us
    pallas_call x1, Pallas kernels: 2.29 us -> 0.07 us  [tiles_of(): one_step(functools.partial(tiles_kernel, frames), [whole(value.shape)], [...]
  transfers between devices with their start and end apart: 12 -> 13, of which waited for: 3 -> 5; matrix products, arithmetic and copies ran while one was open for 0% -> 0% of each run, Pallas kernels for 16% -> 10%
where the time goes in v3:
time: 210 us; the launch traced here: 209 us
  starting transfers between devices  87.7 us (42%)
  waiting for transfers between devices  53.5 us (25%)
  Pallas kernels  31.8 us (15%)
  blocking collectives  28.3 us (13%)
  local copies, waits for them, and re-layouts  7.86 us (4%)
    ppermute x10, starting transfers between devices, shifted(): return lax.ppermute(value, axis, pairs)  70.2 us
    ppermute x10, waiting for transfers between devices, shifted(): return lax.ppermute(value, axis, pairs)  28.9 us
    all_to_all x1, blocking collectives, exchange(): return lax.all_to_all(value, 'hd', split_axis=0, concat_axis=0, tiled=True)  28.3 us
    all_to_all x3, waiting for transfers between devices, exchange(): return lax.all_to_all(value, 'hd', split_axis=0, concat_axis=0, tiled=True)  24.6 us
    all_to_all x3, starting transfers between devices, exchange(): return lax.all_to_all(value, 'hd', split_axis=0, concat_axis=0, tiled=True)  17.6 us
    pallas_call x2, Pallas kernels, attend(): pl.pallas_call(functools.partial(attend_kernel, tuple(((spans, low) for _...  17.5 us
    pallas_call x3, Pallas kernels, pack(): one_step(kernel, in_specs, outs, 4 * math.prod(outs[0]), PACK_GRANT)  7.85 us
    unnamed x28, local copies, waits for them, and re-layouts  7.69 us
  transfers between devices with their start and end apart: 13, of which 5 were waited for; matrix products, arithmetic and copies ran while one was open for 0% of the time, Pallas kernels for 10%

profile of v3, /device:TPU:1, one launch (start us, length us, event | category | flops | bytes accessed | tf_op | source)
XLA Modules:
  0.0 209.4 jit_solution(17477597881320182652)
XLA Ops:
  0.0 2.8 %shard_map.68 = bf16[8,16,32,128]{3,2,1,0:T(8,128)(2,1)} custom-call(bf16[4,4,8,9216]{3,2,1,0:T(8,128)(2,1)} %refs_1_.3, bf16[4,4,8,9216]{3,2,1,0:T(8,128)(2,1)} %refs_1_.3, f32[1,128]{1,0:T(1,128)} %bitcast.2, f32[1,128]{1,0:T(1,128)} %bitcast.5), custom_call_target="tpu_custom_call" | custom-call | flops 2097152 | bytes 2097152 | tf_op jit(solution)/shard_map/pallas_call | solution.py:77
  2.8 7.6 %all-to-all-start.2 = ((bf16[8,16,32,128]{3,2,1,0:T(8,128)(2,1)}), bf16[8,16,32,128]{3,2,1,0:T(8,128)(2,1)S(1)}, u32[]{:S(2)}, u32[]{:S(2)}) async-start(bf16[8,16,32,128]{3,2,1,0:T(8,128)(2,1)} %shard_map.68), calls=%async_computation.2 | async-start | bytes 2097152 | tf_op jit(solution)/shard_map/all_to_all | solution.py:311
  10.4 2.6 %shard_map.64 = (bf16[8,8,32,128]{3,2,1,0:T(8,128)(2,1)}, bf16[8,4,32,128]{3,2,1,0:T(8,128)(2,1)}, bf16[8,4,32,128]{3,2,1,0:T(8,128)(2,1)}) custom-call(bf16[4,4,8,9216]{3,2,1,0:T(8,128)(2,1)} %refs_1_.3, bf16[4,4,8,9216]{3,2,1,0:T(8,128)(2,1)} %refs_1_.3, f32[1,128]{1,0:T(1,128)} %bitcast.3, f32[1,128]{1,0:T(1,128)} %bitcast.6), custom_call_target="tpu_custom_call" | custom-call | flops 1048576 | bytes 1048576 | tf_op jit(solution)/shard_map/pallas_call | solution.py:77
  13.0 10.6 %collective-permute-start = (bf16[8,4,32,128]{3,2,1,0:T(8,128)(2,1)}, bf16[8,4,32,128]{3,2,1,0:T(8,128)(2,1)S(1)}, u32[]{:S(2)}, u32[]{:S(2)}) collective-permute-start(bf16[8,4,32,128]{3,2,1,0:T(8,128)(2,1)} %get-tuple-element.17), channel_id=1, source_target_pairs={{0,64},{64,128},{128,192},{192,256},{256,320},{320,384},{384,448},... | collective-permute-start | bytes 786440 | tf_op jit(solution)/shard_map/ppermute | solution.py:307
  23.6 1.3 collective-permute-start.1
  24.9 3.8 %collective-permute-done.t0_ref = bf16[8,4,32,128]{3,2,1,0:T(8,128)(2,1)S(1)} collective-permute-done((bf16[8,4,32,128]{3,2,1,0:T(8,128)(2,1)}, bf16[8,4,32,128]{3,2,1,0:T(8,128)(2,1)S(1)}, u32[]{:S(2)}, u32[]{:S(2)}) %collective-permute-start) | collective-permute-done | bytes 262176 | tf_op jit(solution)/shard_map/ppermute | solution.py:307
  28.8 13.0 %collective-permute-done.1.t1_ref = bf16[8,4,32,128]{3,2,1,0:T(8,128)(2,1)S(1)} collective-permute-done((bf16[8,4,32,128]{3,2,1,0:T(8,128)(2,1)}, bf16[8,4,32,128]{3,2,1,0:T(8,128)(2,1)S(1)}, u32[]{:S(2)}, u32[]{:S(2)}) %collective-permute-start.1) | collective-permute-done | bytes 262176 | tf_op jit(solution)/shard_map/ppermute | solution.py:307
  42.5 2.2 %shard_map.65 = bf16[8,16,32,128]{3,2,1,0:T(8,128)(2,1)} custom-call(bf16[8,8,32,128]{3,2,1,0:T(8,128)(2,1)} %get-tuple-element.16.c_ref, bf16[8,4,32,128]{3,2,1,0:T(8,128)(2,1)} %copy-done.9, bf16[8,4,32,128]{3,2,1,0:T(8,128)(2,1)} %copy-done.10), custom_call_target="tpu_custom_call" | custom-call | flops 2097152 | bytes 2097152 | tf_op jit(solution)/shard_map/pallas_call | solution.py:98
  45.7 6.4 %all-to-all-start = ((bf16[8,16,32,128]{3,2,1,0:T(8,128)(2,1)}), bf16[8,16,32,128]{3,2,1,0:T(8,128)(2,1)S(1)}, u32[]{:S(2)}, u32[]{:S(2)}) async-start(bf16[8,16,32,128]{3,2,1,0:T(8,128)(2,1)} %shard_map.65), calls=%async_computation | async-start | bytes 2097152 | tf_op jit(solution)/shard_map/all_to_all | solution.py:311
  52.1 2.5 %shard_map.67 = bf16[8,12,32,128]{3,2,1,0:T(8,128)(2,1)} custom-call(bf16[4,4,8,9216]{3,2,1,0:T(8,128)(2,1)} %refs_1_.3, f32[1,128]{1,0:T(1,128)} %bitcast.4, f32[1,128]{1,0:T(1,128)} %bitcast.7), custom_call_target="tpu_custom_call" | custom-call | flops 1572864 | bytes 1572864 | tf_op jit(solution)/shard_map/pallas_call | solution.py:77
  54.6 24.6 %all-to-all-done.refs_0_ = bf16[8,16,32,128]{3,2,1,0:T(8,128)(2,1)S(1)} async-done(((bf16[8,16,32,128]{3,2,1,0:T(8,128)(2,1)}), bf16[8,16,32,128]{3,2,1,0:T(8,128)(2,1)S(1)}, u32[]{:S(2)}, u32[]{:S(2)}) %all-to-all-start) | async-done | bytes 1048608 | tf_op jit(solution)/shard_map/all_to_all | solution.py:311
  79.2 3.5 %all-to-all-start.1 = ((bf16[8,12,32,128]{3,2,1,0:T(8,128)(2,1)}), bf16[8,12,32,128]{3,2,1,0:T(8,128)(2,1)S(1)}, u32[]{:S(2)}, u32[]{:S(2)}) async-start(bf16[8,12,32,128]{3,2,1,0:T(8,128)(2,1)} %shard_map.67), calls=%async_computation.1 | async-start | bytes 1572864 | tf_op jit(solution)/shard_map/all_to_all | solution.py:311
  84.1 1.5 collective-permute-start.4
  85.6 1.3 collective-permute-start.5
  87.7 17.0 %collective-permute-start.6 = (bf16[8,16,16,128]{3,2,1,0:T(8,128)(2,1)S(1)}, bf16[8,16,16,128]{3,2,1,0:T(8,128)(2,1)S(1)}, u32[]{:S(2)}, u32[]{:S(2)}) collective-permute-start(bf16[8,16,16,128]{3,2,1,0:T(8,128)(2,1)S(1)} %get-tuple-element.23), channel_id=1, source_target_pairs={{0,8},{8,16},{16,24},{24,32},{32,40},{40,48},{48,56},{1,9},{9,17},... | collective-permute-start | bytes 1572872 | tf_op jit(solution)/shard_map/ppermute | solution.py:307
  104.7 1.9 collective-permute-start.7
  106.7 10.9 %collective-permute-done.5.refs_1_.refs_2_ = bf16[8,8,32,128]{3,2,1,0:T(8,128)(2,1)S(1)} collective-permute-done((bf16[8,8,32,128]{3,2,1,0:T(8,128)(2,1)S(1)}, bf16[8,8,32,128]{3,2,1,0:T(8,128)(2,1)S(1)}, u32[]{:S(2)}, u32[]{:S(2)}) %collective-permute-start.5) | collective-permute-done | bytes 524320 | tf_op jit(solution)/shard_map/ppermute | solution.py:307
  119.5 29.1 %collective-permute-start.8 = (bf16[8,16,16,128]{3,2,1,0:T(8,128)(2,1)}, bf16[8,16,16,128]{3,2,1,0:T(8,128)(2,1)}, u32[]{:S(2)}, u32[]{:S(2)}) collective-permute-start(bf16[8,16,16,128]{3,2,1,0:T(8,128)(2,1)} %get-tuple-element.25), channel_id=1, source_target_pairs={{0,8},{8,16},{16,24},{24,32},{32,40},{40,48},{48,56},{1,9},{9,17},... | collective-permute-start | bytes 1572872 | tf_op jit(solution)/shard_map/ppermute | solution.py:307
  148.6 1.9 collective-permute-start.9
  151.6 3.6 %collective-permute-start.2 = (bf16[8,16,16,128]{3,2,1,0:T(8,128)(2,1)}, bf16[8,16,16,128]{3,2,1,0:T(8,128)(2,1)}, u32[]{:S(2)}, u32[]{:S(2)}) collective-permute-start(bf16[8,16,16,128]{3,2,1,0:T(8,128)(2,1)} %get-tuple-element.19), channel_id=1, source_target_pairs={{0,8},{8,16},{16,24},{24,32},{32,40},{40,48},{48,56},{1,9},{9,17},... | collective-permute-start | bytes 1572872 | tf_op jit(solution)/shard_map/ppermute | solution.py:307
  156.0 1.9 collective-permute-start.3
  162.5 11.2 %attend.2.refs_4_ = bf16[8,2,4,32,128]{4,3,2,1,0:T(8,128)(2,1)S(1)} custom-call(s32[17]{0:T(128)S(1)} %pad_add_fusion.info_ref, bf16[8,16,32,128]{3,2,1,0:T(8,128)(2,1)S(1)} %copy-done.2, bf16[8,8,32,128]{3,2,1,0:T(8,128)(2,1)S(1)} %copy-done.4, bf16[8,8,32,128]{3,2,1,0:T(8,128)(2,1)S(1)} %copy-done.6, bf16[8,16,16,128]{3,2,1,0:T(8,128)(2,1)S(1)} %copy-done.8, ...), custom_call_target="tpu_custom_call" | custom-call | flops 1509949440 | bytes 8388608 | tf_op jit(solution)/shard_map/attend/pallas_call | solution.py:256
  173.8 6.3 %attend.3 = bf16[8,3,4,32,128]{4,3,2,1,0:T(8,128)(2,1)S(1)} custom-call(s32[17]{0:T(128)S(1)} %pad_add_fusion.info_ref, bf16[8,16,32,128]{3,2,1,0:T(8,128)(2,1)S(1)} %all-to-all-done.refs_0_, bf16[8,16,16,128]{3,2,1,0:T(8,128)(2,1)} %collective-permute-done.2.refs_1_, bf16[8,16,16,128]{3,2,1,0:T(8,128)(2,1)} %collective-permute-done.3.refs_2_, ...), custom_call_target="tpu_custom_call" | custom-call | flops 754974720 | bytes 4194304 | tf_op jit(solution)/shard_map/attend/pallas_call | solution.py:256
  180.1 28.3 %all_to_all.20.in_ref = bf16[8,3,4,32,128]{4,3,2,1,0:T(8,128)(2,1)S(1)} all-to-all(bf16[8,3,4,32,128]{4,3,2,1,0:T(8,128)(2,1)S(1)} %attend.3), channel_id=1, replica_groups=mesh['ta'=8,'ha'=8,'hd'=8] {'hd'}, dimensions={0} | all-to-all | bytes 1572864 | tf_op jit(solution)/shard_map/all_to_all | solution.py:311
  (45 shorter events, 13.3 us)
Async XLA Ops:
  2.8 42.0 %all-to-all-start.2 = ((bf16[8,16,32,128]{3,2,1,0:T(8,128)(2,1)}), bf16[8,16,32,128]{3,2,1,0:T(8,128)(2,1)S(1)}, u32[]{:S(2)}, u32[]{:S(2)}) async-start(bf16[8,16,32,128]{3,2,1,0:T(8,128)(2,1)} %shard_map.68), calls=%async_computation.2 | async-start | bytes 2097152 | tf_op jit(solution)/shard_map/all_to_all | solution.py:311
  13.0 15.8 %collective-permute-start = (bf16[8,4,32,128]{3,2,1,0:T(8,128)(2,1)}, bf16[8,4,32,128]{3,2,1,0:T(8,128)(2,1)S(1)}, u32[]{:S(2)}, u32[]{:S(2)}) collective-permute-start(bf16[8,4,32,128]{3,2,1,0:T(8,128)(2,1)} %get-tuple-element.17), channel_id=1, source_target_pairs={{0,64},{64,128},{128,192},{192,256},{256,320},{320,384},{384,448},... | collective-permute-start | bytes 786440 | tf_op jit(solution)/shard_map/ppermute | solution.py:307
  23.6 18.1 %collective-permute-start.1 = (bf16[8,4,32,128]{3,2,1,0:T(8,128)(2,1)}, bf16[8,4,32,128]{3,2,1,0:T(8,128)(2,1)S(1)}, u32[]{:S(2)}, u32[]{:S(2)}) collective-permute-start(bf16[8,4,32,128]{3,2,1,0:T(8,128)(2,1)} %get-tuple-element.18), channel_id=1, source_target_pairs={{64,0},{128,64},{192,128},{256,192},{320,256},{384,320},{448,384},... | collective-permute-start | bytes 786440 | tf_op jit(solution)/shard_map/ppermute | solution.py:307
  28.8 13.0 %copy-start.9 = (bf16[8,4,32,128]{3,2,1,0:T(8,128)(2,1)}, bf16[8,4,32,128]{3,2,1,0:T(8,128)(2,1)S(1)}, u32[]{:S(2)}) copy-start(bf16[8,4,32,128]{3,2,1,0:T(8,128)(2,1)S(1)} %collective-permute-done.t0_ref) | copy-start | bytes 786436
  44.7 1.0 copy-start
  45.7 33.5 %all-to-all-start = ((bf16[8,16,32,128]{3,2,1,0:T(8,128)(2,1)}), bf16[8,16,32,128]{3,2,1,0:T(8,128)(2,1)S(1)}, u32[]{:S(2)}, u32[]{:S(2)}) async-start(bf16[8,16,32,128]{3,2,1,0:T(8,128)(2,1)} %shard_map.65), calls=%async_computation | async-start | bytes 2097152 | tf_op jit(solution)/shard_map/all_to_all | solution.py:311
  79.2 79.0 %all-to-all-start.1 = ((bf16[8,12,32,128]{3,2,1,0:T(8,128)(2,1)}), bf16[8,12,32,128]{3,2,1,0:T(8,128)(2,1)S(1)}, u32[]{:S(2)}, u32[]{:S(2)}) async-start(bf16[8,12,32,128]{3,2,1,0:T(8,128)(2,1)} %shard_map.67), calls=%async_computation.1 | async-start | bytes 1572864 | tf_op jit(solution)/shard_map/all_to_all | solution.py:311
  82.8 1.2 copy-start.1
  84.0 74.0 %copy-start.11 = (s32[3,3]{1,0:T(4,128)S(1)}, s32[3,3]{1,0:T(4,128)}, u32[]{:S(2)}) copy-start(s32[3,3]{1,0:T(4,128)} %param.9) | copy-start | bytes 112
  84.0 74.1 %copy-start.12 = (s32[16]{0:T(128)S(1)}, s32[16]{0:T(128)}, u32[]{:S(2)}) copy-start(s32[16]{0:T(128)} %param.11) | copy-start | bytes 196
  84.0 74.1 %copy-start.13 = (s32[16]{0:T(128)S(1)}, s32[16]{0:T(128)}, u32[]{:S(2)}) copy-start(s32[16]{0:T(128)} %param.10) | copy-start | bytes 196
  84.0 75.4 %copy-start.2 = (bf16[8,16,32,128]{3,2,1,0:T(8,128)(2,1)S(1)}, bf16[8,16,32,128]{3,2,1,0:T(8,128)(2,1)}, u32[]{:S(2)}) copy-start(bf16[8,16,32,128]{3,2,1,0:T(8,128)(2,1)} %copy-done) | copy-start | bytes 3145732
  84.1 22.6 %collective-permute-start.4 = (bf16[8,8,32,128]{3,2,1,0:T(8,128)(2,1)S(1)}, bf16[8,8,32,128]{3,2,1,0:T(8,128)(2,1)S(1)}, u32[]{:S(2)}, u32[]{:S(2)}) collective-permute-start(bf16[8,8,32,128]{3,2,1,0:T(8,128)(2,1)S(1)} %get-tuple-element.21), channel_id=1, source_target_pairs={{0,64},{64,128},{128,192},{192,256},{256,320},{320,384},{384,448},... | collective-permute-start | bytes 1572872 | tf_op jit(solution)/shard_map/ppermute | solution.py:307
  85.6 32.0 %collective-permute-start.5 = (bf16[8,8,32,128]{3,2,1,0:T(8,128)(2,1)S(1)}, bf16[8,8,32,128]{3,2,1,0:T(8,128)(2,1)S(1)}, u32[]{:S(2)}, u32[]{:S(2)}) collective-permute-start(bf16[8,8,32,128]{3,2,1,0:T(8,128)(2,1)S(1)} %get-tuple-element.22), channel_id=1, source_target_pairs={{64,0},{128,64},{192,128},{256,192},{320,256},{384,320},{448,384},... | collective-permute-start | bytes 1572872 | tf_op jit(solution)/shard_map/ppermute | solution.py:307
  87.7 67.5 %collective-permute-start.6 = (bf16[8,16,16,128]{3,2,1,0:T(8,128)(2,1)S(1)}, bf16[8,16,16,128]{3,2,1,0:T(8,128)(2,1)S(1)}, u32[]{:S(2)}, u32[]{:S(2)}) collective-permute-start(bf16[8,16,16,128]{3,2,1,0:T(8,128)(2,1)S(1)} %get-tuple-element.23), channel_id=1, source_target_pairs={{0,8},{8,16},{16,24},{24,32},{32,40},{40,48},{48,56},{1,9},{9,17},... | collective-permute-start | bytes 1572872 | tf_op jit(solution)/shard_map/ppermute | solution.py:307
  104.7 53.5 %collective-permute-start.7 = (bf16[8,16,16,128]{3,2,1,0:T(8,128)(2,1)}, bf16[8,16,16,128]{3,2,1,0:T(8,128)(2,1)}, u32[]{:S(2)}, u32[]{:S(2)}) collective-permute-start(bf16[8,16,16,128]{3,2,1,0:T(8,128)(2,1)} %get-tuple-element.24), channel_id=1, source_target_pairs={{8,0},{16,8},{24,16},{32,24},{40,32},{48,40},{56,48},{9,1},{17,9},... | collective-permute-start | bytes 1572872 | tf_op jit(solution)/shard_map/ppermute | solution.py:307
  117.5 1.1 copy-start.5
  119.5 38.8 %collective-permute-start.8 = (bf16[8,16,16,128]{3,2,1,0:T(8,128)(2,1)}, bf16[8,16,16,128]{3,2,1,0:T(8,128)(2,1)}, u32[]{:S(2)}, u32[]{:S(2)}) collective-permute-start(bf16[8,16,16,128]{3,2,1,0:T(8,128)(2,1)} %get-tuple-element.25), channel_id=1, source_target_pairs={{0,8},{8,16},{16,24},{24,32},{32,40},{40,48},{48,56},{1,9},{9,17},... | collective-permute-start | bytes 1572872 | tf_op jit(solution)/shard_map/ppermute | solution.py:307
  148.6 10.8 %collective-permute-start.9 = (bf16[8,16,16,128]{3,2,1,0:T(8,128)(2,1)}, bf16[8,16,16,128]{3,2,1,0:T(8,128)(2,1)}, u32[]{:S(2)}, u32[]{:S(2)}) collective-permute-start(bf16[8,16,16,128]{3,2,1,0:T(8,128)(2,1)} %get-tuple-element.26), channel_id=1, source_target_pairs={{8,0},{16,8},{24,16},{32,24},{40,32},{48,40},{56,48},{9,1},{17,9},... | collective-permute-start | bytes 1572872 | tf_op jit(solution)/shard_map/ppermute | solution.py:307
  151.6 22.2 %collective-permute-start.2 = (bf16[8,16,16,128]{3,2,1,0:T(8,128)(2,1)}, bf16[8,16,16,128]{3,2,1,0:T(8,128)(2,1)}, u32[]{:S(2)}, u32[]{:S(2)}) collective-permute-start(bf16[8,16,16,128]{3,2,1,0:T(8,128)(2,1)} %get-tuple-element.19), channel_id=1, source_target_pairs={{0,8},{8,16},{16,24},{24,32},{32,40},{40,48},{48,56},{1,9},{9,17},... | collective-permute-start | bytes 1572872 | tf_op jit(solution)/shard_map/ppermute | solution.py:307
  156.0 17.7 %collective-permute-start.3 = (bf16[8,16,16,128]{3,2,1,0:T(8,128)(2,1)}, bf16[8,16,16,128]{3,2,1,0:T(8,128)(2,1)}, u32[]{:S(2)}, u32[]{:S(2)}) collective-permute-start(bf16[8,16,16,128]{3,2,1,0:T(8,128)(2,1)} %get-tuple-element.20), channel_id=1, source_target_pairs={{8,0},{16,8},{24,16},{32,24},{40,32},{48,40},{56,48},{9,1},{17,9},... | collective-permute-start | bytes 1572872 | tf_op jit(solution)/shard_map/ppermute | solution.py:307
  159.4 1.0 copy-start.4
  160.4 1.0 copy-start.6
  161.5 1.0 copy-start.8
  (3 other events, 2.4 us)

commit v4 on v3

--- a/solution.py
+++ b/solution.py
@@ -145,7 +145,7 @@
     )(*arrays)
 
 
-def attend_kernel(pieces, frames, span, reach, scale, slot, info_ref, *refs):
+def attend_kernel(pieces, frames, span, reach, scale, head, slot, info_ref, *refs):
     count = len(pieces)
     piece_refs = refs[:count]
     q_ref = refs[count]
@@ -166,70 +166,78 @@
 
     tiles_t = frames // TT
     tiles_h = own // edge
-    halves = groups // span
-    per_col = 3 * TT * 3 * edge
-    nq = span * TT * edge
-    nk = reach * per_col
-    firsts = [min(max(half * span - 1, 0), groups - reach) for half in range(halves)]
     base_t = info_ref.shape[0] - (tiles_t + 2) - (tiles_h + 2)
     base_h = base_t + tiles_t + 2
-    head = here
+    head = head + pl.program_id(0)
     rad_t = info_ref[3 * head]
     rad_h = info_ref[3 * head + 1]
     rad_w = info_ref[3 * head + 2]
-
-    q_col = lax.broadcasted_iota(jnp.int32, (nq, nk), 0) // (TT * edge)
-    k_col = lax.broadcasted_iota(jnp.int32, (nq, nk), 1) // per_col
-    for half, first in enumerate(firsts):
-        gap = jnp.abs(q_col - k_col + (half * span - first))
-        bias_ref[half] = jnp.where(gap <= rad_w, 0.0, NEG)
-
-    at = lax.broadcasted_iota(jnp.int32, (1, nk), 1) % per_col
-    k_frame = at // (3 * edge)
-    k_row = (at % (3 * edge)) // TW
+    nq = span * TT * edge
     at_q = lax.broadcasted_iota(jnp.int32, (nq, 1), 0) % (TT * edge)
     q_frame = at_q // edge
     q_row = (at_q % edge) // TW
-
-    @pl.loop(0, tiles_t * tiles_h)
-    def _(step):
-        th = step % tiles_h
-        tt = step // tiles_h
-        ok_t = jnp.zeros((1, nk), jnp.bool_)
-        ok_h = jnp.zeros((1, nk), jnp.bool_)
-        for near in range(3):
-            away = abs(near - 1)
-            live_t = jnp.where(away <= rad_t, info_ref[base_t + tt + near], 0)
-            live_h = jnp.where(away <= rad_h, info_ref[base_h + th + near], 0)
-            ok_t = ok_t | ((k_frame // TT == near) & (k_frame % TT < live_t))
-            ok_h = ok_h | ((k_row // TH == near) & (k_row % TH < live_h))
-        key_bias = jnp.where(ok_t & ok_h, 0.0, NEG)
-        live = (q_frame < info_ref[base_t + tt + 1]) & (q_row < info_ref[base_h + th + 1])
-        q_rows = pl.ds(pl.multiple_of(th * edge, edge), edge)
-        k_rows = pl.ds(pl.multiple_of(th * edge, edge), 3 * edge)
-        q_frames = pl.ds(tt * TT, TT)
-        k_frames = pl.ds(tt * TT, 3 * TT)
+    firsts = [min(max(half * span - 1, 0), groups - reach) for half in range(groups // span)]
+
+    def over(far_t, far_h):
+        near_t = 1 + 2 * far_t
+        near_h = 1 + 2 * far_h
+        per_col = near_t * TT * near_h * edge
+        nk = reach * per_col
+        q_col = lax.broadcasted_iota(jnp.int32, (nq, nk), 0) // (TT * edge)
+        k_col = lax.broadcasted_iota(jnp.int32, (nq, nk), 1) // per_col
         for half, first in enumerate(firsts):
-            q_cols = slice(half * span, (half + 1) * span)
-            k_cols = slice(first, first + reach)
-            q = q_ref[q_cols, q_frames, q_rows, :].reshape(nq, head_dim)
-            k = k_ref[k_cols, k_frames, k_rows, :].reshape(nk, head_dim)
-            v = v_ref[k_cols, k_frames, k_rows, :].reshape(nk, head_dim)
-            scores = lax.dot_general(
-                q, k, (((1,), (1,)), ((), ())), preferred_element_type=jnp.float32
-            )
-            scores = scores * scale + (bias_ref[half] + key_bias)
-            top = jnp.max(scores, axis=1, keepdims=True)
-            raised = jnp.exp2(scores - top)
-            summed = jnp.sum(raised, axis=1, keepdims=True)
-            blended = jnp.dot(
-                raised.astype(jnp.bfloat16), v, preferred_element_type=jnp.float32
-            )
-            result = jnp.where(live, blended / summed, 0.0).astype(jnp.bfloat16)
-            out_ref[q_cols, here, q_frames, q_rows, :] = result.reshape(span, TT, edge, head_dim)
-
-
-def attend(info, pieces, queries, heads, slot, before, frames):
+            gap = jnp.abs(q_col - k_col + (half * span - first))
+            bias_ref[half, :, :nk] = jnp.where(gap <= rad_w, 0.0, NEG)
+        at = lax.broadcasted_iota(jnp.int32, (1, nk), 1) % per_col
+        k_frame = at // (near_h * edge)
+        k_row = (at % (near_h * edge)) // TW
+
+        @pl.loop(0, tiles_t * tiles_h)
+        def _(step):
+            th = step % tiles_h
+            tt = step // tiles_h
+            live_t = jnp.zeros((1, nk), jnp.int32)
+            live_h = jnp.zeros((1, nk), jnp.int32)
+            for near in range(near_t):
+                count = info_ref[base_t + tt + 1 - far_t + near]
+                live_t = jnp.where(k_frame // TT == near, count, live_t)
+            for near in range(near_h):
+                count = info_ref[base_h + th + 1 - far_h + near]
+                live_h = jnp.where(k_row // TH == near, count, live_h)
+            key_ok = (k_frame % TT < live_t) & (k_row % TH < live_h)
+            key_bias = jnp.where(key_ok, 0.0, NEG)
+            live = (q_frame < info_ref[base_t + tt + 1]) & (q_row < info_ref[base_h + th + 1])
+            q_rows = pl.ds(pl.multiple_of(th * edge, edge), edge)
+            k_rows = pl.ds(pl.multiple_of((th + 1 - far_h) * edge, edge), near_h * edge)
+            q_frames = pl.ds(tt * TT, TT)
+            k_frames = pl.ds((tt + 1 - far_t) * TT, near_t * TT)
+            for half, first in enumerate(firsts):
+                q_cols = slice(half * span, (half + 1) * span)
+                k_cols = slice(first, first + reach)
+                q = q_ref[q_cols, q_frames, q_rows, :].reshape(nq, head_dim)
+                k = k_ref[k_cols, k_frames, k_rows, :].reshape(nk, head_dim)
+                v = v_ref[k_cols, k_frames, k_rows, :].reshape(nk, head_dim)
+                scores = lax.dot_general(
+                    q, k, (((1,), (1,)), ((), ())), preferred_element_type=jnp.float32
+                )
+                scores = scores * scale + (bias_ref[half, :, :nk] + key_bias)
+                top = jnp.max(scores, axis=1, keepdims=True)
+                raised = jnp.exp2(scores - top)
+                summed = jnp.sum(raised, axis=1, keepdims=True)
+                blended = jnp.dot(
+                    raised.astype(jnp.bfloat16), v, preferred_element_type=jnp.float32
+                )
+                result = jnp.where(live, blended / summed, 0.0).astype(jnp.bfloat16)
+                out_ref[q_cols, here, q_frames, q_rows, :] = result.reshape(
+                    span, TT, edge, head_dim
+                )
+
+    for far_t in (0, 1):
+        for far_h in (0, 1):
+            pl.when((rad_t == far_t) & (rad_h == far_h))(functools.partial(over, far_t, far_h))
+
+
+def attend(info, pieces, queries, heads, head, slot, before, frames):
     groups, _, own, head_dim = queries.shape
     span = max(groups // 2, 1)
     reach = min(span + 1, groups)
@@ -246,7 +254,7 @@
         for a, spans, _ in pieces
     ]
     in_specs += [
-        pl.BlockSpec((groups, frames, own, head_dim), lambda h: (0, slot + h, 0, 0)),
+        pl.BlockSpec((groups, frames, own, head_dim), lambda h: (0, head + h, 0, 0)),
     ]
     args = [info, *(a for a, _, _ in pieces), queries]
     total = slot + heads
@@ -261,6 +269,7 @@
             span,
             reach,
             math.log2(math.e) / math.sqrt(head_dim),
+            head,
             slot,
         ),
         grid=(heads,),
@@ -278,21 +287,21 @@
     )(*args)
 
 
-def unpack_kernel(in_ref, out_ref):
+def unpack_kernel(order, in_ref, out_ref):
     frames, rows, cols = out_ref.shape[:3]
     groups, heads, _, _, head_dim = in_ref.shape
-    for head in range(heads):
+    for slot, head in enumerate(order):
         for group in range(groups):
             at = (heads * group + head) * head_dim
-            x = in_ref[group, head].astype(jnp.float32).reshape(frames, rows, cols, head_dim)
+            x = in_ref[group, slot].astype(jnp.float32).reshape(frames, rows, cols, head_dim)
             out_ref[:, :, :, at : at + head_dim] = x.astype(jnp.bfloat16)
 
 
-def unpack(value, rows, cols):
+def unpack(value, order, rows, cols):
     groups, heads, frames, _, head_dim = value.shape
     out = (frames, rows, cols, groups * heads * head_dim)
     return pl.pallas_call(
-        unpack_kernel,
+        functools.partial(unpack_kernel, order),
         in_specs=[pl.BlockSpec(memory_space=pltpu.VMEM)],
         out_specs=pl.BlockSpec(memory_space=pltpu.VMEM),
         out_shape=jax.ShapeDtypeStruct(out, jnp.bfloat16),
@@ -367,9 +376,9 @@
         (ht1, beside, edge + own),
     )
     pieces_z = ((got_z, every, edge), (hz0, every, 0), (hz1, every, edge + own))
-    out = attend(info, pieces_n, got_q, rest, 0, None, frames)
-    out = attend(info, pieces_z, got_q, 1, rest, out, frames)
-    return unpack(exchange(out), rows, cols)
+    out = attend(info, pieces_z, got_q, 1, rest, 0, None, frames)
+    out = attend(info, pieces_n, got_q, rest, 0, 1, out, frames)
+    return unpack(exchange(out), (rest, *range(rest)), rows, cols)
 
 
 def solution(mesh):

time: 210 us -> 197 us (0.938)
  the two profiles are of different devices: /device:TPU:1 before, /device:TPU:64 now
where the time goes in v4:
time: 197 us; the launch traced here: 196 us
  waiting for transfers between devices  76.9 us (39%)
  starting transfers between devices  54.6 us (28%)
  blocking collectives  31.7 us (16%)
  Pallas kernels  29.8 us (15%)
  local copies, waits for them, and re-layouts  2.75 us (1%)
    ppermute x10, waiting for transfers between devices, shifted(): return lax.ppermute(value, axis, pairs)  51.7 us
    ppermute x10, starting transfers between devices, shifted(): return lax.ppermute(value, axis, pairs)  37 us
    all_to_all x1, blocking collectives, exchange(): return lax.all_to_all(value, 'hd', split_axis=0, concat_axis=0, tiled=True)  31.7 us
    all_to_all x3, waiting for transfers between devices, exchange(): return lax.all_to_all(value, 'hd', split_axis=0, concat_axis=0, tiled=True)  25.2 us
    all_to_all x3, starting transfers between devices, exchange(): return lax.all_to_all(value, 'hd', split_axis=0, concat_axis=0, tiled=True)  17.6 us
    pallas_call x2, Pallas kernels, attend(): pl.pallas_call(functools.partial(attend_kernel, tuple(((spans, low) for _...  14.3 us
    pallas_call x3, Pallas kernels, pack(): one_step(kernel, in_specs, outs, 4 * math.prod(outs[0]), PACK_GRANT)  7.89 us
    pallas_call x3, Pallas kernels, rim(): one_step(functools.partial(rim_kernel, edge, counts), in_specs, [out, out...  4.22 us
  transfers between devices with their start and end apart: 13, of which 6 were waited for; matrix products, arithmetic and copies ran while one was open for 0% of the time, Pallas kernels for 8%

profile of v4, /device:TPU:64, one launch (start us, length us, event | category | flops | bytes accessed | tf_op | source)
XLA Modules:
  0.0 196.1 jit_solution(6300121625649348715)
XLA Ops:
  0.0 2.8 %shard_map.64 = bf16[8,16,32,128]{3,2,1,0:T(8,128)(2,1)} custom-call(bf16[4,4,8,9216]{3,2,1,0:T(8,128)(2,1)} %refs_1_.3, bf16[4,4,8,9216]{3,2,1,0:T(8,128)(2,1)} %refs_1_.3, f32[1,128]{1,0:T(1,128)} %bitcast.2, f32[1,128]{1,0:T(1,128)} %bitcast.5), custom_call_target="tpu_custom_call" | custom-call | flops 2097152 | bytes 2097152 | tf_op jit(solution)/shard_map/pallas_call | solution.py:77
  2.8 7.1 %all-to-all-start = ((bf16[8,16,32,128]{3,2,1,0:T(8,128)(2,1)}), bf16[8,16,32,128]{3,2,1,0:T(8,128)(2,1)S(1)}, u32[]{:S(2)}, u32[]{:S(2)}) async-start(bf16[8,16,32,128]{3,2,1,0:T(8,128)(2,1)} %shard_map.64), calls=%async_computation | async-start | bytes 2097152 | tf_op jit(solution)/shard_map/all_to_all | solution.py:320
  9.9 2.6 %shard_map.69 = (bf16[8,8,32,128]{3,2,1,0:T(8,128)(2,1)}, bf16[8,4,32,128]{3,2,1,0:T(8,128)(2,1)}, bf16[8,4,32,128]{3,2,1,0:T(8,128)(2,1)}) custom-call(bf16[4,4,8,9216]{3,2,1,0:T(8,128)(2,1)} %refs_1_.3, bf16[4,4,8,9216]{3,2,1,0:T(8,128)(2,1)} %refs_1_.3, f32[1,128]{1,0:T(1,128)} %bitcast.3, f32[1,128]{1,0:T(1,128)} %bitcast.6), custom_call_target="tpu_custom_call" | custom-call | flops 1048576 | bytes 1048576 | tf_op jit(solution)/shard_map/pallas_call | solution.py:77
  12.5 10.0 %collective-permute-start.6 = (bf16[8,4,32,128]{3,2,1,0:T(8,128)(2,1)}, bf16[8,4,32,128]{3,2,1,0:T(8,128)(2,1)S(1)}, u32[]{:S(2)}, u32[]{:S(2)}) collective-permute-start(bf16[8,4,32,128]{3,2,1,0:T(8,128)(2,1)} %get-tuple-element.23), channel_id=1, source_target_pairs={{0,64},{64,128},{128,192},{192,256},{256,320},{320,384},{384,448},... | collective-permute-start | bytes 786440 | tf_op jit(solution)/shard_map/ppermute | solution.py:316
  23.8 9.9 %collective-permute-done.6.t0_ref = bf16[8,4,32,128]{3,2,1,0:T(8,128)(2,1)S(1)} collective-permute-done((bf16[8,4,32,128]{3,2,1,0:T(8,128)(2,1)}, bf16[8,4,32,128]{3,2,1,0:T(8,128)(2,1)S(1)}, u32[]{:S(2)}, u32[]{:S(2)}) %collective-permute-start.6) | collective-permute-done | bytes 262176 | tf_op jit(solution)/shard_map/ppermute | solution.py:316
  33.7 11.9 %collective-permute-done.7.t1_ref = bf16[8,4,32,128]{3,2,1,0:T(8,128)(2,1)S(1)} collective-permute-done((bf16[8,4,32,128]{3,2,1,0:T(8,128)(2,1)}, bf16[8,4,32,128]{3,2,1,0:T(8,128)(2,1)S(1)}, u32[]{:S(2)}, u32[]{:S(2)}) %collective-permute-start.7) | collective-permute-done | bytes 262176 | tf_op jit(solution)/shard_map/ppermute | solution.py:316
  46.3 2.2 %shard_map.70 = bf16[8,16,32,128]{3,2,1,0:T(8,128)(2,1)} custom-call(bf16[8,8,32,128]{3,2,1,0:T(8,128)(2,1)} %get-tuple-element.22.c_ref, bf16[8,4,32,128]{3,2,1,0:T(8,128)(2,1)} %copy-done.2, bf16[8,4,32,128]{3,2,1,0:T(8,128)(2,1)} %copy-done.3), custom_call_target="tpu_custom_call" | custom-call | flops 2097152 | bytes 2097152 | tf_op jit(solution)/shard_map/pallas_call | solution.py:98
  48.5 6.9 %all-to-all-start.2 = ((bf16[8,16,32,128]{3,2,1,0:T(8,128)(2,1)}), bf16[8,16,32,128]{3,2,1,0:T(8,128)(2,1)}, u32[]{:S(2)}, u32[]{:S(2)}) async-start(bf16[8,16,32,128]{3,2,1,0:T(8,128)(2,1)} %shard_map.70), calls=%async_computation.2 | async-start | bytes 2097152 | tf_op jit(solution)/shard_map/all_to_all | solution.py:320
  55.4 2.5 %shard_map.68 = bf16[8,12,32,128]{3,2,1,0:T(8,128)(2,1)} custom-call(bf16[4,4,8,9216]{3,2,1,0:T(8,128)(2,1)} %refs_1_.3, f32[1,128]{1,0:T(1,128)} %bitcast.4, f32[1,128]{1,0:T(1,128)} %bitcast.7), custom_call_target="tpu_custom_call" | custom-call | flops 1572864 | bytes 1572864 | tf_op jit(solution)/shard_map/pallas_call | solution.py:77
  57.9 25.2 %all-to-all-done.2.refs_0_ = bf16[8,16,32,128]{3,2,1,0:T(8,128)(2,1)} async-done(((bf16[8,16,32,128]{3,2,1,0:T(8,128)(2,1)}), bf16[8,16,32,128]{3,2,1,0:T(8,128)(2,1)}, u32[]{:S(2)}, u32[]{:S(2)}) %all-to-all-start.2) | async-done | bytes 1048608 | tf_op jit(solution)/shard_map/all_to_all | solution.py:320
  83.1 3.5 %all-to-all-start.1 = ((bf16[8,12,32,128]{3,2,1,0:T(8,128)(2,1)}), bf16[8,12,32,128]{3,2,1,0:T(8,128)(2,1)S(1)}, u32[]{:S(2)}, u32[]{:S(2)}) async-start(bf16[8,12,32,128]{3,2,1,0:T(8,128)(2,1)} %shard_map.68), calls=%async_computation.1 | async-start | bytes 1572864 | tf_op jit(solution)/shard_map/all_to_all | solution.py:320
  86.8 8.2 %collective-permute-start = (bf16[8,8,32,128]{3,2,1,0:T(8,128)(2,1)S(1)}, bf16[8,8,32,128]{3,2,1,0:T(8,128)(2,1)S(1)}, u32[]{:S(2)}, u32[]{:S(2)}) collective-permute-start(bf16[8,8,32,128]{3,2,1,0:T(8,128)(2,1)S(1)} %get-tuple-element.16), channel_id=1, source_target_pairs={{0,64},{64,128},{128,192},{192,256},{256,320},{320,384},{384,448},... | collective-permute-start | bytes 1572872 | tf_op jit(solution)/shard_map/ppermute | solution.py:316
  96.3 2.1 %shard_map.71 = (bf16[8,16,16,128]{3,2,1,0:T(8,128)(2,1)}, bf16[8,16,16,128]{3,2,1,0:T(8,128)(2,1)S(1)}) custom-call(bf16[8,16,32,128]{3,2,1,0:T(8,128)(2,1)} %all-to-all-done.2.refs_0_), custom_call_target="tpu_custom_call" | custom-call | flops 2097152 | bytes 2097152 | tf_op jit(solution)/shard_map/pallas_call | solution.py:143
  98.4 1.9 collective-permute-start.8
  100.3 3.6 %collective-permute-start.9 = (bf16[8,16,16,128]{3,2,1,0:T(8,128)(2,1)}, bf16[8,16,16,128]{3,2,1,0:T(8,128)(2,1)}, u32[]{:S(2)}, u32[]{:S(2)}) collective-permute-start(bf16[8,16,16,128]{3,2,1,0:T(8,128)(2,1)} %get-tuple-element.26), channel_id=1, source_target_pairs={{8,0},{16,8},{24,16},{32,24},{40,32},{48,40},{56,48},{9,1},{17,9},... | collective-permute-start | bytes 1572872 | tf_op jit(solution)/shard_map/ppermute | solution.py:316
  105.0 3.2 %collective-permute-start.2 = (bf16[8,16,16,128]{3,2,1,0:T(8,128)(2,1)}, bf16[8,16,16,128]{3,2,1,0:T(8,128)(2,1)}, u32[]{:S(2)}, u32[]{:S(2)}) collective-permute-start(bf16[8,16,16,128]{3,2,1,0:T(8,128)(2,1)} %get-tuple-element.18), channel_id=1, source_target_pairs={{0,8},{8,16},{16,24},{24,32},{32,40},{40,48},{48,56},{1,9},{9,17},... | collective-permute-start | bytes 1572872 | tf_op jit(solution)/shard_map/ppermute | solution.py:316
  108.2 4.9 %collective-permute-done.refs_0_.refs_1_ = bf16[8,8,32,128]{3,2,1,0:T(8,128)(2,1)S(1)} collective-permute-done((bf16[8,8,32,128]{3,2,1,0:T(8,128)(2,1)S(1)}, bf16[8,8,32,128]{3,2,1,0:T(8,128)(2,1)S(1)}, u32[]{:S(2)}, u32[]{:S(2)}) %collective-permute-start) | collective-permute-done | bytes 524320 | tf_op jit(solution)/shard_map/ppermute | solution.py:316
  113.2 1.9 collective-permute-start.3
  115.1 24.1 %collective-permute-done.1.refs_1_.refs_2_ = bf16[8,8,32,128]{3,2,1,0:T(8,128)(2,1)S(1)} collective-permute-done((bf16[8,8,32,128]{3,2,1,0:T(8,128)(2,1)S(1)}, bf16[8,8,32,128]{3,2,1,0:T(8,128)(2,1)S(1)}, u32[]{:S(2)}, u32[]{:S(2)}) %collective-permute-start.1) | collective-permute-done | bytes 524320 | tf_op jit(solution)/shard_map/ppermute | solution.py:316
  140.3 1.9 collective-permute-start.4
  143.0 3.6 %collective-permute-start.5 = (bf16[8,16,16,128]{3,2,1,0:T(8,128)(2,1)}, bf16[8,16,16,128]{3,2,1,0:T(8,128)(2,1)}, u32[]{:S(2)}, u32[]{:S(2)}) collective-permute-start(bf16[8,16,16,128]{3,2,1,0:T(8,128)(2,1)} %get-tuple-element.21), channel_id=1, source_target_pairs={{8,0},{16,8},{24,16},{32,24},{40,32},{48,40},{56,48},{9,1},{17,9},... | collective-permute-start | bytes 1572872 | tf_op jit(solution)/shard_map/ppermute | solution.py:316
  148.0 4.7 %attend.2.refs_8_ = bf16[8,1,4,32,128]{4,3,2,1,0:T(8,128)(2,1)S(1)} custom-call(s32[17]{0:T(128)S(1)} %pad_add_fusion.info_ref, bf16[8,16,32,128]{3,2,1,0:T(8,128)(2,1)} %all-to-all-done.2.refs_0_, bf16[8,16,16,128]{3,2,1,0:T(8,128)(2,1)S(1)} %copy-done.1, bf16[8,16,16,128]{3,2,1,0:T(8,128)(2,1)} %collective-permute-done.9.refs_2_, ...), custom_call_target="tpu_custom_call" | custom-call | flops 754974720 | bytes 4194304 | tf_op jit(solution)/shard_map/attend/pallas_call | solution.py:264
  153.6 9.7 %attend.3 = bf16[8,3,4,32,128]{4,3,2,1,0:T(8,128)(2,1)S(1)} custom-call(s32[17]{0:T(128)S(1)} %pad_add_fusion.info_ref, bf16[8,16,32,128]{3,2,1,0:T(8,128)(2,1)S(1)} %all-to-all-done.ref.refs_0_, bf16[8,8,32,128]{3,2,1,0:T(8,128)(2,1)S(1)} %collective-permute-done.refs_0_.refs_1_, bf16[8,8,32,128]{3,2,1,0:T(8,128)(2,1)S(1)} %collective-permute-done.1.refs_1_.refs_2_, ...), custom_call_target="tpu_custom_call" | custom-call | flops 1509949440 | bytes 8388608 | tf_op jit(solution)/shard_map/attend/pallas_call | solution.py:264
  163.3 31.7 %all_to_all.20.in_ref = bf16[8,3,4,32,128]{4,3,2,1,0:T(8,128)(2,1)S(1)} all-to-all(bf16[8,3,4,32,128]{4,3,2,1,0:T(8,128)(2,1)S(1)} %attend.3), channel_id=1, replica_groups=mesh['ta'=8,'ha'=8,'hd'=8] {'hd'}, dimensions={0} | all-to-all | bytes 1572864 | tf_op jit(solution)/shard_map/all_to_all | solution.py:320
  (31 shorter events, 9.7 us)
Async XLA Ops:
  2.8 45.7 %all-to-all-start = ((bf16[8,16,32,128]{3,2,1,0:T(8,128)(2,1)}), bf16[8,16,32,128]{3,2,1,0:T(8,128)(2,1)S(1)}, u32[]{:S(2)}, u32[]{:S(2)}) async-start(bf16[8,16,32,128]{3,2,1,0:T(8,128)(2,1)} %shard_map.64), calls=%async_computation | async-start | bytes 2097152 | tf_op jit(solution)/shard_map/all_to_all | solution.py:320
  12.5 21.2 %collective-permute-start.6 = (bf16[8,4,32,128]{3,2,1,0:T(8,128)(2,1)}, bf16[8,4,32,128]{3,2,1,0:T(8,128)(2,1)S(1)}, u32[]{:S(2)}, u32[]{:S(2)}) collective-permute-start(bf16[8,4,32,128]{3,2,1,0:T(8,128)(2,1)} %get-tuple-element.23), channel_id=1, source_target_pairs={{0,64},{64,128},{128,192},{192,256},{256,320},{320,384},{384,448},... | collective-permute-start | bytes 786440 | tf_op jit(solution)/shard_map/ppermute | solution.py:316
  22.5 23.1 %collective-permute-start.7 = (bf16[8,4,32,128]{3,2,1,0:T(8,128)(2,1)}, bf16[8,4,32,128]{3,2,1,0:T(8,128)(2,1)S(1)}, u32[]{:S(2)}, u32[]{:S(2)}) collective-permute-start(bf16[8,4,32,128]{3,2,1,0:T(8,128)(2,1)} %get-tuple-element.24), channel_id=1, source_target_pairs={{64,0},{128,64},{192,128},{256,192},{320,256},{384,320},{448,384},... | collective-permute-start | bytes 786440 | tf_op jit(solution)/shard_map/ppermute | solution.py:316
  33.7 11.9 %copy-start.2 = (bf16[8,4,32,128]{3,2,1,0:T(8,128)(2,1)}, bf16[8,4,32,128]{3,2,1,0:T(8,128)(2,1)S(1)}, u32[]{:S(2)}) copy-start(bf16[8,4,32,128]{3,2,1,0:T(8,128)(2,1)S(1)} %collective-permute-done.6.t0_ref) | copy-start | bytes 786436
  45.6 0.7 copy-start.3
  48.5 34.6 %all-to-all-start.2 = ((bf16[8,16,32,128]{3,2,1,0:T(8,128)(2,1)}), bf16[8,16,32,128]{3,2,1,0:T(8,128)(2,1)}, u32[]{:S(2)}, u32[]{:S(2)}) async-start(bf16[8,16,32,128]{3,2,1,0:T(8,128)(2,1)} %shard_map.70), calls=%async_computation.2 | async-start | bytes 2097152 | tf_op jit(solution)/shard_map/all_to_all | solution.py:320
  83.1 63.8 %all-to-all-start.1 = ((bf16[8,12,32,128]{3,2,1,0:T(8,128)(2,1)}), bf16[8,12,32,128]{3,2,1,0:T(8,128)(2,1)S(1)}, u32[]{:S(2)}, u32[]{:S(2)}) async-start(bf16[8,12,32,128]{3,2,1,0:T(8,128)(2,1)} %shard_map.68), calls=%async_computation.1 | async-start | bytes 1572864 | tf_op jit(solution)/shard_map/all_to_all | solution.py:320
  86.7 60.0 %copy-start.4 = (s32[3,3]{1,0:T(4,128)S(1)}, s32[3,3]{1,0:T(4,128)}, u32[]{:S(2)}) copy-start(s32[3,3]{1,0:T(4,128)} %param.9) | copy-start | bytes 112
  86.7 60.1 %copy-start.5 = (s32[16]{0:T(128)S(1)}, s32[16]{0:T(128)}, u32[]{:S(2)}) copy-start(s32[16]{0:T(128)} %param.11) | copy-start | bytes 196
  86.7 60.1 %copy-start.6 = (s32[16]{0:T(128)S(1)}, s32[16]{0:T(128)}, u32[]{:S(2)}) copy-start(s32[16]{0:T(128)} %param.10) | copy-start | bytes 196
  86.8 26.4 %collective-permute-start = (bf16[8,8,32,128]{3,2,1,0:T(8,128)(2,1)S(1)}, bf16[8,8,32,128]{3,2,1,0:T(8,128)(2,1)S(1)}, u32[]{:S(2)}, u32[]{:S(2)}) collective-permute-start(bf16[8,8,32,128]{3,2,1,0:T(8,128)(2,1)S(1)} %get-tuple-element.16), channel_id=1, source_target_pairs={{0,64},{64,128},{128,192},{192,256},{256,320},{320,384},{384,448},... | collective-permute-start | bytes 1572872 | tf_op jit(solution)/shard_map/ppermute | solution.py:316
  95.0 44.2 %collective-permute-start.1 = (bf16[8,8,32,128]{3,2,1,0:T(8,128)(2,1)S(1)}, bf16[8,8,32,128]{3,2,1,0:T(8,128)(2,1)S(1)}, u32[]{:S(2)}, u32[]{:S(2)}) collective-permute-start(bf16[8,8,32,128]{3,2,1,0:T(8,128)(2,1)S(1)} %get-tuple-element.17), channel_id=1, source_target_pairs={{64,0},{128,64},{192,128},{256,192},{320,256},{384,320},{448,384},... | collective-permute-start | bytes 1572872 | tf_op jit(solution)/shard_map/ppermute | solution.py:316
  98.4 43.8 %collective-permute-start.8 = (bf16[8,16,16,128]{3,2,1,0:T(8,128)(2,1)S(1)}, bf16[8,16,16,128]{3,2,1,0:T(8,128)(2,1)S(1)}, u32[]{:S(2)}, u32[]{:S(2)}) collective-permute-start(bf16[8,16,16,128]{3,2,1,0:T(8,128)(2,1)S(1)} %get-tuple-element.25), channel_id=1, source_target_pairs={{0,8},{8,16},{16,24},{24,32},{32,40},{40,48},{48,56},{1,9},{9,17},... | collective-permute-start | bytes 1572872 | tf_op jit(solution)/shard_map/ppermute | solution.py:316
  100.3 46.6 %collective-permute-start.9 = (bf16[8,16,16,128]{3,2,1,0:T(8,128)(2,1)}, bf16[8,16,16,128]{3,2,1,0:T(8,128)(2,1)}, u32[]{:S(2)}, u32[]{:S(2)}) collective-permute-start(bf16[8,16,16,128]{3,2,1,0:T(8,128)(2,1)} %get-tuple-element.26), channel_id=1, source_target_pairs={{8,0},{16,8},{24,16},{32,24},{40,32},{48,40},{56,48},{9,1},{17,9},... | collective-permute-start | bytes 1572872 | tf_op jit(solution)/shard_map/ppermute | solution.py:316
  105.0 47.6 %collective-permute-start.2 = (bf16[8,16,16,128]{3,2,1,0:T(8,128)(2,1)}, bf16[8,16,16,128]{3,2,1,0:T(8,128)(2,1)}, u32[]{:S(2)}, u32[]{:S(2)}) collective-permute-start(bf16[8,16,16,128]{3,2,1,0:T(8,128)(2,1)} %get-tuple-element.18), channel_id=1, source_target_pairs={{0,8},{8,16},{16,24},{24,32},{32,40},{40,48},{48,56},{1,9},{9,17},... | collective-permute-start | bytes 1572872 | tf_op jit(solution)/shard_map/ppermute | solution.py:316
  113.2 39.5 %collective-permute-start.3 = (bf16[8,16,16,128]{3,2,1,0:T(8,128)(2,1)}, bf16[8,16,16,128]{3,2,1,0:T(8,128)(2,1)}, u32[]{:S(2)}, u32[]{:S(2)}) collective-permute-start(bf16[8,16,16,128]{3,2,1,0:T(8,128)(2,1)} %get-tuple-element.19), channel_id=1, source_target_pairs={{8,0},{16,8},{24,16},{32,24},{40,32},{48,40},{56,48},{9,1},{17,9},... | collective-permute-start | bytes 1572872 | tf_op jit(solution)/shard_map/ppermute | solution.py:316
  140.3 12.4 %collective-permute-start.4 = (bf16[8,16,16,128]{3,2,1,0:T(8,128)(2,1)}, bf16[8,16,16,128]{3,2,1,0:T(8,128)(2,1)}, u32[]{:S(2)}, u32[]{:S(2)}) collective-permute-start(bf16[8,16,16,128]{3,2,1,0:T(8,128)(2,1)} %get-tuple-element.20), channel_id=1, source_target_pairs={{0,8},{8,16},{16,24},{24,32},{32,40},{40,48},{48,56},{1,9},{9,17},... | collective-permute-start | bytes 1572872 | tf_op jit(solution)/shard_map/ppermute | solution.py:316
  142.2 0.8 copy-start
  143.0 10.6 %collective-permute-start.5 = (bf16[8,16,16,128]{3,2,1,0:T(8,128)(2,1)}, bf16[8,16,16,128]{3,2,1,0:T(8,128)(2,1)}, u32[]{:S(2)}, u32[]{:S(2)}) collective-permute-start(bf16[8,16,16,128]{3,2,1,0:T(8,128)(2,1)} %get-tuple-element.21), channel_id=1, source_target_pairs={{8,0},{16,8},{24,16},{32,24},{40,32},{48,40},{56,48},{9,1},{17,9},... | collective-permute-start | bytes 1572872 | tf_op jit(solution)/shard_map/ppermute | solution.py:316
  146.9 1.0 copy-start.1

commit v5 on v4

--- a/solution.py
+++ b/solution.py
@@ -80,6 +80,38 @@
     return packed if tiles else packed[0]
 
 
+def pack_shifts_kernel(heads, groups, me_ref, part_ref, gain_ref, *out_refs):
+    frames, rows, cols = part_ref.shape[:3]
+    head_dim = gain_ref.shape[-1]
+    gain = gain_ref[...].reshape(1, 1, 1, head_dim)
+    for shift in range(groups):
+        dest = lax.rem(me_ref[0] + shift, groups)
+        for head in range(heads):
+            at = pl.multiple_of((heads * dest + head) * head_dim, head_dim)
+            x = part_ref[:, :, :, pl.ds(at, head_dim)].astype(jnp.float32)
+            meansq = jnp.mean(x * x, axis=-1, keepdims=True)
+            x = x * lax.rsqrt(meansq + 1e-06) * gain
+            x = x.reshape(frames, rows * cols, head_dim).astype(jnp.bfloat16)
+            out_refs[shift][head * frames : (head + 1) * frames] = x
+
+
+def pack_shifts(me, qkv, gain, heads, groups):
+    frames, rows, cols, channels = qkv.shape
+    head_dim = gain.shape[-1]
+    outs = [(heads * frames, rows * cols, head_dim)] * groups
+    return one_step(
+        functools.partial(pack_shifts_kernel, heads, groups),
+        [
+            pl.BlockSpec(memory_space=pltpu.SMEM),
+            pl.BlockSpec((frames, rows, cols, channels // 3), lambda i: (0, 0, 0, 0)),
+            whole((1, head_dim)),
+        ],
+        outs,
+        4 * groups * math.prod(outs[0]),
+        PACK_GRANT,
+    )(me, qkv, gain.reshape(1, -1))
+
+
 def join_kernel(frames, c_ref, t0_ref, t1_ref, out_ref):
     long = frames + 2 * TT
     for kv in range(2):
@@ -148,12 +180,11 @@
 def attend_kernel(pieces, frames, span, reach, scale, head, slot, info_ref, *refs):
     count = len(pieces)
     piece_refs = refs[:count]
-    q_ref = refs[count]
-    out_ref, k_ref, v_ref, bias_ref = refs[-4:]
+    out_ref, k_ref, v_ref, q_ref, bias_ref = refs[-5:]
+    groups = q_ref.shape[0]
     here = slot + pl.program_id(0)
-    if len(refs) > count + 5:
-        out_ref[:, 0:slot] = refs[count + 1][...]
-    groups = q_ref.shape[0]
+    if slot:
+        out_ref[:, 0:slot] = refs[count + groups][...]
     own, head_dim = q_ref.shape[2:]
     edge = TH * TW
     for ref, (spans, low) in zip(piece_refs, pieces):
@@ -168,6 +199,8 @@
     tiles_h = own // edge
     base_t = info_ref.shape[0] - (tiles_t + 2) - (tiles_h + 2)
     base_h = base_t + tiles_t + 2
+    for shift in range(groups):
+        q_ref[lax.rem(info_ref[base_t - 1] + (groups - shift), groups)] = refs[count + shift][...]
     head = head + pl.program_id(0)
     rad_t = info_ref[3 * head]
     rad_h = info_ref[3 * head + 1]
@@ -238,7 +271,8 @@
 
 
 def attend(info, pieces, queries, heads, head, slot, before, frames):
-    groups, _, own, head_dim = queries.shape
+    groups = len(queries)
+    _, own, head_dim = queries[0].shape
     span = max(groups // 2, 1)
     reach = min(span + 1, groups)
     edge = TH * TW
@@ -254,9 +288,9 @@
         for a, spans, _ in pieces
     ]
     in_specs += [
-        pl.BlockSpec((groups, frames, own, head_dim), lambda h: (0, head + h, 0, 0)),
+        pl.BlockSpec((frames, own, head_dim), lambda h: (head + h, 0, 0)) for _ in queries
     ]
-    args = [info, *(a for a, _, _ in pieces), queries]
+    args = [info, *(a for a, _, _ in pieces), *queries]
     total = slot + heads
     if before is not None:
         in_specs.append(pl.BlockSpec(before.shape, lambda h: (0, 0, 0, 0, 0)))
@@ -279,6 +313,7 @@
         scratch_shapes=[
             pltpu.VMEM(ext, jnp.bfloat16),
             pltpu.VMEM(ext, jnp.bfloat16),
+            pltpu.VMEM((groups, frames, own, head_dim), jnp.bfloat16),
             pltpu.VMEM((groups // span, nq, nk), jnp.float32),
         ],
         cost_estimate=cost(4 * steps * nq * nk * head_dim, heads * (4 << 20), steps * nq * nk),
@@ -329,13 +364,14 @@
     own = rows * cols
     tiles_t = frames // TT
     tiles_h = rows // TH
+    me = lax.axis_index("hd").astype(jnp.int32).reshape(1)
     near_t = lax.dynamic_slice(
         jnp.pad(frame_counts, (1, 1)), (lax.axis_index("ta") * tiles_t,), (tiles_t + 2,)
     )
     near_h = lax.dynamic_slice(
         jnp.pad(row_counts, (1, 1)), (lax.axis_index("ha") * tiles_h,), (tiles_h + 2,)
     )
-    info = jnp.concatenate([windows.reshape(-1), near_t, near_h])
+    info = jnp.concatenate([windows.reshape(-1), me, near_t, near_h])
 
     def packed(entries, tiles=False):
         return pack(qkv, q_gain, k_gain, tuple(entries), heads, groups, tiles)
@@ -347,7 +383,11 @@
     tz1 = shifted(first_z, "ta", -1)
     value_n = packed([(part, head) for head in range(rest) for part in (1, 2)])
     got_n = exchange(value_n)
-    got_q = exchange(packed([(0, head) for head in range(heads)]))
+    value_q = pack_shifts(me, qkv, q_gain, heads, groups)
+    got_q = list(value_q[:1])
+    for shift in range(1, groups):
+        hops = [(i, (i + shift) % groups) for i in range(groups)]
+        got_q.append(lax.ppermute(value_q[shift], "hd", hops))
     joined = join(value_z, tz0, tz1)
     got_z = exchange(joined)
 

time: 197 us -> 188 us (0.954)
  the two profiles are of different devices: /device:TPU:64 before, /device:TPU:65 now
where the time goes in v5:
time: 188 us; the launch traced here: 187 us
  starting transfers between devices  71.4 us (38%)
  waiting for transfers between devices  54.3 us (29%)
  Pallas kernels  30.4 us (16%)
  blocking collectives  27.5 us (15%)
  local copies, waits for them, and re-layouts  3.56 us (2%)
    ppermute x10, starting transfers between devices, shifted(): return lax.ppermute(value, axis, pairs)  39.5 us
    all_to_all x1, blocking collectives, exchange(): return lax.all_to_all(value, 'hd', split_axis=0, concat_axis=0, tiled=True)  27.5 us
    ppermute x10, waiting for transfers between devices, shifted(): return lax.ppermute(value, axis, pairs)  24.6 us
    all_to_all x2, waiting for transfers between devices, exchange(): return lax.all_to_all(value, 'hd', split_axis=0, concat_axis=0, tiled=True)  18.9 us
    ppermute x7, starting transfers between devices, shards(): got_q.append(lax.ppermute(value_q[shift], 'hd', hops))  18.7 us
    pallas_call x2, Pallas kernels, attend(): pl.pallas_call(functools.partial(attend_kernel, tuple(((spans, low) for _...  14.3 us
    all_to_all x2, starting transfers between devices, exchange(): return lax.all_to_all(value, 'hd', split_axis=0, concat_axis=0, tiled=True)  13.2 us
    ppermute x7, waiting for transfers between devices, shards(): got_q.append(lax.ppermute(value_q[shift], 'hd', hops))  10.7 us
  transfers between devices with their start and end apart: 19, of which 8 were waited for; matrix products, arithmetic and copies ran while one was open for 0% of the time, Pallas kernels for 9%

profile of v5, /device:TPU:65, one launch (start us, length us, event | category | flops | bytes accessed | tf_op | source)
XLA Modules:
  0.0 187.5 jit_solution(3800490085599175769)
XLA Ops:
  0.0 2.7 %shard_map.64 = bf16[8,16,32,128]{3,2,1,0:T(8,128)(2,1)} custom-call(bf16[4,4,8,9216]{3,2,1,0:T(8,128)(2,1)} %refs_1_.3, bf16[4,4,8,9216]{3,2,1,0:T(8,128)(2,1)} %refs_1_.3, f32[1,128]{1,0:T(1,128)} %bitcast.3, f32[1,128]{1,0:T(1,128)} %bitcast.6), custom_call_target="tpu_custom_call" | custom-call | flops 2097152 | bytes 2097152 | tf_op jit(solution)/shard_map/pallas_call | solution.py:77
  2.8 6.8 %all-to-all-start = ((bf16[8,16,32,128]{3,2,1,0:T(8,128)(2,1)}), bf16[8,16,32,128]{3,2,1,0:T(8,128)(2,1)S(1)}, u32[]{:S(2)}, u32[]{:S(2)}) async-start(bf16[8,16,32,128]{3,2,1,0:T(8,128)(2,1)} %shard_map.64), calls=%async_computation | async-start | bytes 2097152 | tf_op jit(solution)/shard_map/all_to_all | solution.py:355
  9.6 2.6 %shard_map.69 = (bf16[8,8,32,128]{3,2,1,0:T(8,128)(2,1)}, bf16[8,4,32,128]{3,2,1,0:T(8,128)(2,1)}, bf16[8,4,32,128]{3,2,1,0:T(8,128)(2,1)}) custom-call(bf16[4,4,8,9216]{3,2,1,0:T(8,128)(2,1)} %refs_1_.3, bf16[4,4,8,9216]{3,2,1,0:T(8,128)(2,1)} %refs_1_.3, f32[1,128]{1,0:T(1,128)} %bitcast.4, f32[1,128]{1,0:T(1,128)} %bitcast.7), custom_call_target="tpu_custom_call" | custom-call | flops 1048576 | bytes 1048576 | tf_op jit(solution)/shard_map/pallas_call | solution.py:77
  12.1 9.7 %collective-permute-start.13 = (bf16[8,4,32,128]{3,2,1,0:T(8,128)(2,1)}, bf16[8,4,32,128]{3,2,1,0:T(8,128)(2,1)S(1)}, u32[]{:S(2)}, u32[]{:S(2)}) collective-permute-start(bf16[8,4,32,128]{3,2,1,0:T(8,128)(2,1)} %get-tuple-element.39), channel_id=1, source_target_pairs={{0,64},{64,128},{128,192},{192,256},{256,320},{320,384},{384,448},... | collective-permute-start | bytes 786440 | tf_op jit(solution)/shard_map/ppermute | solution.py:351
  23.2 6.9 %collective-permute-done.13.t0_ref = bf16[8,4,32,128]{3,2,1,0:T(8,128)(2,1)S(1)} collective-permute-done((bf16[8,4,32,128]{3,2,1,0:T(8,128)(2,1)}, bf16[8,4,32,128]{3,2,1,0:T(8,128)(2,1)S(1)}, u32[]{:S(2)}, u32[]{:S(2)}) %collective-permute-start.13) | collective-permute-done | bytes 262176 | tf_op jit(solution)/shard_map/ppermute | solution.py:351
  30.1 14.5 %collective-permute-done.14.t1_ref = bf16[8,4,32,128]{3,2,1,0:T(8,128)(2,1)S(1)} collective-permute-done((bf16[8,4,32,128]{3,2,1,0:T(8,128)(2,1)}, bf16[8,4,32,128]{3,2,1,0:T(8,128)(2,1)S(1)}, u32[]{:S(2)}, u32[]{:S(2)}) %collective-permute-start.14) | collective-permute-done | bytes 262176 | tf_op jit(solution)/shard_map/ppermute | solution.py:351
  47.6 6.4 %all-to-all-start.1 = ((bf16[8,16,32,128]{3,2,1,0:T(8,128)(2,1)}), bf16[8,16,32,128]{3,2,1,0:T(8,128)(2,1)S(1)}, u32[]{:S(2)}, u32[]{:S(2)}) async-start(bf16[8,16,32,128]{3,2,1,0:T(8,128)(2,1)} %shard_map.70), calls=%async_computation.1 | async-start | bytes 2097152 | tf_op jit(solution)/shard_map/all_to_all | solution.py:355
  55.0 7.9 %collective-permute-start = (bf16[8,8,32,128]{3,2,1,0:T(8,128)(2,1)}, bf16[8,8,32,128]{3,2,1,0:T(8,128)(2,1)S(1)}, u32[]{:S(2)}, u32[]{:S(2)}) collective-permute-start(bf16[8,8,32,128]{3,2,1,0:T(8,128)(2,1)} %get-tuple-element.24), channel_id=1, source_target_pairs={{0,64},{64,128},{128,192},{192,256},{256,320},{320,384},{384,448},... | collective-permute-start | bytes 1572872 | tf_op jit(solution)/shard_map/ppermute | solution.py:351
  64.2 18.9 %all-to-all-done.1.refs_0_ = bf16[8,16,32,128]{3,2,1,0:T(8,128)(2,1)S(1)} async-done(((bf16[8,16,32,128]{3,2,1,0:T(8,128)(2,1)}), bf16[8,16,32,128]{3,2,1,0:T(8,128)(2,1)S(1)}, u32[]{:S(2)}, u32[]{:S(2)}) %all-to-all-start.1) | async-done | bytes 1048608 | tf_op jit(solution)/shard_map/all_to_all | solution.py:355
  85.8 4.9 %collective-permute-start.15 = (bf16[8,16,16,128]{3,2,1,0:T(8,128)(2,1)}, bf16[8,16,16,128]{3,2,1,0:T(8,128)(2,1)}, u32[]{:S(2)}, u32[]{:S(2)}) collective-permute-start(bf16[8,16,16,128]{3,2,1,0:T(8,128)(2,1)} %get-tuple-element.41), channel_id=1, source_target_pairs={{0,8},{8,16},{16,24},{24,32},{32,40},{40,48},{48,56},{1,9},{9,17},... | collective-permute-start | bytes 1572872 | tf_op jit(solution)/shard_map/ppermute | solution.py:351
  90.7 2.3 %shard_map.68 = (bf16[12,32,128]{2,1,0:T(8,128)(2,1)}, bf16[12,32,128]{2,1,0:T(8,128)(2,1)}, bf16[12,32,128]{2,1,0:T(8,128)(2,1)}, bf16[12,32,128]{2,1,0:T(8,128...) custom-call(s32[1]{0:T(128)} %bitcast.me_ref, ...), custom_call_target="tpu_custom_call" | custom-call | flops 1572864 | bytes 1572864 | tf_op jit(solution)/shard_map/pallas_call | solution.py:102
  93.1 2.3 %collective-permute-start.6 = (bf16[12,32,128]{2,1,0:T(8,128)(2,1)}, bf16[12,32,128]{2,1,0:T(8,128)(2,1)S(1)}, u32[]{:S(2)}, u32[]{:S(2)}) collective-permute-start(bf16[12,32,128]{2,1,0:T(8,128)(2,1)} %get-tuple-element.31), channel_id=1, source_target_pairs={{0,1},{1,2},{2,3},{3,4},{4,5},{5,6},{6,7},{7,0},{8,9},{9,10},{10,1... | collective-permute-start | bytes 294920 | tf_op jit(solution)/shard_map/ppermute | solution.py:390
  97.3 5.1 %collective-permute-done.6.refs_4_.refs_8_ = bf16[12,32,128]{2,1,0:T(8,128)(2,1)S(1)} collective-permute-done((bf16[12,32,128]{2,1,0:T(8,128)(2,1)}, bf16[12,32,128]{2,1,0:T(8,128)(2,1)S(1)}, u32[]{:S(2)}, u32[]{:S(2)}) %collective-permute-start.6) | collective-permute-done | bytes 98336 | tf_op jit(solution)/shard_map/ppermute | solution.py:390
  105.0 3.4 %collective-permute-start.9 = (bf16[12,32,128]{2,1,0:T(8,128)(2,1)}, bf16[12,32,128]{2,1,0:T(8,128)(2,1)S(1)}, u32[]{:S(2)}, u32[]{:S(2)}) collective-permute-start(bf16[12,32,128]{2,1,0:T(8,128)(2,1)} %get-tuple-element.34), channel_id=1, source_target_pairs={{0,4},{1,5},{2,6},{3,7},{4,0},{5,1},{6,2},{7,3},{8,12},{9,13},{10,... | collective-permute-start | bytes 294920 | tf_op jit(solution)/shard_map/ppermute | solution.py:390
  108.4 2.9 %collective-permute-done.8.refs_6_.refs_10_ = bf16[12,32,128]{2,1,0:T(8,128)(2,1)S(1)} collective-permute-done((bf16[12,32,128]{2,1,0:T(8,128)(2,1)}, bf16[12,32,128]{2,1,0:T(8,128)(2,1)S(1)}, u32[]{:S(2)}, u32[]{:S(2)}) %collective-permute-start.8) | collective-permute-done | bytes 98336 | tf_op jit(solution)/shard_map/ppermute | solution.py:390
  111.3 4.0 %collective-permute-start.10 = (bf16[12,32,128]{2,1,0:T(8,128)(2,1)}, bf16[12,32,128]{2,1,0:T(8,128)(2,1)S(1)}, u32[]{:S(2)}, u32[]{:S(2)}) collective-permute-start(bf16[12,32,128]{2,1,0:T(8,128)(2,1)} %get-tuple-element.35), channel_id=1, source_target_pairs={{0,5},{1,6},{2,7},{3,0},{4,1},{5,2},{6,3},{7,4},{8,13},{9,14},{10,... | collective-permute-start | bytes 294920 | tf_op jit(solution)/shard_map/ppermute | solution.py:390
  117.4 2.3 %collective-permute-start.11 = (bf16[12,32,128]{2,1,0:T(8,128)(2,1)}, bf16[12,32,128]{2,1,0:T(8,128)(2,1)S(1)}, u32[]{:S(2)}, u32[]{:S(2)}) collective-permute-start(bf16[12,32,128]{2,1,0:T(8,128)(2,1)} %get-tuple-element.36), channel_id=1, source_target_pairs={{0,6},{1,7},{2,0},{3,1},{4,2},{5,3},{6,4},{7,5},{8,14},{9,15},{10,... | collective-permute-start | bytes 294920 | tf_op jit(solution)/shard_map/ppermute | solution.py:390
  119.7 2.9 %collective-permute-start.12 = (bf16[12,32,128]{2,1,0:T(8,128)(2,1)}, bf16[12,32,128]{2,1,0:T(8,128)(2,1)S(1)}, u32[]{:S(2)}, u32[]{:S(2)}) collective-permute-start(bf16[12,32,128]{2,1,0:T(8,128)(2,1)} %get-tuple-element.37), channel_id=1, source_target_pairs={{0,7},{1,0},{2,1},{3,2},{4,3},{5,4},{6,5},{7,6},{8,15},{9,8},{10,9... | collective-permute-start | bytes 294920 | tf_op jit(solution)/shard_map/ppermute | solution.py:390
  127.8 4.8 %collective-permute-start.2 = (bf16[8,16,16,128]{3,2,1,0:T(8,128)(2,1)}, bf16[8,16,16,128]{3,2,1,0:T(8,128)(2,1)}, u32[]{:S(2)}, u32[]{:S(2)}) collective-permute-start(bf16[8,16,16,128]{3,2,1,0:T(8,128)(2,1)} %get-tuple-element.26), channel_id=1, source_target_pairs={{0,8},{8,16},{16,24},{24,32},{32,40},{40,48},{48,56},{1,9},{9,17},... | collective-permute-start | bytes 1572872 | tf_op jit(solution)/shard_map/ppermute | solution.py:351
  134.6 3.6 %collective-permute-start.4 = (bf16[8,16,16,128]{3,2,1,0:T(8,128)(2,1)}, bf16[8,16,16,128]{3,2,1,0:T(8,128)(2,1)}, u32[]{:S(2)}, u32[]{:S(2)}) collective-permute-start(bf16[8,16,16,128]{3,2,1,0:T(8,128)(2,1)} %get-tuple-element.28), channel_id=1, source_target_pairs={{0,8},{8,16},{16,24},{24,32},{32,40},{40,48},{48,56},{1,9},{9,17},... | collective-permute-start | bytes 1572872 | tf_op jit(solution)/shard_map/ppermute | solution.py:351
  141.3 4.5 %attend.2.refs_15_ = bf16[8,1,4,32,128]{4,3,2,1,0:T(8,128)(2,1)S(1)} custom-call(s32[18]{0:T(128)S(1)} %pad_add_fusion.info_ref, bf16[8,16,32,128]{3,2,1,0:T(8,128)(2,1)S(1)} %copy-done.1, bf16[8,16,16,128]{3,2,1,0:T(8,128)(2,1)} %collective-permute-done.15.refs_1_, bf16[8,16,16,128]{3,2,1,0:T(8,128)(2,1)} %collective-permute-done.16.refs_2_, ...), custom_call_target="tpu_custom_call" | custom-call | flops 754974720 | bytes 4194304 | tf_op jit(solution)/shard_map/attend/pallas_call | solution.py:298
  145.9 3.2 %collective-permute-done.5.refs_6_ = bf16[8,16,16,128]{3,2,1,0:T(8,128)(2,1)} collective-permute-done((bf16[8,16,16,128]{3,2,1,0:T(8,128)(2,1)}, bf16[8,16,16,128]{3,2,1,0:T(8,128)(2,1)}, u32[]{:S(2)}, u32[]{:S(2)}) %collective-permute-start.5) | collective-permute-done | bytes 524320 | tf_op jit(solution)/shard_map/ppermute | solution.py:351
  149.1 9.8 %attend.3 = bf16[8,3,4,32,128]{4,3,2,1,0:T(8,128)(2,1)S(1)} custom-call(s32[18]{0:T(128)S(1)} %pad_add_fusion.info_ref, bf16[8,16,32,128]{3,2,1,0:T(8,128)(2,1)S(1)} %all-to-all-done.ref.refs_0_, bf16[8,8,32,128]{3,2,1,0:T(8,128)(2,1)S(1)} %collective-permute-done.refs_0_.refs_1_, bf16[8,8,32,128]{3,2,1,0:T(8,128)(2,1)} %collective-permute-done.1.refs_1_.refs_2_, ...), custom_call_target="tpu_custom_call" | custom-call | flops 1509949440 | bytes 8388608 | tf_op jit(solution)/shard_map/attend/pallas_call | solution.py:298
  158.9 27.5 %all_to_all.15.in_ref = bf16[8,3,4,32,128]{4,3,2,1,0:T(8,128)(2,1)S(1)} all-to-all(bf16[8,3,4,32,128]{4,3,2,1,0:T(8,128)(2,1)S(1)} %attend.3), channel_id=1, replica_groups=mesh['ta'=8,'ha'=8,'hd'=8] {'hd'}, dimensions={0} | all-to-all | bytes 1572864 | tf_op jit(solution)/shard_map/all_to_all | solution.py:355
  (47 shorter events, 26.9 us)
Async XLA Ops:
  2.8 44.8 %all-to-all-start = ((bf16[8,16,32,128]{3,2,1,0:T(8,128)(2,1)}), bf16[8,16,32,128]{3,2,1,0:T(8,128)(2,1)S(1)}, u32[]{:S(2)}, u32[]{:S(2)}) async-start(bf16[8,16,32,128]{3,2,1,0:T(8,128)(2,1)} %shard_map.64), calls=%async_computation | async-start | bytes 2097152 | tf_op jit(solution)/shard_map/all_to_all | solution.py:355
  12.1 18.0 %collective-permute-start.13 = (bf16[8,4,32,128]{3,2,1,0:T(8,128)(2,1)}, bf16[8,4,32,128]{3,2,1,0:T(8,128)(2,1)S(1)}, u32[]{:S(2)}, u32[]{:S(2)}) collective-permute-start(bf16[8,4,32,128]{3,2,1,0:T(8,128)(2,1)} %get-tuple-element.39), channel_id=1, source_target_pairs={{0,64},{64,128},{128,192},{192,256},{256,320},{320,384},{384,448},... | collective-permute-start | bytes 786440 | tf_op jit(solution)/shard_map/ppermute | solution.py:351
  21.9 22.8 %collective-permute-start.14 = (bf16[8,4,32,128]{3,2,1,0:T(8,128)(2,1)}, bf16[8,4,32,128]{3,2,1,0:T(8,128)(2,1)S(1)}, u32[]{:S(2)}, u32[]{:S(2)}) collective-permute-start(bf16[8,4,32,128]{3,2,1,0:T(8,128)(2,1)} %get-tuple-element.40), channel_id=1, source_target_pairs={{64,0},{128,64},{192,128},{256,192},{320,256},{384,320},{448,384},... | collective-permute-start | bytes 786440 | tf_op jit(solution)/shard_map/ppermute | solution.py:351
  30.1 14.6 %copy-start.4 = (bf16[8,4,32,128]{3,2,1,0:T(8,128)(2,1)}, bf16[8,4,32,128]{3,2,1,0:T(8,128)(2,1)S(1)}, u32[]{:S(2)}) copy-start(bf16[8,4,32,128]{3,2,1,0:T(8,128)(2,1)S(1)} %collective-permute-done.13.t0_ref) | copy-start | bytes 786436
  47.6 35.6 %all-to-all-start.1 = ((bf16[8,16,32,128]{3,2,1,0:T(8,128)(2,1)}), bf16[8,16,32,128]{3,2,1,0:T(8,128)(2,1)S(1)}, u32[]{:S(2)}, u32[]{:S(2)}) async-start(bf16[8,16,32,128]{3,2,1,0:T(8,128)(2,1)} %shard_map.70), calls=%async_computation.1 | async-start | bytes 2097152 | tf_op jit(solution)/shard_map/all_to_all | solution.py:355
  55.0 64.7 %collective-permute-start = (bf16[8,8,32,128]{3,2,1,0:T(8,128)(2,1)}, bf16[8,8,32,128]{3,2,1,0:T(8,128)(2,1)S(1)}, u32[]{:S(2)}, u32[]{:S(2)}) collective-permute-start(bf16[8,8,32,128]{3,2,1,0:T(8,128)(2,1)} %get-tuple-element.24), channel_id=1, source_target_pairs={{0,64},{64,128},{128,192},{192,256},{256,320},{320,384},{384,448},... | collective-permute-start | bytes 1572872 | tf_op jit(solution)/shard_map/ppermute | solution.py:351
  62.9 59.7 %collective-permute-start.1 = (bf16[8,8,32,128]{3,2,1,0:T(8,128)(2,1)}, bf16[8,8,32,128]{3,2,1,0:T(8,128)(2,1)}, u32[]{:S(2)}, u32[]{:S(2)}) collective-permute-start(bf16[8,8,32,128]{3,2,1,0:T(8,128)(2,1)} %get-tuple-element.25), channel_id=1, source_target_pairs={{64,0},{128,64},{192,128},{256,192},{320,256},{384,320},{448,384},... | collective-permute-start | bytes 1572872 | tf_op jit(solution)/shard_map/ppermute | solution.py:351
  85.8 54.4 %copy-start.6 = (s32[3,3]{1,0:T(4,128)S(1)}, s32[3,3]{1,0:T(4,128)}, u32[]{:S(2)}) copy-start(s32[3,3]{1,0:T(4,128)} %param.9) | copy-start | bytes 112
  85.8 54.5 %copy-start.7 = (s32[16]{0:T(128)S(1)}, s32[16]{0:T(128)}, u32[]{:S(2)}) copy-start(s32[16]{0:T(128)} %param.11) | copy-start | bytes 196
  85.8 54.5 %copy-start.8 = (s32[16]{0:T(128)S(1)}, s32[16]{0:T(128)}, u32[]{:S(2)}) copy-start(s32[16]{0:T(128)} %param.10) | copy-start | bytes 196
  85.8 52.4 %collective-permute-start.15 = (bf16[8,16,16,128]{3,2,1,0:T(8,128)(2,1)}, bf16[8,16,16,128]{3,2,1,0:T(8,128)(2,1)}, u32[]{:S(2)}, u32[]{:S(2)}) collective-permute-start(bf16[8,16,16,128]{3,2,1,0:T(8,128)(2,1)} %get-tuple-element.41), channel_id=1, source_target_pairs={{0,8},{8,16},{16,24},{24,32},{32,40},{40,48},{48,56},{1,9},{9,17},... | collective-permute-start | bytes 1572872 | tf_op jit(solution)/shard_map/ppermute | solution.py:351
  93.1 47.4 %copy-start.1 = (bf16[8,16,32,128]{3,2,1,0:T(8,128)(2,1)S(1)}, bf16[8,16,32,128]{3,2,1,0:T(8,128)(2,1)}, u32[]{:S(2)}) copy-start(bf16[8,16,32,128]{3,2,1,0:T(8,128)(2,1)} %copy-done) | copy-start | bytes 3145732
  93.1 9.3 %collective-permute-start.6 = (bf16[12,32,128]{2,1,0:T(8,128)(2,1)}, bf16[12,32,128]{2,1,0:T(8,128)(2,1)S(1)}, u32[]{:S(2)}, u32[]{:S(2)}) collective-permute-start(bf16[12,32,128]{2,1,0:T(8,128)(2,1)} %get-tuple-element.31), channel_id=1, source_target_pairs={{0,1},{1,2},{2,3},{3,4},{4,5},{5,6},{6,7},{7,0},{8,9},{9,10},{10,1... | collective-permute-start | bytes 294920 | tf_op jit(solution)/shard_map/ppermute | solution.py:390
  95.4 9.6 %collective-permute-start.7 = (bf16[12,32,128]{2,1,0:T(8,128)(2,1)}, bf16[12,32,128]{2,1,0:T(8,128)(2,1)S(1)}, u32[]{:S(2)}, u32[]{:S(2)}) collective-permute-start(bf16[12,32,128]{2,1,0:T(8,128)(2,1)} %get-tuple-element.32), channel_id=1, source_target_pairs={{0,2},{1,3},{2,4},{3,5},{4,6},{5,7},{6,0},{7,1},{8,10},{9,11},{10,... | collective-permute-start | bytes 294920 | tf_op jit(solution)/shard_map/ppermute | solution.py:390
  102.4 8.9 %collective-permute-start.8 = (bf16[12,32,128]{2,1,0:T(8,128)(2,1)}, bf16[12,32,128]{2,1,0:T(8,128)(2,1)S(1)}, u32[]{:S(2)}, u32[]{:S(2)}) collective-permute-start(bf16[12,32,128]{2,1,0:T(8,128)(2,1)} %get-tuple-element.33), channel_id=1, source_target_pairs={{0,3},{1,4},{2,5},{3,6},{4,7},{5,0},{6,1},{7,2},{8,11},{9,12},{10,... | collective-permute-start | bytes 294920 | tf_op jit(solution)/shard_map/ppermute | solution.py:390
  105.0 12.4 %collective-permute-start.9 = (bf16[12,32,128]{2,1,0:T(8,128)(2,1)}, bf16[12,32,128]{2,1,0:T(8,128)(2,1)S(1)}, u32[]{:S(2)}, u32[]{:S(2)}) collective-permute-start(bf16[12,32,128]{2,1,0:T(8,128)(2,1)} %get-tuple-element.34), channel_id=1, source_target_pairs={{0,4},{1,5},{2,6},{3,7},{4,0},{5,1},{6,2},{7,3},{8,12},{9,13},{10,... | collective-permute-start | bytes 294920 | tf_op jit(solution)/shard_map/ppermute | solution.py:390
  111.3 16.5 %collective-permute-start.10 = (bf16[12,32,128]{2,1,0:T(8,128)(2,1)}, bf16[12,32,128]{2,1,0:T(8,128)(2,1)S(1)}, u32[]{:S(2)}, u32[]{:S(2)}) collective-permute-start(bf16[12,32,128]{2,1,0:T(8,128)(2,1)} %get-tuple-element.35), channel_id=1, source_target_pairs={{0,5},{1,6},{2,7},{3,0},{4,1},{5,2},{6,3},{7,4},{8,13},{9,14},{10,... | collective-permute-start | bytes 294920 | tf_op jit(solution)/shard_map/ppermute | solution.py:390
  117.4 15.3 %collective-permute-start.11 = (bf16[12,32,128]{2,1,0:T(8,128)(2,1)}, bf16[12,32,128]{2,1,0:T(8,128)(2,1)S(1)}, u32[]{:S(2)}, u32[]{:S(2)}) collective-permute-start(bf16[12,32,128]{2,1,0:T(8,128)(2,1)} %get-tuple-element.36), channel_id=1, source_target_pairs={{0,6},{1,7},{2,0},{3,1},{4,2},{5,3},{6,4},{7,5},{8,14},{9,15},{10,... | collective-permute-start | bytes 294920 | tf_op jit(solution)/shard_map/ppermute | solution.py:390
  119.7 14.9 %collective-permute-start.12 = (bf16[12,32,128]{2,1,0:T(8,128)(2,1)}, bf16[12,32,128]{2,1,0:T(8,128)(2,1)S(1)}, u32[]{:S(2)}, u32[]{:S(2)}) collective-permute-start(bf16[12,32,128]{2,1,0:T(8,128)(2,1)} %get-tuple-element.37), channel_id=1, source_target_pairs={{0,7},{1,0},{2,1},{3,2},{4,3},{5,4},{6,5},{7,6},{8,15},{9,8},{10,9... | collective-permute-start | bytes 294920 | tf_op jit(solution)/shard_map/ppermute | solution.py:390
  122.6 17.8 %collective-permute-start.16 = (bf16[8,16,16,128]{3,2,1,0:T(8,128)(2,1)}, bf16[8,16,16,128]{3,2,1,0:T(8,128)(2,1)}, u32[]{:S(2)}, u32[]{:S(2)}) collective-permute-start(bf16[8,16,16,128]{3,2,1,0:T(8,128)(2,1)} %copy-done.3), channel_id=1, source_target_pairs={{8,0},{16,8},{24,16},{32,24},{40,32},{48,40},{56,48},{9,1},{17,9},... | collective-permute-start | bytes 1572872 | tf_op jit(solution)/shard_map/ppermute | solution.py:351
  127.8 18.1 %collective-permute-start.2 = (bf16[8,16,16,128]{3,2,1,0:T(8,128)(2,1)}, bf16[8,16,16,128]{3,2,1,0:T(8,128)(2,1)}, u32[]{:S(2)}, u32[]{:S(2)}) collective-permute-start(bf16[8,16,16,128]{3,2,1,0:T(8,128)(2,1)} %get-tuple-element.26), channel_id=1, source_target_pairs={{0,8},{8,16},{16,24},{24,32},{32,40},{40,48},{48,56},{1,9},{9,17},... | collective-permute-start | bytes 1572872 | tf_op jit(solution)/shard_map/ppermute | solution.py:351
  132.6 13.3 %collective-permute-start.3 = (bf16[8,16,16,128]{3,2,1,0:T(8,128)(2,1)}, bf16[8,16,16,128]{3,2,1,0:T(8,128)(2,1)}, u32[]{:S(2)}, u32[]{:S(2)}) collective-permute-start(bf16[8,16,16,128]{3,2,1,0:T(8,128)(2,1)} %get-tuple-element.27), channel_id=1, source_target_pairs={{8,0},{16,8},{24,16},{32,24},{40,32},{48,40},{56,48},{9,1},{17,9},... | collective-permute-start | bytes 1572872 | tf_op jit(solution)/shard_map/ppermute | solution.py:351
  134.6 11.3 %collective-permute-start.4 = (bf16[8,16,16,128]{3,2,1,0:T(8,128)(2,1)}, bf16[8,16,16,128]{3,2,1,0:T(8,128)(2,1)}, u32[]{:S(2)}, u32[]{:S(2)}) collective-permute-start(bf16[8,16,16,128]{3,2,1,0:T(8,128)(2,1)} %get-tuple-element.28), channel_id=1, source_target_pairs={{0,8},{8,16},{16,24},{24,32},{32,40},{40,48},{48,56},{1,9},{9,17},... | collective-permute-start | bytes 1572872 | tf_op jit(solution)/shard_map/ppermute | solution.py:351
  138.2 10.8 %collective-permute-start.5 = (bf16[8,16,16,128]{3,2,1,0:T(8,128)(2,1)}, bf16[8,16,16,128]{3,2,1,0:T(8,128)(2,1)}, u32[]{:S(2)}, u32[]{:S(2)}) collective-permute-start(bf16[8,16,16,128]{3,2,1,0:T(8,128)(2,1)} %get-tuple-element.29), channel_id=1, source_target_pairs={{8,0},{16,8},{24,16},{32,24},{40,32},{48,40},{56,48},{9,1},{17,9},... | collective-permute-start | bytes 1572872 | tf_op jit(solution)/shard_map/ppermute | solution.py:351
  (4 other events, 3.4 us)

commit v6 on v4

--- a/solution.py
+++ b/solution.py
@@ -80,20 +80,21 @@
     return packed if tiles else packed[0]
 
 
-def join_kernel(frames, c_ref, t0_ref, t1_ref, out_ref):
+def join_kernel(frames, c_ref, t0_ref, t1_ref, q_ref, out_ref):
     long = frames + 2 * TT
     for kv in range(2):
         at = kv * long
         out_ref[:, at : at + TT] = t0_ref[:, kv * TT : (kv + 1) * TT]
         out_ref[:, at + TT : at + TT + frames] = c_ref[:, kv * frames : (kv + 1) * frames]
         out_ref[:, at + TT + frames : at + long] = t1_ref[:, kv * TT : (kv + 1) * TT]
-
-
-def join(center, t0, t1):
+    out_ref[:, 2 * long :] = q_ref[...]
+
+
+def join(center, t0, t1, queries):
     groups, slabs, own, head_dim = center.shape
     frames = slabs // 2
-    total = 2 * (frames + 2 * TT)
-    arrays = (center, t0, t1)
+    total = 2 * (frames + 2 * TT) + queries.shape[1]
+    arrays = (center, t0, t1, queries)
     out = (groups, total, own, head_dim)
     return one_step(
         functools.partial(join_kernel, frames),
@@ -105,18 +106,18 @@
 
 
 def tiles_kernel(frames, ref, first_ref, last_ref):
-    for n in range(ref.shape[1] // frames):
+    for n in range(first_ref.shape[1] // TT):
         to = slice(n * TT, (n + 1) * TT)
         first_ref[:, to] = ref[:, n * frames : n * frames + TT]
         last_ref[:, to] = ref[:, (n + 1) * frames - TT : (n + 1) * frames]
 
 
-def tiles_of(value, frames):
-    groups, slabs, own, head_dim = value.shape
+def tiles_of(value, slabs, frames):
+    groups, _, own, head_dim = value.shape
     out = (groups, slabs // frames * TT, own, head_dim)
     return one_step(
         functools.partial(tiles_kernel, frames),
-        [whole(value.shape)],
+        [whole((groups, slabs, own, head_dim))],
         [out, out],
         8 * math.prod(out),
     )(value)
@@ -237,7 +238,7 @@
             pl.when((rad_t == far_t) & (rad_h == far_h))(functools.partial(over, far_t, far_h))
 
 
-def attend(info, pieces, queries, heads, head, slot, before, frames):
+def attend(info, pieces, queries, q_block, heads, head, slot, before, frames):
     groups, _, own, head_dim = queries.shape
     span = max(groups // 2, 1)
     reach = min(span + 1, groups)
@@ -254,7 +255,7 @@
         for a, spans, _ in pieces
     ]
     in_specs += [
-        pl.BlockSpec((groups, frames, own, head_dim), lambda h: (0, head + h, 0, 0)),
+        pl.BlockSpec((groups, frames, own, head_dim), lambda h: (0, q_block + h, 0, 0)),
     ]
     args = [info, *(a for a, _, _ in pieces), queries]
     total = slot + heads
@@ -345,13 +346,14 @@
     value_z, first_z, last_z = packed([(1, rest), (2, rest)], True)
     tz0 = shifted(last_z, "ta", 1)
     tz1 = shifted(first_z, "ta", -1)
-    value_n = packed([(part, head) for head in range(rest) for part in (1, 2)])
+    entries_n = [(part, head) for head in range(rest) for part in (1, 2)]
+    value_n = packed([*entries_n, (0, rest)])
     got_n = exchange(value_n)
-    got_q = exchange(packed([(0, head) for head in range(heads)]))
-    joined = join(value_z, tz0, tz1)
+    value_q = packed([(0, head) for head in range(rest)])
+    joined = join(value_z, tz0, tz1, value_q)
     got_z = exchange(joined)
 
-    first_n, last_n = tiles_of(got_n, frames)
+    first_n, last_n = tiles_of(got_n, 2 * rest * frames, frames)
     tn0 = shifted(last_n, "ta", 1)
     tn1 = shifted(first_n, "ta", -1)
     low_c, high_c = rim((got_n,), (frames,), 2 * rest, edge)
@@ -376,8 +378,8 @@
         (ht1, beside, edge + own),
     )
     pieces_z = ((got_z, every, edge), (hz0, every, 0), (hz1, every, edge + own))
-    out = attend(info, pieces_z, got_q, 1, rest, 0, None, frames)
-    out = attend(info, pieces_n, got_q, rest, 0, 1, out, frames)
+    out = attend(info, pieces_z, got_n, 2 * rest, 1, rest, 0, None, frames)
+    out = attend(info, pieces_n, got_z, 2 * long // frames, rest, 0, 1, out, frames)
     return unpack(exchange(out), (rest, *range(rest)), rows, cols)
 
 

time: 197 us -> 169 us (0.86)
  the two profiles are of different devices: /device:TPU:64 before, /device:TPU:67 now
where the time goes in v6:
time: 169 us; the launch traced here: 168 us
  starting transfers between devices  52.8 us (31%)
  waiting for transfers between devices  50.8 us (30%)
  Pallas kernels  31.6 us (19%)
  blocking collectives  29.8 us (18%)
  local copies, waits for them, and re-layouts  2.71 us (2%)
    ppermute x10, starting transfers between devices, shifted(): return lax.ppermute(value, axis, pairs)  39.6 us
    all_to_all x1, blocking collectives, exchange(): return lax.all_to_all(value, 'hd', split_axis=0, concat_axis=0, tiled=True)  29.8 us
    all_to_all x2, waiting for transfers between devices, exchange(): return lax.all_to_all(value, 'hd', split_axis=0, concat_axis=0, tiled=True)  29.3 us
    ppermute x10, waiting for transfers between devices, shifted(): return lax.ppermute(value, axis, pairs)  21.4 us
    pallas_call x2, Pallas kernels, attend(): pl.pallas_call(functools.partial(attend_kernel, tuple(((spans, low) for _...  14.5 us
    all_to_all x2, starting transfers between devices, exchange(): return lax.all_to_all(value, 'hd', split_axis=0, concat_axis=0, tiled=True)  13.2 us
    pallas_call x3, Pallas kernels, pack(): one_step(kernel, in_specs, outs, 4 * math.prod(outs[0]), PACK_GRANT)  8.12 us
    pallas_call x3, Pallas kernels, rim(): one_step(functools.partial(rim_kernel, edge, counts), in_specs, [out, out...  4.22 us
  transfers between devices with their start and end apart: 12, of which 4 were waited for; matrix products, arithmetic and copies ran while one was open for 0% of the time, Pallas kernels for 10%

profile of v6, /device:TPU:67, one launch (start us, length us, event | category | flops | bytes accessed | tf_op | source)
XLA Modules:
  0.0 167.9 jit_solution(179346740814898187)
XLA Ops:
  0.0 3.2 %shard_map.64 = bf16[8,20,32,128]{3,2,1,0:T(8,128)(2,1)} custom-call(bf16[4,4,8,9216]{3,2,1,0:T(8,128)(2,1)} %refs_0_.5, bf16[4,4,8,9216]{3,2,1,0:T(8,128)(2,1)} %refs_0_.5, bf16[4,4,8,9216]{3,2,1,0:T(8,128)(2,1)} %refs_0_.5, f32[1,128]{1,0:T(1,128)} %bitcast.2, f32[1,128]{1,0:T(1,128)} %bitcast.5), custom_call_target="tpu_custom_call" | custom-call | flops 2621440 | bytes 2621440 | tf_op jit(solution)/shard_map/pallas_call | solution.py:77
  3.2 6.8 %all-to-all-start = ((bf16[8,20,32,128]{3,2,1,0:T(8,128)(2,1)}), bf16[8,20,32,128]{3,2,1,0:T(8,128)(2,1)S(1)}, u32[]{:S(2)}, u32[]{:S(2)}) async-start(bf16[8,20,32,128]{3,2,1,0:T(8,128)(2,1)} %shard_map.64), calls=%async_computation | async-start | bytes 2621440 | tf_op jit(solution)/shard_map/all_to_all | solution.py:321
  10.1 2.6 %shard_map.68 = (bf16[8,8,32,128]{3,2,1,0:T(8,128)(2,1)}, bf16[8,4,32,128]{3,2,1,0:T(8,128)(2,1)}, bf16[8,4,32,128]{3,2,1,0:T(8,128)(2,1)}) custom-call(bf16[4,4,8,9216]{3,2,1,0:T(8,128)(2,1)} %refs_0_.5, bf16[4,4,8,9216]{3,2,1,0:T(8,128)(2,1)} %refs_0_.5, f32[1,128]{1,0:T(1,128)} %bitcast.3, f32[1,128]{1,0:T(1,128)} %bitcast.6), custom_call_target="tpu_custom_call" | custom-call | flops 1048576 | bytes 1048576 | tf_op jit(solution)/shard_map/pallas_call | solution.py:77
  12.6 9.7 %collective-permute-start.6 = (bf16[8,4,32,128]{3,2,1,0:T(8,128)(2,1)}, bf16[8,4,32,128]{3,2,1,0:T(8,128)(2,1)S(1)}, u32[]{:S(2)}, u32[]{:S(2)}) collective-permute-start(bf16[8,4,32,128]{3,2,1,0:T(8,128)(2,1)} %get-tuple-element.23), channel_id=1, source_target_pairs={{0,64},{64,128},{128,192},{192,256},{256,320},{320,384},{384,448},... | collective-permute-start | bytes 786440 | tf_op jit(solution)/shard_map/ppermute | solution.py:317
  22.4 1.9 %collective-permute-start.7 = (bf16[8,4,32,128]{3,2,1,0:T(8,128)(2,1)}, bf16[8,4,32,128]{3,2,1,0:T(8,128)(2,1)S(1)}, u32[]{:S(2)}, u32[]{:S(2)}) collective-permute-start(bf16[8,4,32,128]{3,2,1,0:T(8,128)(2,1)} %get-tuple-element.24), channel_id=1, source_target_pairs={{64,0},{128,64},{192,128},{256,192},{320,256},{384,320},{448,384},... | collective-permute-start | bytes 786440 | tf_op jit(solution)/shard_map/ppermute | solution.py:317
  24.3 2.3 %shard_map.69.q_ref = bf16[8,8,32,128]{3,2,1,0:T(8,128)(2,1)} custom-call(bf16[4,4,8,9216]{3,2,1,0:T(8,128)(2,1)} %refs_0_.5, f32[1,128]{1,0:T(1,128)} %bitcast.4, f32[1,128]{1,0:T(1,128)} %bitcast.7), custom_call_target="tpu_custom_call" | custom-call | flops 1048576 | bytes 1048576 | tf_op jit(solution)/shard_map/pallas_call | solution.py:77
  26.6 7.9 %collective-permute-done.6.t0_ref = bf16[8,4,32,128]{3,2,1,0:T(8,128)(2,1)S(1)} collective-permute-done((bf16[8,4,32,128]{3,2,1,0:T(8,128)(2,1)}, bf16[8,4,32,128]{3,2,1,0:T(8,128)(2,1)S(1)}, u32[]{:S(2)}, u32[]{:S(2)}) %collective-permute-start.6) | collective-permute-done | bytes 262176 | tf_op jit(solution)/shard_map/ppermute | solution.py:317
  34.5 10.6 %collective-permute-done.7.t1_ref = bf16[8,4,32,128]{3,2,1,0:T(8,128)(2,1)S(1)} collective-permute-done((bf16[8,4,32,128]{3,2,1,0:T(8,128)(2,1)}, bf16[8,4,32,128]{3,2,1,0:T(8,128)(2,1)S(1)}, u32[]{:S(2)}, u32[]{:S(2)}) %collective-permute-start.7) | collective-permute-done | bytes 262176 | tf_op jit(solution)/shard_map/ppermute | solution.py:317
  45.8 2.6 %shard_map.70 = bf16[8,24,32,128]{3,2,1,0:T(8,128)(2,1)} custom-call(bf16[8,8,32,128]{3,2,1,0:T(8,128)(2,1)} %get-tuple-element.22.c_ref, bf16[8,4,32,128]{3,2,1,0:T(8,128)(2,1)} %copy-done.2, bf16[8,4,32,128]{3,2,1,0:T(8,128)(2,1)} %copy-done.3, bf16[8,8,32,128]{3,2,1,0:T(8,128)(2,1)} %shard_map.69.q_ref), custom_call_target="tpu_custom_call" | custom-call | flops 3145728 | bytes 3145728 | tf_op jit(solution)/shard_map/pallas_call | solution.py:99
  48.4 6.4 %all-to-all-start.1 = ((bf16[8,24,32,128]{3,2,1,0:T(8,128)(2,1)}), bf16[8,24,32,128]{3,2,1,0:T(8,128)(2,1)}, u32[]{:S(2)}, u32[]{:S(2)}) async-start(bf16[8,24,32,128]{3,2,1,0:T(8,128)(2,1)} %shard_map.70), calls=%async_computation.1 | async-start | bytes 3145728 | tf_op jit(solution)/shard_map/all_to_all | solution.py:321
  55.9 7.8 %collective-permute-start = (bf16[8,8,32,128]{3,2,1,0:T(8,128)(2,1)}, bf16[8,8,32,128]{3,2,1,0:T(8,128)(2,1)S(1)}, u32[]{:S(2)}, u32[]{:S(2)}) collective-permute-start(bf16[8,8,32,128]{3,2,1,0:T(8,128)(2,1)} %get-tuple-element.16), channel_id=1, source_target_pairs={{0,64},{64,128},{128,192},{192,256},{256,320},{320,384},{384,448},... | collective-permute-start | bytes 1572872 | tf_op jit(solution)/shard_map/ppermute | solution.py:317
  63.7 2.3 %collective-permute-start.1 = (bf16[8,8,32,128]{3,2,1,0:T(8,128)(2,1)}, bf16[8,8,32,128]{3,2,1,0:T(8,128)(2,1)S(1)}, u32[]{:S(2)}, u32[]{:S(2)}) collective-permute-start(bf16[8,8,32,128]{3,2,1,0:T(8,128)(2,1)} %get-tuple-element.17), channel_id=1, source_target_pairs={{64,0},{128,64},{192,128},{256,192},{320,256},{384,320},{448,384},... | collective-permute-start | bytes 1572872 | tf_op jit(solution)/shard_map/ppermute | solution.py:317
  66.0 29.3 %all-to-all-done.1.refs_0_.refs_7_ = bf16[8,24,32,128]{3,2,1,0:T(8,128)(2,1)} async-done(((bf16[8,24,32,128]{3,2,1,0:T(8,128)(2,1)}), bf16[8,24,32,128]{3,2,1,0:T(8,128)(2,1)}, u32[]{:S(2)}, u32[]{:S(2)}) %all-to-all-start.1) | async-done | bytes 1572896 | tf_op jit(solution)/shard_map/all_to_all | solution.py:321
  95.3 2.1 %shard_map.71 = (bf16[8,16,16,128]{3,2,1,0:T(8,128)(2,1)}, bf16[8,16,16,128]{3,2,1,0:T(8,128)(2,1)S(1)}) custom-call(bf16[8,24,32,128]{3,2,1,0:T(8,128)(2,1)} %all-to-all-done.1.refs_0_.refs_7_), custom_call_target="tpu_custom_call" | custom-call | flops 2097152 | bytes 2097152 | tf_op jit(solution)/shard_map/pallas_call | solution.py:144
  97.4 4.9 %collective-permute-start.8 = (bf16[8,16,16,128]{3,2,1,0:T(8,128)(2,1)S(1)}, bf16[8,16,16,128]{3,2,1,0:T(8,128)(2,1)S(1)}, u32[]{:S(2)}, u32[]{:S(2)}) collective-permute-start(bf16[8,16,16,128]{3,2,1,0:T(8,128)(2,1)S(1)} %get-tuple-element.25), channel_id=1, source_target_pairs={{0,8},{8,16},{16,24},{24,32},{32,40},{40,48},{48,56},{1,9},{9,17},... | collective-permute-start | bytes 1572872 | tf_op jit(solution)/shard_map/ppermute | solution.py:317
  102.3 1.9 %collective-permute-start.9 = (bf16[8,16,16,128]{3,2,1,0:T(8,128)(2,1)}, bf16[8,16,16,128]{3,2,1,0:T(8,128)(2,1)}, u32[]{:S(2)}, u32[]{:S(2)}) collective-permute-start(bf16[8,16,16,128]{3,2,1,0:T(8,128)(2,1)} %get-tuple-element.26), channel_id=1, source_target_pairs={{8,0},{16,8},{24,16},{32,24},{40,32},{48,40},{56,48},{9,1},{17,9},... | collective-permute-start | bytes 1572872 | tf_op jit(solution)/shard_map/ppermute | solution.py:317
  105.4 3.6 %collective-permute-start.2 = (bf16[8,16,16,128]{3,2,1,0:T(8,128)(2,1)}, bf16[8,16,16,128]{3,2,1,0:T(8,128)(2,1)S(1)}, u32[]{:S(2)}, u32[]{:S(2)}) collective-permute-start(bf16[8,16,16,128]{3,2,1,0:T(8,128)(2,1)} %get-tuple-element.18), channel_id=1, source_target_pairs={{0,8},{8,16},{16,24},{24,32},{32,40},{40,48},{48,56},{1,9},{9,17},... | collective-permute-start | bytes 1572872 | tf_op jit(solution)/shard_map/ppermute | solution.py:317
  109.0 1.9 %collective-permute-start.3 = (bf16[8,16,16,128]{3,2,1,0:T(8,128)(2,1)}, bf16[8,16,16,128]{3,2,1,0:T(8,128)(2,1)}, u32[]{:S(2)}, u32[]{:S(2)}) collective-permute-start(bf16[8,16,16,128]{3,2,1,0:T(8,128)(2,1)} %get-tuple-element.19), channel_id=1, source_target_pairs={{8,0},{16,8},{24,16},{32,24},{40,32},{48,40},{56,48},{9,1},{17,9},... | collective-permute-start | bytes 1572872 | tf_op jit(solution)/shard_map/ppermute | solution.py:317
  112.0 3.6 %collective-permute-start.4 = (bf16[8,16,16,128]{3,2,1,0:T(8,128)(2,1)}, bf16[8,16,16,128]{3,2,1,0:T(8,128)(2,1)}, u32[]{:S(2)}, u32[]{:S(2)}) collective-permute-start(bf16[8,16,16,128]{3,2,1,0:T(8,128)(2,1)} %get-tuple-element.20), channel_id=1, source_target_pairs={{0,8},{8,16},{16,24},{24,32},{32,40},{40,48},{48,56},{1,9},{9,17},... | collective-permute-start | bytes 1572872 | tf_op jit(solution)/shard_map/ppermute | solution.py:317
  116.4 1.9 %collective-permute-start.5 = (bf16[8,16,16,128]{3,2,1,0:T(8,128)(2,1)}, bf16[8,16,16,128]{3,2,1,0:T(8,128)(2,1)}, u32[]{:S(2)}, u32[]{:S(2)}) collective-permute-start(bf16[8,16,16,128]{3,2,1,0:T(8,128)(2,1)} %get-tuple-element.21), channel_id=1, source_target_pairs={{8,0},{16,8},{24,16},{32,24},{40,32},{48,40},{56,48},{9,1},{17,9},... | collective-permute-start | bytes 1572872 | tf_op jit(solution)/shard_map/ppermute | solution.py:317
  119.7 4.7 %attend.2.refs_8_ = bf16[8,1,4,32,128]{4,3,2,1,0:T(8,128)(2,1)S(1)} custom-call(s32[17]{0:T(128)S(1)} %pad_add_fusion.info_ref, bf16[8,24,32,128]{3,2,1,0:T(8,128)(2,1)} %all-to-all-done.1.refs_0_.refs_7_, bf16[8,16,16,128]{3,2,1,0:T(8,128)(2,1)S(1)} %copy-done.1, bf16[8,16,16,128]{3,2,1,0:T(8,128)(2,1)} %collective-permute-done.9.refs_2_, ...), custom_call_target="tpu_custom_call" | custom-call | flops 754974720 | bytes 4194304 | tf_op jit(solution)/shard_map/attend/pallas_call | solution.py:265
  124.4 2.9 %collective-permute-done.5.refs_6_ = bf16[8,16,16,128]{3,2,1,0:T(8,128)(2,1)} collective-permute-done((bf16[8,16,16,128]{3,2,1,0:T(8,128)(2,1)}, bf16[8,16,16,128]{3,2,1,0:T(8,128)(2,1)}, u32[]{:S(2)}, u32[]{:S(2)}) %collective-permute-start.5) | collective-permute-done | bytes 524320 | tf_op jit(solution)/shard_map/ppermute | solution.py:317
  127.2 9.8 %attend.3 = bf16[8,3,4,32,128]{4,3,2,1,0:T(8,128)(2,1)S(1)} custom-call(s32[17]{0:T(128)S(1)} %pad_add_fusion.info_ref, bf16[8,20,32,128]{3,2,1,0:T(8,128)(2,1)S(1)} %all-to-all-done.ref.refs_0_.refs_3_, bf16[8,8,32,128]{3,2,1,0:T(8,128)(2,1)S(1)} %collective-permute-done.refs_0_.refs_1_, bf16[8,8,32,128]{3,2,1,0:T(8,128)(2,1)S(1)} %collective-permute-done.1.refs_1_.refs_2_, ...), custom_call_target="tpu_custom_call" | custom-call | flops 1509949440 | bytes 8388608 | tf_op jit(solution)/shard_map/attend/pallas_call | solution.py:265
  137.1 29.8 %all_to_all.15.in_ref = bf16[8,3,4,32,128]{4,3,2,1,0:T(8,128)(2,1)S(1)} all-to-all(bf16[8,3,4,32,128]{4,3,2,1,0:T(8,128)(2,1)S(1)} %attend.3), channel_id=1, replica_groups=mesh['ta'=8,'ha'=8,'hd'=8] {'hd'}, dimensions={0} | all-to-all | bytes 1572864 | tf_op jit(solution)/shard_map/all_to_all | solution.py:321
  (29 shorter events, 7.2 us)
Async XLA Ops:
  3.2 45.2 %all-to-all-start = ((bf16[8,20,32,128]{3,2,1,0:T(8,128)(2,1)}), bf16[8,20,32,128]{3,2,1,0:T(8,128)(2,1)S(1)}, u32[]{:S(2)}, u32[]{:S(2)}) async-start(bf16[8,20,32,128]{3,2,1,0:T(8,128)(2,1)} %shard_map.64), calls=%async_computation | async-start | bytes 2621440 | tf_op jit(solution)/shard_map/all_to_all | solution.py:321
  12.6 21.9 %collective-permute-start.6 = (bf16[8,4,32,128]{3,2,1,0:T(8,128)(2,1)}, bf16[8,4,32,128]{3,2,1,0:T(8,128)(2,1)S(1)}, u32[]{:S(2)}, u32[]{:S(2)}) collective-permute-start(bf16[8,4,32,128]{3,2,1,0:T(8,128)(2,1)} %get-tuple-element.23), channel_id=1, source_target_pairs={{0,64},{64,128},{128,192},{192,256},{256,320},{320,384},{384,448},... | collective-permute-start | bytes 786440 | tf_op jit(solution)/shard_map/ppermute | solution.py:317
  22.4 22.8 %collective-permute-start.7 = (bf16[8,4,32,128]{3,2,1,0:T(8,128)(2,1)}, bf16[8,4,32,128]{3,2,1,0:T(8,128)(2,1)S(1)}, u32[]{:S(2)}, u32[]{:S(2)}) collective-permute-start(bf16[8,4,32,128]{3,2,1,0:T(8,128)(2,1)} %get-tuple-element.24), channel_id=1, source_target_pairs={{64,0},{128,64},{192,128},{256,192},{320,256},{384,320},{448,384},... | collective-permute-start | bytes 786440 | tf_op jit(solution)/shard_map/ppermute | solution.py:317
  34.5 10.6 %copy-start.2 = (bf16[8,4,32,128]{3,2,1,0:T(8,128)(2,1)}, bf16[8,4,32,128]{3,2,1,0:T(8,128)(2,1)S(1)}, u32[]{:S(2)}) copy-start(bf16[8,4,32,128]{3,2,1,0:T(8,128)(2,1)S(1)} %collective-permute-done.6.t0_ref) | copy-start | bytes 786436
  45.1 0.7 copy-start.3
  48.4 46.9 %all-to-all-start.1 = ((bf16[8,24,32,128]{3,2,1,0:T(8,128)(2,1)}), bf16[8,24,32,128]{3,2,1,0:T(8,128)(2,1)}, u32[]{:S(2)}, u32[]{:S(2)}) async-start(bf16[8,24,32,128]{3,2,1,0:T(8,128)(2,1)} %shard_map.70), calls=%async_computation.1 | async-start | bytes 3145728 | tf_op jit(solution)/shard_map/all_to_all | solution.py:321
  55.9 53.1 %collective-permute-start = (bf16[8,8,32,128]{3,2,1,0:T(8,128)(2,1)}, bf16[8,8,32,128]{3,2,1,0:T(8,128)(2,1)S(1)}, u32[]{:S(2)}, u32[]{:S(2)}) collective-permute-start(bf16[8,8,32,128]{3,2,1,0:T(8,128)(2,1)} %get-tuple-element.16), channel_id=1, source_target_pairs={{0,64},{64,128},{128,192},{192,256},{256,320},{320,384},{384,448},... | collective-permute-start | bytes 1572872 | tf_op jit(solution)/shard_map/ppermute | solution.py:317
  63.7 47.2 %collective-permute-start.1 = (bf16[8,8,32,128]{3,2,1,0:T(8,128)(2,1)}, bf16[8,8,32,128]{3,2,1,0:T(8,128)(2,1)S(1)}, u32[]{:S(2)}, u32[]{:S(2)}) collective-permute-start(bf16[8,8,32,128]{3,2,1,0:T(8,128)(2,1)} %get-tuple-element.17), channel_id=1, source_target_pairs={{64,0},{128,64},{192,128},{256,192},{320,256},{384,320},{448,384},... | collective-permute-start | bytes 1572872 | tf_op jit(solution)/shard_map/ppermute | solution.py:317
  97.4 21.0 %copy-start.4 = (s32[3,3]{1,0:T(4,128)S(1)}, s32[3,3]{1,0:T(4,128)}, u32[]{:S(2)}) copy-start(s32[3,3]{1,0:T(4,128)} %param.9) | copy-start | bytes 112
  97.4 21.1 %copy-start.5 = (s32[16]{0:T(128)S(1)}, s32[16]{0:T(128)}, u32[]{:S(2)}) copy-start(s32[16]{0:T(128)} %param.11) | copy-start | bytes 196
  97.4 21.1 %copy-start.6 = (s32[16]{0:T(128)S(1)}, s32[16]{0:T(128)}, u32[]{:S(2)}) copy-start(s32[16]{0:T(128)} %param.10) | copy-start | bytes 196
  97.4 18.2 %collective-permute-start.8 = (bf16[8,16,16,128]{3,2,1,0:T(8,128)(2,1)S(1)}, bf16[8,16,16,128]{3,2,1,0:T(8,128)(2,1)S(1)}, u32[]{:S(2)}, u32[]{:S(2)}) collective-permute-start(bf16[8,16,16,128]{3,2,1,0:T(8,128)(2,1)S(1)} %get-tuple-element.25), channel_id=1, source_target_pairs={{0,8},{8,16},{16,24},{24,32},{32,40},{40,48},{48,56},{1,9},{9,17},... | collective-permute-start | bytes 1572872 | tf_op jit(solution)/shard_map/ppermute | solution.py:317
  102.3 16.3 %collective-permute-start.9 = (bf16[8,16,16,128]{3,2,1,0:T(8,128)(2,1)}, bf16[8,16,16,128]{3,2,1,0:T(8,128)(2,1)}, u32[]{:S(2)}, u32[]{:S(2)}) collective-permute-start(bf16[8,16,16,128]{3,2,1,0:T(8,128)(2,1)} %get-tuple-element.26), channel_id=1, source_target_pairs={{8,0},{16,8},{24,16},{32,24},{40,32},{48,40},{56,48},{9,1},{17,9},... | collective-permute-start | bytes 1572872 | tf_op jit(solution)/shard_map/ppermute | solution.py:317
  105.4 19.0 %collective-permute-start.2 = (bf16[8,16,16,128]{3,2,1,0:T(8,128)(2,1)}, bf16[8,16,16,128]{3,2,1,0:T(8,128)(2,1)S(1)}, u32[]{:S(2)}, u32[]{:S(2)}) collective-permute-start(bf16[8,16,16,128]{3,2,1,0:T(8,128)(2,1)} %get-tuple-element.18), channel_id=1, source_target_pairs={{0,8},{8,16},{16,24},{24,32},{32,40},{40,48},{48,56},{1,9},{9,17},... | collective-permute-start | bytes 1572872 | tf_op jit(solution)/shard_map/ppermute | solution.py:317
  109.0 15.4 %collective-permute-start.3 = (bf16[8,16,16,128]{3,2,1,0:T(8,128)(2,1)}, bf16[8,16,16,128]{3,2,1,0:T(8,128)(2,1)}, u32[]{:S(2)}, u32[]{:S(2)}) collective-permute-start(bf16[8,16,16,128]{3,2,1,0:T(8,128)(2,1)} %get-tuple-element.19), channel_id=1, source_target_pairs={{8,0},{16,8},{24,16},{32,24},{40,32},{48,40},{56,48},{9,1},{17,9},... | collective-permute-start | bytes 1572872 | tf_op jit(solution)/shard_map/ppermute | solution.py:317
  112.0 12.4 %collective-permute-start.4 = (bf16[8,16,16,128]{3,2,1,0:T(8,128)(2,1)}, bf16[8,16,16,128]{3,2,1,0:T(8,128)(2,1)}, u32[]{:S(2)}, u32[]{:S(2)}) collective-permute-start(bf16[8,16,16,128]{3,2,1,0:T(8,128)(2,1)} %get-tuple-element.20), channel_id=1, source_target_pairs={{0,8},{8,16},{16,24},{24,32},{32,40},{40,48},{48,56},{1,9},{9,17},... | collective-permute-start | bytes 1572872 | tf_op jit(solution)/shard_map/ppermute | solution.py:317
  115.6 0.8 copy-start
  116.4 10.8 %collective-permute-start.5 = (bf16[8,16,16,128]{3,2,1,0:T(8,128)(2,1)}, bf16[8,16,16,128]{3,2,1,0:T(8,128)(2,1)}, u32[]{:S(2)}, u32[]{:S(2)}) collective-permute-start(bf16[8,16,16,128]{3,2,1,0:T(8,128)(2,1)} %get-tuple-element.21), channel_id=1, source_target_pairs={{8,0},{16,8},{24,16},{32,24},{40,32},{48,40},{56,48},{9,1},{17,9},... | collective-permute-start | bytes 1572872 | tf_op jit(solution)/shard_map/ppermute | solution.py:317
  118.6 1.0 copy-start.1

commit v7 on v4

--- a/solution.py
+++ b/solution.py
@@ -287,27 +287,30 @@
     )(*args)
 
 
-def unpack_kernel(order, in_ref, out_ref):
+def unpack_kernel(order, *refs):
+    out_ref = refs[-1]
     frames, rows, cols = out_ref.shape[:3]
-    groups, heads, _, _, head_dim = in_ref.shape
-    for slot, head in enumerate(order):
+    heads = len(order)
+    slots = [(ref, slot) for ref in refs[:-1] for slot in range(ref.shape[1])]
+    for (ref, slot), head in zip(slots, order):
+        groups, _, _, _, head_dim = ref.shape
         for group in range(groups):
             at = (heads * group + head) * head_dim
-            x = in_ref[group, slot].astype(jnp.float32).reshape(frames, rows, cols, head_dim)
+            x = ref[group, slot].astype(jnp.float32).reshape(frames, rows, cols, head_dim)
             out_ref[:, :, :, at : at + head_dim] = x.astype(jnp.bfloat16)
 
 
-def unpack(value, order, rows, cols):
-    groups, heads, frames, _, head_dim = value.shape
-    out = (frames, rows, cols, groups * heads * head_dim)
+def unpack(values, order, rows, cols):
+    groups, _, frames, _, head_dim = values[0].shape
+    out = (frames, rows, cols, groups * len(order) * head_dim)
     return pl.pallas_call(
         functools.partial(unpack_kernel, order),
-        in_specs=[pl.BlockSpec(memory_space=pltpu.VMEM)],
+        in_specs=[pl.BlockSpec(memory_space=pltpu.VMEM)] * len(values),
         out_specs=pl.BlockSpec(memory_space=pltpu.VMEM),
         out_shape=jax.ShapeDtypeStruct(out, jnp.bfloat16),
         compiler_params=pltpu.CompilerParams(vmem_limit_bytes=16 << 20),
         name="unpack",
-    )(value)
+    )(*values)
 
 
 def shifted(value, axis, step):
@@ -376,9 +379,10 @@
         (ht1, beside, edge + own),
     )
     pieces_z = ((got_z, every, edge), (hz0, every, 0), (hz1, every, edge + own))
-    out = attend(info, pieces_z, got_q, 1, rest, 0, None, frames)
-    out = attend(info, pieces_n, got_q, rest, 0, 1, out, frames)
-    return unpack(exchange(out), (rest, *range(rest)), rows, cols)
+    out_z = attend(info, pieces_z, got_q, 1, rest, 0, None, frames)
+    back_z = exchange(out_z)
+    out_n = attend(info, pieces_n, got_q, rest, 0, 0, None, frames)
+    return unpack((back_z, exchange(out_n)), (rest, *range(rest)), rows, cols)
 
 
 def solution(mesh):

time: 197 us -> 199 us (1.010)
  starting transfers between devices: 54.6 us -> 63.1 us
  blocking collectives: 31.7 us -> 24.5 us
    all_to_all x3 -> x4, starting transfers between devices: 17.6 us -> 26.1 us  [exchange(): return lax.all_to_all(value, 'hd', split_axis=0, concat_axis=0, tiled=True)]
    all_to_all x1, blocking collectives: 31.7 us -> 24.5 us  [exchange(): return lax.all_to_all(value, 'hd', split_axis=0, concat_axis=0, tiled=True)]
    all_to_all x3 -> x4, waiting for transfers between devices: 25.2 us -> 25.3 us  [exchange(): return lax.all_to_all(value, 'hd', split_axis=0, concat_axis=0, tiled=True)]
  transfers between devices with their start and end apart: 13 -> 14, of which waited for: 6 -> 6; matrix products, arithmetic and copies ran while one was open for 0% -> 0% of each run, Pallas kernels for 8% -> 14%
where the time goes in v7:
time: 199 us; the launch traced here: 198 us
  waiting for transfers between devices  76.1 us (38%)
  starting transfers between devices  63.1 us (32%)
  Pallas kernels  31.7 us (16%)
  blocking collectives  24.5 us (12%)
    ppermute x10, waiting for transfers between devices, shifted(): return lax.ppermute(value, axis, pairs)  50.8 us
    ppermute x10, starting transfers between devices, shifted(): return lax.ppermute(value, axis, pairs)  37 us
    all_to_all x4, starting transfers between devices, exchange(): return lax.all_to_all(value, 'hd', split_axis=0, concat_axis=0, tiled=True)  26.1 us
    all_to_all x4, waiting for transfers between devices, exchange(): return lax.all_to_all(value, 'hd', split_axis=0, concat_axis=0, tiled=True)  25.3 us
    all_to_all x1, blocking collectives, exchange(): return lax.all_to_all(value, 'hd', split_axis=0, concat_axis=0, tiled=True)  24.5 us
    pallas_call x2, Pallas kernels, attend(): pl.pallas_call(functools.partial(attend_kernel, tuple(((spans, low) for _...  15 us
    pallas_call x3, Pallas kernels, pack(): one_step(kernel, in_specs, outs, 4 * math.prod(outs[0]), PACK_GRANT)  7.87 us
    pallas_call x3, Pallas kernels, rim(): one_step(functools.partial(rim_kernel, edge, counts), in_specs, [out, out...  4.44 us
  transfers between devices with their start and end apart: 14, of which 6 were waited for; matrix products, arithmetic and copies ran while one was open for 0% of the time, Pallas kernels for 14%

profile of v7, /device:TPU:64, one launch (start us, length us, event | category | flops | bytes accessed | tf_op | source)
XLA Modules:
  0.0 197.7 jit_solution(4071457335413579946)
XLA Ops:
  0.0 2.8 %shard_map.68 = bf16[8,16,32,128]{3,2,1,0:T(8,128)(2,1)} custom-call(bf16[4,4,8,9216]{3,2,1,0:T(8,128)(2,1)} %refs_1_.3, bf16[4,4,8,9216]{3,2,1,0:T(8,128)(2,1)} %refs_1_.3, f32[1,128]{1,0:T(1,128)} %bitcast.2, f32[1,128]{1,0:T(1,128)} %bitcast.5), custom_call_target="tpu_custom_call" | custom-call | flops 2097152 | bytes 2097152 | tf_op jit(solution)/shard_map/pallas_call | solution.py:77
  2.8 7.1 %all-to-all-start.3 = ((bf16[8,16,32,128]{3,2,1,0:T(8,128)(2,1)}), bf16[8,16,32,128]{3,2,1,0:T(8,128)(2,1)S(1)}, u32[]{:S(2)}, u32[]{:S(2)}) async-start(bf16[8,16,32,128]{3,2,1,0:T(8,128)(2,1)} %shard_map.68), calls=%async_computation.3 | async-start | bytes 2097152 | tf_op jit(solution)/shard_map/all_to_all | solution.py:323
  9.9 2.6 %shard_map.64 = (bf16[8,8,32,128]{3,2,1,0:T(8,128)(2,1)}, bf16[8,4,32,128]{3,2,1,0:T(8,128)(2,1)}, bf16[8,4,32,128]{3,2,1,0:T(8,128)(2,1)}) custom-call(bf16[4,4,8,9216]{3,2,1,0:T(8,128)(2,1)} %refs_1_.3, bf16[4,4,8,9216]{3,2,1,0:T(8,128)(2,1)} %refs_1_.3, f32[1,128]{1,0:T(1,128)} %bitcast.3, f32[1,128]{1,0:T(1,128)} %bitcast.6), custom_call_target="tpu_custom_call" | custom-call | flops 1048576 | bytes 1048576 | tf_op jit(solution)/shard_map/pallas_call | solution.py:77
  12.5 10.0 %collective-permute-start = (bf16[8,4,32,128]{3,2,1,0:T(8,128)(2,1)}, bf16[8,4,32,128]{3,2,1,0:T(8,128)(2,1)S(1)}, u32[]{:S(2)}, u32[]{:S(2)}) collective-permute-start(bf16[8,4,32,128]{3,2,1,0:T(8,128)(2,1)} %get-tuple-element.17), channel_id=1, source_target_pairs={{0,64},{64,128},{128,192},{192,256},{256,320},{320,384},{384,448},... | collective-permute-start | bytes 786440 | tf_op jit(solution)/shard_map/ppermute | solution.py:319
  23.8 9.9 %collective-permute-done.t0_ref = bf16[8,4,32,128]{3,2,1,0:T(8,128)(2,1)S(1)} collective-permute-done((bf16[8,4,32,128]{3,2,1,0:T(8,128)(2,1)}, bf16[8,4,32,128]{3,2,1,0:T(8,128)(2,1)S(1)}, u32[]{:S(2)}, u32[]{:S(2)}) %collective-permute-start) | collective-permute-done | bytes 262176 | tf_op jit(solution)/shard_map/ppermute | solution.py:319
  33.7 11.9 %collective-permute-done.1.t1_ref = bf16[8,4,32,128]{3,2,1,0:T(8,128)(2,1)S(1)} collective-permute-done((bf16[8,4,32,128]{3,2,1,0:T(8,128)(2,1)}, bf16[8,4,32,128]{3,2,1,0:T(8,128)(2,1)S(1)}, u32[]{:S(2)}, u32[]{:S(2)}) %collective-permute-start.1) | collective-permute-done | bytes 262176 | tf_op jit(solution)/shard_map/ppermute | solution.py:319
  46.2 2.2 %shard_map.65 = bf16[8,16,32,128]{3,2,1,0:T(8,128)(2,1)} custom-call(bf16[8,8,32,128]{3,2,1,0:T(8,128)(2,1)} %get-tuple-element.16.c_ref, bf16[8,4,32,128]{3,2,1,0:T(8,128)(2,1)} %copy-done.2, bf16[8,4,32,128]{3,2,1,0:T(8,128)(2,1)} %copy-done.3), custom_call_target="tpu_custom_call" | custom-call | flops 2097152 | bytes 2097152 | tf_op jit(solution)/shard_map/pallas_call | solution.py:98
  48.5 6.9 %all-to-all-start = ((bf16[8,16,32,128]{3,2,1,0:T(8,128)(2,1)}), bf16[8,16,32,128]{3,2,1,0:T(8,128)(2,1)}, u32[]{:S(2)}, u32[]{:S(2)}) async-start(bf16[8,16,32,128]{3,2,1,0:T(8,128)(2,1)} %shard_map.65), calls=%async_computation | async-start | bytes 2097152 | tf_op jit(solution)/shard_map/all_to_all | solution.py:323
  55.4 2.5 %shard_map.67 = bf16[8,12,32,128]{3,2,1,0:T(8,128)(2,1)} custom-call(bf16[4,4,8,9216]{3,2,1,0:T(8,128)(2,1)} %refs_1_.3, f32[1,128]{1,0:T(1,128)} %bitcast.4, f32[1,128]{1,0:T(1,128)} %bitcast.7), custom_call_target="tpu_custom_call" | custom-call | flops 1572864 | bytes 1572864 | tf_op jit(solution)/shard_map/pallas_call | solution.py:77
  57.9 25.2 %all-to-all-done.refs_0_ = bf16[8,16,32,128]{3,2,1,0:T(8,128)(2,1)} async-done(((bf16[8,16,32,128]{3,2,1,0:T(8,128)(2,1)}), bf16[8,16,32,128]{3,2,1,0:T(8,128)(2,1)}, u32[]{:S(2)}, u32[]{:S(2)}) %all-to-all-start) | async-done | bytes 1048608 | tf_op jit(solution)/shard_map/all_to_all | solution.py:323
  83.1 3.5 %all-to-all-start.1 = ((bf16[8,12,32,128]{3,2,1,0:T(8,128)(2,1)}), bf16[8,12,32,128]{3,2,1,0:T(8,128)(2,1)S(1)}, u32[]{:S(2)}, u32[]{:S(2)}) async-start(bf16[8,12,32,128]{3,2,1,0:T(8,128)(2,1)} %shard_map.67), calls=%async_computation.1 | async-start | bytes 1572864 | tf_op jit(solution)/shard_map/all_to_all | solution.py:323
  87.7 8.2 %collective-permute-start.4 = (bf16[8,8,32,128]{3,2,1,0:T(8,128)(2,1)}, bf16[8,8,32,128]{3,2,1,0:T(8,128)(2,1)S(1)}, u32[]{:S(2)}, u32[]{:S(2)}) collective-permute-start(bf16[8,8,32,128]{3,2,1,0:T(8,128)(2,1)} %get-tuple-element.21), channel_id=1, source_target_pairs={{0,64},{64,128},{128,192},{192,256},{256,320},{320,384},{384,448},... | collective-permute-start | bytes 1572872 | tf_op jit(solution)/shard_map/ppermute | solution.py:319
  97.3 2.3 %shard_map.66 = (bf16[8,16,16,128]{3,2,1,0:T(8,128)(2,1)}, bf16[8,16,16,128]{3,2,1,0:T(8,128)(2,1)}) custom-call(bf16[8,16,32,128]{3,2,1,0:T(8,128)(2,1)} %all-to-all-done.refs_0_), custom_call_target="tpu_custom_call" | custom-call | flops 2097152 | bytes 2097152 | tf_op jit(solution)/shard_map/pallas_call | solution.py:143
  101.4 3.6 %collective-permute-start.3 = (bf16[8,16,16,128]{3,2,1,0:T(8,128)(2,1)}, bf16[8,16,16,128]{3,2,1,0:T(8,128)(2,1)}, u32[]{:S(2)}, u32[]{:S(2)}) collective-permute-start(bf16[8,16,16,128]{3,2,1,0:T(8,128)(2,1)} %get-tuple-element.20), channel_id=1, source_target_pairs={{8,0},{16,8},{24,16},{32,24},{40,32},{48,40},{56,48},{9,1},{17,9},... | collective-permute-start | bytes 1572872 | tf_op jit(solution)/shard_map/ppermute | solution.py:319
  106.1 3.2 %collective-permute-start.6 = (bf16[8,16,16,128]{3,2,1,0:T(8,128)(2,1)}, bf16[8,16,16,128]{3,2,1,0:T(8,128)(2,1)}, u32[]{:S(2)}, u32[]{:S(2)}) collective-permute-start(bf16[8,16,16,128]{3,2,1,0:T(8,128)(2,1)} %get-tuple-element.23), channel_id=1, source_target_pairs={{0,8},{8,16},{16,24},{24,32},{32,40},{40,48},{48,56},{1,9},{9,17},... | collective-permute-start | bytes 1572872 | tf_op jit(solution)/shard_map/ppermute | solution.py:319
  109.4 5.1 %collective-permute-done.4.refs_0_.refs_1_ = bf16[8,8,32,128]{3,2,1,0:T(8,128)(2,1)S(1)} collective-permute-done((bf16[8,8,32,128]{3,2,1,0:T(8,128)(2,1)}, bf16[8,8,32,128]{3,2,1,0:T(8,128)(2,1)S(1)}, u32[]{:S(2)}, u32[]{:S(2)}) %collective-permute-start.4) | collective-permute-done | bytes 524320 | tf_op jit(solution)/shard_map/ppermute | solution.py:319
  114.5 1.9 collective-permute-start.7
  116.4 24.0 %collective-permute-done.5.refs_1_.refs_2_ = bf16[8,8,32,128]{3,2,1,0:T(8,128)(2,1)S(1)} collective-permute-done((bf16[8,8,32,128]{3,2,1,0:T(8,128)(2,1)}, bf16[8,8,32,128]{3,2,1,0:T(8,128)(2,1)S(1)}, u32[]{:S(2)}, u32[]{:S(2)}) %collective-permute-start.5) | collective-permute-done | bytes 524320 | tf_op jit(solution)/shard_map/ppermute | solution.py:319
  141.5 1.9 collective-permute-start.8
  143.4 3.6 %collective-permute-start.9 = (bf16[8,16,16,128]{3,2,1,0:T(8,128)(2,1)}, bf16[8,16,16,128]{3,2,1,0:T(8,128)(2,1)}, u32[]{:S(2)}, u32[]{:S(2)}) collective-permute-start(bf16[8,16,16,128]{3,2,1,0:T(8,128)(2,1)} %get-tuple-element.26), channel_id=1, source_target_pairs={{8,0},{16,8},{24,16},{32,24},{40,32},{48,40},{56,48},{9,1},{17,9},... | collective-permute-start | bytes 1572872 | tf_op jit(solution)/shard_map/ppermute | solution.py:319
  147.3 5.4 %attend.2 = bf16[8,1,4,32,128]{4,3,2,1,0:T(8,128)(2,1)} custom-call(s32[17]{0:T(128)S(1)} %pad_add_fusion.info_ref, bf16[8,16,32,128]{3,2,1,0:T(8,128)(2,1)} %all-to-all-done.refs_0_, bf16[8,16,16,128]{3,2,1,0:T(8,128)(2,1)S(1)} %collective-permute-done.2.refs_1_, bf16[8,16,16,128]{3,2,1,0:T(8,128)(2,1)} %collective-permute-done.3.refs_2_, ...), custom_call_target="tpu_custom_call" | custom-call | flops 754974720 | bytes 4194304 | tf_op jit(solution)/shard_map/attend/pallas_call | solution.py:264
  152.7 8.5 %all-to-all-start.2 = ((bf16[8,1,4,32,128]{4,3,2,1,0:T(8,128)(2,1)}), bf16[8,1,4,32,128]{4,3,2,1,0:T(8,128)(2,1)S(1)}, u32[]{:S(2)}, u32[]{:S(2)}) async-start(bf16[8,1,4,32,128]{4,3,2,1,0:T(8,128)(2,1)} %attend.2), calls=%async_computation.2 | async-start | bytes 524288 | tf_op jit(solution)/shard_map/all_to_all | solution.py:323
  162.3 9.6 %attend.3 = bf16[8,2,4,32,128]{4,3,2,1,0:T(8,128)(2,1)S(1)} custom-call(s32[17]{0:T(128)S(1)} %pad_add_fusion.info_ref, bf16[8,16,32,128]{3,2,1,0:T(8,128)(2,1)S(1)} %all-to-all-done.3.ref.refs_0_, bf16[8,8,32,128]{3,2,1,0:T(8,128)(2,1)S(1)} %collective-permute-done.4.refs_0_.refs_1_, bf16[8,8,32,128]{3,2,1,0:T(8,128)(2,1)S(1)} %copy-done.1, ...), custom_call_target="tpu_custom_call" | custom-call | flops 1509949440 | bytes 8388608 | tf_op jit(solution)/shard_map/attend/pallas_call | solution.py:264
  172.1 24.5 %all_to_all.25.refs_1_ = bf16[8,2,4,32,128]{4,3,2,1,0:T(8,128)(2,1)S(1)} all-to-all(bf16[8,2,4,32,128]{4,3,2,1,0:T(8,128)(2,1)S(1)} %attend.3), channel_id=1, replica_groups=mesh['ta'=8,'ha'=8,'hd'=8] {'hd'}, dimensions={0} | all-to-all | bytes 1048576 | tf_op jit(solution)/shard_map/all_to_all | solution.py:323
  (33 shorter events, 10.9 us)
Async XLA Ops:
  2.8 45.7 %all-to-all-start.3 = ((bf16[8,16,32,128]{3,2,1,0:T(8,128)(2,1)}), bf16[8,16,32,128]{3,2,1,0:T(8,128)(2,1)S(1)}, u32[]{:S(2)}, u32[]{:S(2)}) async-start(bf16[8,16,32,128]{3,2,1,0:T(8,128)(2,1)} %shard_map.68), calls=%async_computation.3 | async-start | bytes 2097152 | tf_op jit(solution)/shard_map/all_to_all | solution.py:323
  12.5 21.2 %collective-permute-start = (bf16[8,4,32,128]{3,2,1,0:T(8,128)(2,1)}, bf16[8,4,32,128]{3,2,1,0:T(8,128)(2,1)S(1)}, u32[]{:S(2)}, u32[]{:S(2)}) collective-permute-start(bf16[8,4,32,128]{3,2,1,0:T(8,128)(2,1)} %get-tuple-element.17), channel_id=1, source_target_pairs={{0,64},{64,128},{128,192},{192,256},{256,320},{320,384},{384,448},... | collective-permute-start | bytes 786440 | tf_op jit(solution)/shard_map/ppermute | solution.py:319
  22.5 23.1 %collective-permute-start.1 = (bf16[8,4,32,128]{3,2,1,0:T(8,128)(2,1)}, bf16[8,4,32,128]{3,2,1,0:T(8,128)(2,1)S(1)}, u32[]{:S(2)}, u32[]{:S(2)}) collective-permute-start(bf16[8,4,32,128]{3,2,1,0:T(8,128)(2,1)} %get-tuple-element.18), channel_id=1, source_target_pairs={{64,0},{128,64},{192,128},{256,192},{320,256},{384,320},{448,384},... | collective-permute-start | bytes 786440 | tf_op jit(solution)/shard_map/ppermute | solution.py:319
  33.7 11.9 %copy-start.2 = (bf16[8,4,32,128]{3,2,1,0:T(8,128)(2,1)}, bf16[8,4,32,128]{3,2,1,0:T(8,128)(2,1)S(1)}, u32[]{:S(2)}) copy-start(bf16[8,4,32,128]{3,2,1,0:T(8,128)(2,1)S(1)} %collective-permute-done.t0_ref) | copy-start | bytes 786436
  45.5 0.7 copy-start.3
  48.5 34.6 %all-to-all-start = ((bf16[8,16,32,128]{3,2,1,0:T(8,128)(2,1)}), bf16[8,16,32,128]{3,2,1,0:T(8,128)(2,1)}, u32[]{:S(2)}, u32[]{:S(2)}) async-start(bf16[8,16,32,128]{3,2,1,0:T(8,128)(2,1)} %shard_map.65), calls=%async_computation | async-start | bytes 2097152 | tf_op jit(solution)/shard_map/all_to_all | solution.py:323
  83.1 64.2 %all-to-all-start.1 = ((bf16[8,12,32,128]{3,2,1,0:T(8,128)(2,1)}), bf16[8,12,32,128]{3,2,1,0:T(8,128)(2,1)S(1)}, u32[]{:S(2)}, u32[]{:S(2)}) async-start(bf16[8,12,32,128]{3,2,1,0:T(8,128)(2,1)} %shard_map.67), calls=%async_computation.1 | async-start | bytes 1572864 | tf_op jit(solution)/shard_map/all_to_all | solution.py:323
  86.7 60.4 %copy-start.5 = (s32[16]{0:T(128)S(1)}, s32[16]{0:T(128)}, u32[]{:S(2)}) copy-start(s32[16]{0:T(128)} %param.11) | copy-start | bytes 196
  86.7 60.4 %copy-start.6 = (s32[16]{0:T(128)S(1)}, s32[16]{0:T(128)}, u32[]{:S(2)}) copy-start(s32[16]{0:T(128)} %param.10) | copy-start | bytes 196
  86.7 60.5 %copy-start.4 = (s32[3,3]{1,0:T(4,128)S(1)}, s32[3,3]{1,0:T(4,128)}, u32[]{:S(2)}) copy-start(s32[3,3]{1,0:T(4,128)} %param.9) | copy-start | bytes 112
  87.7 26.7 %collective-permute-start.4 = (bf16[8,8,32,128]{3,2,1,0:T(8,128)(2,1)}, bf16[8,8,32,128]{3,2,1,0:T(8,128)(2,1)S(1)}, u32[]{:S(2)}, u32[]{:S(2)}) collective-permute-start(bf16[8,8,32,128]{3,2,1,0:T(8,128)(2,1)} %get-tuple-element.21), channel_id=1, source_target_pairs={{0,64},{64,128},{128,192},{192,256},{256,320},{320,384},{384,448},... | collective-permute-start | bytes 1572872 | tf_op jit(solution)/shard_map/ppermute | solution.py:319
  96.0 44.4 %collective-permute-start.5 = (bf16[8,8,32,128]{3,2,1,0:T(8,128)(2,1)}, bf16[8,8,32,128]{3,2,1,0:T(8,128)(2,1)S(1)}, u32[]{:S(2)}, u32[]{:S(2)}) collective-permute-start(bf16[8,8,32,128]{3,2,1,0:T(8,128)(2,1)} %get-tuple-element.22), channel_id=1, source_target_pairs={{64,0},{128,64},{192,128},{256,192},{320,256},{384,320},{448,384},... | collective-permute-start | bytes 1572872 | tf_op jit(solution)/shard_map/ppermute | solution.py:319
  99.5 43.9 %collective-permute-start.2 = (bf16[8,16,16,128]{3,2,1,0:T(8,128)(2,1)}, bf16[8,16,16,128]{3,2,1,0:T(8,128)(2,1)S(1)}, u32[]{:S(2)}, u32[]{:S(2)}) collective-permute-start(bf16[8,16,16,128]{3,2,1,0:T(8,128)(2,1)} %get-tuple-element.19), channel_id=1, source_target_pairs={{0,8},{8,16},{16,24},{24,32},{32,40},{40,48},{48,56},{1,9},{9,17},... | collective-permute-start | bytes 1572872 | tf_op jit(solution)/shard_map/ppermute | solution.py:319
  101.4 45.9 %collective-permute-start.3 = (bf16[8,16,16,128]{3,2,1,0:T(8,128)(2,1)}, bf16[8,16,16,128]{3,2,1,0:T(8,128)(2,1)}, u32[]{:S(2)}, u32[]{:S(2)}) collective-permute-start(bf16[8,16,16,128]{3,2,1,0:T(8,128)(2,1)} %get-tuple-element.20), channel_id=1, source_target_pairs={{8,0},{16,8},{24,16},{32,24},{40,32},{48,40},{56,48},{9,1},{17,9},... | collective-permute-start | bytes 1572872 | tf_op jit(solution)/shard_map/ppermute | solution.py:319
  106.1 55.1 %collective-permute-start.6 = (bf16[8,16,16,128]{3,2,1,0:T(8,128)(2,1)}, bf16[8,16,16,128]{3,2,1,0:T(8,128)(2,1)}, u32[]{:S(2)}, u32[]{:S(2)}) collective-permute-start(bf16[8,16,16,128]{3,2,1,0:T(8,128)(2,1)} %get-tuple-element.23), channel_id=1, source_target_pairs={{0,8},{8,16},{16,24},{24,32},{32,40},{40,48},{48,56},{1,9},{9,17},... | collective-permute-start | bytes 1572872 | tf_op jit(solution)/shard_map/ppermute | solution.py:319
  114.5 46.8 %collective-permute-start.7 = (bf16[8,16,16,128]{3,2,1,0:T(8,128)(2,1)}, bf16[8,16,16,128]{3,2,1,0:T(8,128)(2,1)}, u32[]{:S(2)}, u32[]{:S(2)}) collective-permute-start(bf16[8,16,16,128]{3,2,1,0:T(8,128)(2,1)} %get-tuple-element.24), channel_id=1, source_target_pairs={{8,0},{16,8},{24,16},{32,24},{40,32},{48,40},{56,48},{9,1},{17,9},... | collective-permute-start | bytes 1572872 | tf_op jit(solution)/shard_map/ppermute | solution.py:319
  140.3 12.4 %copy-start = (bf16[8,8,32,128]{3,2,1,0:T(8,128)(2,1)}, bf16[8,8,32,128]{3,2,1,0:T(8,128)(2,1)S(1)}, u32[]{:S(2)}) copy-start(bf16[8,8,32,128]{3,2,1,0:T(8,128)(2,1)S(1)} %collective-permute-done.5.refs_1_.refs_2_) | copy-start | bytes 1572868
  141.5 19.8 %collective-permute-start.8 = (bf16[8,16,16,128]{3,2,1,0:T(8,128)(2,1)}, bf16[8,16,16,128]{3,2,1,0:T(8,128)(2,1)}, u32[]{:S(2)}, u32[]{:S(2)}) collective-permute-start(bf16[8,16,16,128]{3,2,1,0:T(8,128)(2,1)} %get-tuple-element.25), channel_id=1, source_target_pairs={{0,8},{8,16},{16,24},{24,32},{32,40},{40,48},{48,56},{1,9},{9,17},... | collective-permute-start | bytes 1572872 | tf_op jit(solution)/shard_map/ppermute | solution.py:319
  143.4 17.9 %collective-permute-start.9 = (bf16[8,16,16,128]{3,2,1,0:T(8,128)(2,1)}, bf16[8,16,16,128]{3,2,1,0:T(8,128)(2,1)}, u32[]{:S(2)}, u32[]{:S(2)}) collective-permute-start(bf16[8,16,16,128]{3,2,1,0:T(8,128)(2,1)} %get-tuple-element.26), channel_id=1, source_target_pairs={{8,0},{16,8},{24,16},{32,24},{40,32},{48,40},{56,48},{9,1},{17,9},... | collective-permute-start | bytes 1572872 | tf_op jit(solution)/shard_map/ppermute | solution.py:319
  152.7 19.4 %all-to-all-start.2 = ((bf16[8,1,4,32,128]{4,3,2,1,0:T(8,128)(2,1)}), bf16[8,1,4,32,128]{4,3,2,1,0:T(8,128)(2,1)S(1)}, u32[]{:S(2)}, u32[]{:S(2)}) async-start(bf16[8,1,4,32,128]{4,3,2,1,0:T(8,128)(2,1)} %attend.2), calls=%async_computation.2 | async-start | bytes 524288 | tf_op jit(solution)/shard_map/all_to_all | solution.py:323
  161.3 1.0 copy-start.1
